TPU v7x, 128 devices: a whole 4x4x4 slice. The times are simulated.
128 devices in a mesh: ctx: 32 (over x, z, core), tp: 4 (over y).
Axes of the slice: x: 4, y: 4, z: 4, core: 2. Of those that a mesh axis runs over, the one named last changes fastest.
Arguments:
- queries: bfloat16 [16384, 5120], P(('ctx', 'tp')), may hold values from -400 to 400
- keys: bfloat16 [16384, 5120], P(('ctx', 'tp')), may hold values from -6 to 6
- values: bfloat16 [16384, 5120], P(('ctx', 'tp')), may hold values from -6 to 6
- dout: bfloat16 [16384, 5120], P(('ctx', 'tp')), may hold values from -6 to 6
- match: int32 [10, 64], replicated, may hold values from 0 to 63, as said below
Outputs:
- attended: bfloat16 [16384, 5120], P(('ctx', 'tp'))
- grad_queries: bfloat16 [16384, 5120], P(('ctx', 'tp'))
- grad_keys: bfloat16 [16384, 5120], P(('ctx', 'tp'))
- grad_values: bfloat16 [16384, 5120], P(('ctx', 'tp'))
Inputs may be any that keep to these rules, and one draw needn't show every extreme that they name: match[g, i] lies in 0 to i; the value i means that query block i has no matched block for group g. Among the 20 pairs of a query block and a group of one ctx index, at most 1 name a block of the tokens of any one other ctx index, and 1 is reached.
All inputs are finite; a program needn't handle non-finite values.
Results may differ from a plain program's by a relative error of at most 0.025.
Values may be sent and summed in bfloat16 or wider, within the bound.
No kernel may reach another device: no remote copies, remote signals or barrier semaphores. Data moves between devices by JAX's collectives and lax.ppermute only.
A program may use at most 128 MiB of HBM per device.

v0:
```python
import jax
import jax.numpy as jnp
from jax import lax
from jax.sharding import PartitionSpec as P

HEAD_DIM = 128
BLOCK = 256
GROUPS = 10
CAP = 1


def slot_tables(match, blocks_here, ctx_count):
    total_blocks = match.shape[1]
    block_ids = jnp.arange(total_blocks, dtype=jnp.int32)
    source = match // blocks_here
    target = block_ids // blocks_here
    remote = (match < block_ids[None, :]) & (source != target[None, :])
    item_count = blocks_here * GROUPS
    source_t = source.T.reshape(ctx_count, item_count)
    remote_t = remote.T.reshape(ctx_count, item_count)
    match_t = match.T.reshape(ctx_count, item_count)
    onehot = (
        (source_t[:, :, None] == jnp.arange(ctx_count, dtype=jnp.int32)) & remote_t[:, :, None]
    ).astype(jnp.int32)
    before = jnp.cumsum(onehot, axis=1) - onehot
    slot_rank = jnp.sum(before * onehot, axis=2)
    return (source_t, remote_t, match_t, slot_rank)


def group_major(tokens_array, blocks_here, per_group):
    split = tokens_array.reshape(blocks_here, BLOCK, per_group, GROUPS, HEAD_DIM)
    return jnp.transpose(split, (0, 3, 1, 2, 4))


def token_major(grouped, tokens_here, width_here):
    return jnp.transpose(grouped, (0, 2, 3, 1, 4)).reshape(tokens_here, width_here)


def pack_pair(k_flat, v_flat, send_row, filled):
    stacked = jnp.stack([k_flat[send_row], v_flat[send_row]], axis=2)
    return jnp.where(filled[:, :, None, None, None], stacked, jnp.zeros_like(stacked))


def unpack_pair(received, k_flat, v_flat, slot_index, near_row, my_remote, blocks_here, per_group):
    flat_slots = received.reshape(
        received.shape[0] * received.shape[1], 2, BLOCK, per_group * HEAD_DIM
    )
    far_pair = flat_slots[slot_index]
    near_pair = jnp.stack([k_flat[near_row], v_flat[near_row]], axis=1)
    matched = jnp.where(my_remote[:, None, None, None], far_pair, near_pair)
    matched = matched.reshape(blocks_here, GROUPS, 2, BLOCK, per_group, HEAD_DIM)
    return (matched[:, :, 0], matched[:, :, 1])


def shards(queries, keys, values, dout, match):
    ctx_count = lax.axis_size("ctx")
    own_ctx = lax.axis_index("ctx")
    head_q, head_k, head_v, head_do = (
        lax.all_to_all(queries, "tp", split_axis=1, concat_axis=0, tiled=True),
        lax.all_to_all(keys, "tp", split_axis=1, concat_axis=0, tiled=True),
        lax.all_to_all(values, "tp", split_axis=1, concat_axis=0, tiled=True),
        lax.all_to_all(dout, "tp", split_axis=1, concat_axis=0, tiled=True),
    )
    tokens_here = head_q.shape[0]
    width_here = head_q.shape[1]
    blocks_here = tokens_here // BLOCK
    per_group = width_here // (HEAD_DIM * GROUPS)
    item_count = blocks_here * GROUPS
    q_blocks = group_major(head_q, blocks_here, per_group)
    k_blocks = group_major(head_k, blocks_here, per_group)
    v_blocks = group_major(head_v, blocks_here, per_group)
    do_blocks = group_major(head_do, blocks_here, per_group)
    flat_rows = (item_count, BLOCK, per_group * HEAD_DIM)
    k_flat = k_blocks.reshape(flat_rows)
    v_flat = v_blocks.reshape(flat_rows)
    source_t, remote_t, match_t, slot_rank = slot_tables(match, blocks_here, ctx_count)
    item_ids = jnp.arange(item_count, dtype=jnp.int32)
    group_ids = item_ids % GROUPS
    slot_ids = jnp.arange(CAP, dtype=jnp.int32)
    chosen = (
        remote_t[:, None, :]
        & (source_t[:, None, :] == own_ctx)
        & (slot_rank[:, None, :] == slot_ids[None, :, None])
    )
    chosen_int = chosen.astype(jnp.int32)
    send_block = jnp.sum(chosen_int * (match_t[:, None, :] - own_ctx * blocks_here), axis=2)
    send_group = jnp.sum(chosen_int * group_ids[None, None, :], axis=2)
    send_filled = jnp.sum(chosen_int, axis=2) > 0
    send_row = jnp.where(send_filled, send_block * GROUPS + send_group, 0)
    my_source = lax.dynamic_index_in_dim(source_t, own_ctx, 0, keepdims=False)
    my_remote = lax.dynamic_index_in_dim(remote_t, own_ctx, 0, keepdims=False)
    my_match = lax.dynamic_index_in_dim(match_t, own_ctx, 0, keepdims=False)
    my_rank = lax.dynamic_index_in_dim(slot_rank, own_ctx, 0, keepdims=False)
    query_block_ids = own_ctx * blocks_here + item_ids // GROUPS
    is_valid = my_match < query_block_ids
    local_hit = is_valid & jnp.logical_not(my_remote)
    slot_index = jnp.where(my_remote, my_source * CAP + my_rank, 0)
    near_row = jnp.where(local_hit, (my_match - own_ctx * blocks_here) * GROUPS + group_ids, 0)
    received = lax.all_to_all(
        pack_pair(k_flat, v_flat, send_row, send_filled),
        "ctx",
        split_axis=0,
        concat_axis=0,
        tiled=True,
    )
    far_keys, far_values = unpack_pair(
        received, k_flat, v_flat, slot_index, near_row, my_remote, blocks_here, per_group
    )
    score_scale = HEAD_DIM ** (-0.5)
    causal = jnp.arange(BLOCK)[:, None] >= jnp.arange(BLOCK)[None, :]
    valid_mask = is_valid.reshape(blocks_here, GROUPS)[:, :, None, None, None]
    s_own = (
        jnp.einsum("ngqrd,ngkrd->ngrqk", q_blocks, k_blocks, preferred_element_type=jnp.float32)
        * score_scale
    )
    s_own = jnp.where(causal, s_own, -jnp.inf)
    s_far = (
        jnp.einsum("ngqrd,ngkrd->ngrqk", q_blocks, far_keys, preferred_element_type=jnp.float32)
        * score_scale
    )
    s_far = jnp.where(valid_mask, s_far, -jnp.inf)
    row_top = jnp.maximum(jnp.max(s_own, axis=-1), jnp.max(s_far, axis=-1))
    row_total = jnp.sum(jnp.exp(s_own - row_top[..., None]), axis=-1) + jnp.sum(
        jnp.exp(s_far - row_top[..., None]), axis=-1
    )
    log_total = row_top + jnp.log(row_total)
    p_own = jnp.exp(s_own - log_total[..., None])
    p_far = jnp.exp(s_far - log_total[..., None])
    pb_own = p_own.astype(jnp.bfloat16)
    pb_far = p_far.astype(jnp.bfloat16)
    attended = jnp.einsum(
        "ngrqk,ngkrd->ngqrd", pb_own, v_blocks, preferred_element_type=jnp.float32
    )
    attended = attended + jnp.einsum(
        "ngrqk,ngkrd->ngqrd", pb_far, far_values, preferred_element_type=jnp.float32
    )
    attended_b = attended.astype(jnp.bfloat16)
    out_tokens = lax.all_to_all(
        token_major(attended_b, tokens_here, width_here),
        "tp",
        split_axis=0,
        concat_axis=1,
        tiled=True,
    )
    received_again = lax.all_to_all(
        pack_pair(k_flat, v_flat, send_row, send_filled),
        "ctx",
        split_axis=0,
        concat_axis=0,
        tiled=True,
    )
    far_keys, far_values = unpack_pair(
        received_again, k_flat, v_flat, slot_index, near_row, my_remote, blocks_here, per_group
    )
    delta = jnp.sum(do_blocks.astype(jnp.float32) * attended_b.astype(jnp.float32), axis=-1)
    delta = jnp.transpose(delta, (0, 1, 3, 2))
    dp_own = jnp.einsum(
        "ngqrd,ngkrd->ngrqk", do_blocks, v_blocks, preferred_element_type=jnp.float32
    )
    dp_far = jnp.einsum(
        "ngqrd,ngkrd->ngrqk", do_blocks, far_values, preferred_element_type=jnp.float32
    )
    ds_own = (p_own * (dp_own - delta[..., None]) * score_scale).astype(jnp.bfloat16)
    ds_far = (p_far * (dp_far - delta[..., None]) * score_scale).astype(jnp.bfloat16)
    grad_q = jnp.einsum("ngrqk,ngkrd->ngqrd", ds_own, k_blocks, preferred_element_type=jnp.float32)
    grad_q = grad_q + jnp.einsum(
        "ngrqk,ngkrd->ngqrd", ds_far, far_keys, preferred_element_type=jnp.float32
    )
    grad_k = jnp.einsum("ngrqk,ngqrd->ngkrd", ds_own, q_blocks, preferred_element_type=jnp.float32)
    grad_v = jnp.einsum("ngrqk,ngqrd->ngkrd", pb_own, do_blocks, preferred_element_type=jnp.float32)
    gk_far = jnp.einsum("ngrqk,ngqrd->ngkrd", ds_far, q_blocks, preferred_element_type=jnp.float32)
    gv_far = jnp.einsum("ngrqk,ngqrd->ngkrd", pb_far, do_blocks, preferred_element_type=jnp.float32)
    gk_items = gk_far.reshape(flat_rows)
    gv_items = gv_far.reshape(flat_rows)
    grad_k = grad_k.reshape(flat_rows)
    grad_v = grad_v.reshape(flat_rows)
    local_target = jnp.where(local_hit, near_row, item_count)
    grad_k = grad_k.at[local_target].add(gk_items, mode="drop")
    grad_v = grad_v.at[local_target].add(gv_items, mode="drop")
    slot_total = ctx_count * CAP
    return_target = jnp.where(my_remote, slot_index, slot_total)
    return_pair = jnp.zeros((slot_total, 2, BLOCK, per_group * HEAD_DIM), jnp.float32)
    return_pair = return_pair.at[return_target].set(
        jnp.stack([gk_items, gv_items], axis=1), mode="drop"
    )
    return_pair = return_pair.reshape(ctx_count, CAP, 2, BLOCK, per_group * HEAD_DIM)
    came_back = lax.all_to_all(
        return_pair.astype(jnp.bfloat16), "ctx", split_axis=0, concat_axis=0, tiled=True
    ).astype(return_pair.dtype)
    came_back = came_back.reshape(slot_total, 2, BLOCK, per_group * HEAD_DIM)
    owner_target = jnp.where(send_filled, send_row, item_count).reshape(slot_total)
    grad_k = grad_k.at[owner_target].add(came_back[:, 0], mode="drop")
    grad_v = grad_v.at[owner_target].add(came_back[:, 1], mode="drop")
    grouped_shape = (blocks_here, GROUPS, BLOCK, per_group, HEAD_DIM)
    grad_q_b = token_major(grad_q.astype(jnp.bfloat16), tokens_here, width_here)
    grad_k_b = token_major(
        grad_k.astype(jnp.bfloat16).reshape(grouped_shape), tokens_here, width_here
    )
    grad_v_b = token_major(
        grad_v.astype(jnp.bfloat16).reshape(grouped_shape), tokens_here, width_here
    )
    back_q, back_k, back_v = (
        lax.all_to_all(grad_q_b, "tp", split_axis=0, concat_axis=1, tiled=True),
        lax.all_to_all(grad_k_b, "tp", split_axis=0, concat_axis=1, tiled=True),
        lax.all_to_all(grad_v_b, "tp", split_axis=0, concat_axis=1, tiled=True),
    )
    return (out_tokens, back_q, back_k, back_v)


def solution(mesh):
    placed = (
        P(("ctx", "tp"), None),
        P(("ctx", "tp"), None),
        P(("ctx", "tp"), None),
        P(("ctx", "tp"), None),
        P(),
    )
    return jax.shard_map(
        shards,
        mesh=mesh,
        in_specs=placed,
        out_specs=(
            P(("ctx", "tp"), None),
            P(("ctx", "tp"), None),
            P(("ctx", "tp"), None),
            P(("ctx", "tp"), None),
        ),
        check_vma=False,
    )
```

profile of v0, /device:TPU:32, one launch (start us, length us, event | category | flops | bytes accessed | tf_op | source)
XLA Modules:
  0.0 373.5 jit_solution(11461313028636679576)
XLA Ops:
  9.1 16.5 %all-to-all-done = bf16[128,4,1280]{0,2,1:T(8,128)(2,1)S(1)} async-done(((bf16[128,4,1280]{0,2,1:T(8,128)(2,1)}), bf16[128,4,1280]{0,2,1:T(8,128)(2,1)S(1)}, u32[]{:S(2)}, u32[]{:S(2)}) %all-to-all-start) | async-done | bytes 1310752 | tf_op jit(solution)/shard_map/all_to_all | solution.py:59
  31.5 14.6 %all-to-all-done.1 = bf16[128,4,1280]{0,2,1:T(8,128)(2,1)S(1)} async-done(((bf16[128,4,1280]{0,2,1:T(8,128)(2,1)}), bf16[128,4,1280]{0,2,1:T(8,128)(2,1)S(1)}, u32[]{:S(2)}, u32[]{:S(2)}) %all-to-all-start.1) | async-done | bytes 1310752 | tf_op jit(solution)/shard_map/all_to_all | solution.py:60
  54.2 11.6 %all-to-all-done.2 = bf16[128,4,1280]{0,2,1:T(8,128)(2,1)S(1)} async-done(((bf16[128,4,1280]{0,2,1:T(8,128)(2,1)}), bf16[128,4,1280]{0,2,1:T(8,128)(2,1)S(1)}, u32[]{:S(2)}, u32[]{:S(2)}) %all-to-all-start.2) | async-done | bytes 1310752 | tf_op jit(solution)/shard_map/all_to_all | solution.py:61
  65.8 4.6 %all-to-all-start.5 = ((bf16[128,4,1280]{0,2,1:T(8,128)(2,1)}), bf16[128,4,1280]{0,2,1:T(8,128)(2,1)}, u32[]{:S(2)}, u32[]{:S(2)}) async-start(bf16[128,4,1280]{0,2,1:T(8,128)(2,1)} %bitcast.304), calls=%async_computation.5 | async-start | bytes 2621440 | tf_op jit(solution)/shard_map/all_to_all | solution.py:62
  70.6 6.9 %copy.174 = bf16[4,128,1280]{1,0,2:T(4,128)(2,1)} copy(bf16[4,128,1280]{1,2,0:T(8,128)(2,1)S(1)} %bitcast.301) | data formatting | bytes 2621440 | tf_op jit(solution)/shard_map/all_to_all | solution.py:60
  85.2 6.9 %copy.187 = bf16[4,128,1280]{1,0,2:T(4,128)(2,1)} copy(bf16[4,128,1280]{1,2,0:T(8,128)(2,1)S(1)} %bitcast.302) | data formatting | bytes 2621440 | tf_op jit(solution)/shard_map/all_to_all | solution.py:61
  108.7 8.8 %all-to-all-start.3 = ((bf16[32,1,2,256,128]{4,3,2,1,0:T(8,128)(2,1)}), bf16[32,1,2,256,128]{4,3,2,1,0:T(8,128)(2,1)}, u32[]{:S(2)}, u32[]{:S(2)}) async-start(bf16[32,1,2,256,128]{4,3,2,1,0:T(8,128)(2,1)} %copy.190), calls=%async_computation.3 | async-start | bytes 8388608 | tf_op jit(solution)/shard_map/all_to_all | solution.py:99
  123.1 6.5 %copy.171 = bf16[4,128,1280]{1,0,2:T(4,128)(2,1)S(1)} copy(bf16[4,128,1280]{1,2,0:T(8,128)(2,1)} %bitcast.299) | data formatting | bytes 2621440 | tf_op jit(solution)/shard_map/all_to_all | solution.py:59
  134.8 7.8 %copy.201 = bf16[4,128,1280]{1,0,2:T(4,128)(2,1)} copy(bf16[4,128,1280]{1,2,0:T(8,128)(2,1)} %bitcast.44) | data formatting | bytes 2621440 | tf_op jit(solution)/shard_map/all_to_all | solution.py:62
  150.0 20.5 %all-to-all-done.3 = bf16[32,1,2,256,128]{4,3,2,1,0:T(8,128)(2,1)} async-done(((bf16[32,1,2,256,128]{4,3,2,1,0:T(8,128)(2,1)}), bf16[32,1,2,256,128]{4,3,2,1,0:T(8,128)(2,1)}, u32[]{:S(2)}, u32[]{:S(2)}) %all-to-all-start.3) | async-done | bytes 4194336 | tf_op jit(solution)/shard_map/all_to_all | solution.py:99
  170.5 4.8 %gather_fusion.2 = bf16[20,2,256,128]{3,2,1,0:T(8,128)(2,1)} fusion(bf16[32,2,256,128]{3,2,1,0:T(8,128)(2,1)} %bitcast.22, s32[1024]{0:T(1024)S(1)} %pad_clamp_fusion.1), kind=kCustom, calls=%fused_computation.2 | custom fusion | bytes 5242960 | tf_op jit(solution)/shard_map/gather | solution.py:48
  205.4 5.0 %all-to-all-start.6 = ((bf16[4,128,1280]{1,2,0:T(8,128)(2,1)}), bf16[4,128,1280]{1,2,0:T(8,128)(2,1)S(1)}, u32[]{:S(2)}, u32[]{:S(2)}) async-start(bf16[4,128,1280]{1,2,0:T(8,128)(2,1)} %copy.212), calls=%async_computation.6 | async-start | bytes 2621440 | tf_op jit(solution)/shard_map/all_to_all | solution.py:203
  220.4 9.6 %scatter_fusion.1 = f32[32,2,256,128]{3,2,1,0:T(8,128)} fusion(f32[32,2,256,128]{3,2,1,0:T(8,128)} %broadcast_in_dim.58, s32[20]{0:T(128)S(1)} %get-tuple-element.21, f32[20,2,256,128]{3,2,1,0:T(8,128)} %pad_maximum_fusion), kind=kCustom, calls=%fused_computation.6 | custom fusion | bytes 15728720 | tf_op jit(solution)/shard_map/scatter | solution.py:183
  230.1 6.1 %convert_bitcast_fusion = bf16[32,1,2,256,128]{4,3,2,1,0:T(8,128)(2,1)} fusion(f32[32,2,256,128]{3,2,1,0:T(8,128)} %scatter_fusion.1), kind=kLoop, calls=%fused_computation.31 | loop fusion | flops 2097152 | bytes 12582912 | tf_op jit(solution)/shard_map/convert_element_type | solution.py:188
  237.2 6.5 %all-to-all-start.7 = ((bf16[32,1,2,256,128]{4,3,2,1,0:T(8,128)(2,1)}), bf16[32,1,2,256,128]{4,3,2,1,0:T(8,128)(2,1)}, u32[]{:S(2)}, u32[]{:S(2)}) async-start(bf16[32,1,2,256,128]{4,3,2,1,0:T(8,128)(2,1)} %convert_bitcast_fusion), calls=%async_computation.7 | async-start | bytes 8388608 | tf_op jit(solution)/shard_map/all_to_all | solution.py:187
  250.4 5.8 %scatter_fusion = f32[20,256,128]{2,1,0:T(8,128)S(1)} fusion(f32[20,256,128]{2,1,0:T(8,128)S(1)} %bitcast.284, s32[20]{0:T(128)S(1)} %get-tuple-element.23, f32[20,256,128]{2,1,0:T(8,128)} %bitcast.289), kind=kCustom, calls=%fused_computation.5 | custom fusion | flops 655360 | bytes 7864400 | tf_op jit(solution)/shard_map/scatter-add | solution.py:178
  256.2 40.7 %all-to-all-done.7 = bf16[32,1,2,256,128]{4,3,2,1,0:T(8,128)(2,1)} async-done(((bf16[32,1,2,256,128]{4,3,2,1,0:T(8,128)(2,1)}), bf16[32,1,2,256,128]{4,3,2,1,0:T(8,128)(2,1)}, u32[]{:S(2)}, u32[]{:S(2)}) %all-to-all-start.7) | async-done | bytes 4194336 | tf_op jit(solution)/shard_map/all_to_all | solution.py:187
  296.9 4.8 %all-to-all-start.4 = ((bf16[4,128,1280]{1,2,0:T(8,128)(2,1)}), bf16[4,128,1280]{1,2,0:T(8,128)(2,1)}, u32[]{:S(2)}, u32[]{:S(2)}) async-start(bf16[4,128,1280]{1,2,0:T(8,128)(2,1)} %copy.199), calls=%async_computation.4 | async-start | bytes 2621440 | tf_op jit(solution)/shard_map/all_to_all | solution.py:138
  308.7 6.5 %scatter_fusion.2 = f32[20,256,128]{2,1,0:T(8,128)S(1)} fusion(f32[20,256,128]{2,1,0:T(8,128)S(1)} %scatter_fusion, s32[32]{0:T(128)S(1)} %fusion.62, f32[32,256,128]{2,1,0:T(8,128)} %get-tuple-element.29), kind=kCustom, calls=%fused_computation.7 | custom fusion | flops 1048576 | bytes 12583040 | tf_op jit(solution)/shard_map/scatter-add | solution.py:192
  322.0 5.1 %all-to-all-start.8 = ((bf16[4,128,1280]{1,2,0:T(8,128)(2,1)}), bf16[4,128,1280]{1,2,0:T(8,128)(2,1)}, u32[]{:S(2)}, u32[]{:S(2)}) async-start(bf16[4,128,1280]{1,2,0:T(8,128)(2,1)} %copy.219), calls=%async_computation.8 | async-start | bytes 2621440 | tf_op jit(solution)/shard_map/all_to_all | solution.py:204
  331.3 5.8 %scatter_fusion.3 = f32[20,256,128]{2,1,0:T(8,128)S(1)} fusion(f32[20,256,128]{2,1,0:T(8,128)S(1)} %bitcast.287, s32[20]{0:T(128)S(1)} %get-tuple-element.23, f32[20,256,128]{2,1,0:T(8,128)} %bitcast.294), kind=kCustom, calls=%fused_computation.8 | custom fusion | flops 655360 | bytes 7864400 | tf_op jit(solution)/shard_map/scatter-add | solution.py:179
  337.1 6.5 %scatter_fusion.4 = f32[20,256,128]{2,1,0:T(8,128)S(1)} fusion(f32[20,256,128]{2,1,0:T(8,128)S(1)} %scatter_fusion.3, s32[32]{0:T(128)S(1)} %fusion.62, f32[32,256,128]{2,1,0:T(8,128)} %get-tuple-element.28), kind=kCustom, calls=%fused_computation.9 | custom fusion | flops 1048576 | bytes 12583040 | tf_op jit(solution)/shard_map/scatter-add | solution.py:193
  350.5 4.8 %all-to-all-start.9 = ((bf16[4,128,1280]{1,2,0:T(8,128)(2,1)}), bf16[4,128,1280]{1,2,0:T(8,128)(2,1)S(1)}, u32[]{:S(2)}, u32[]{:S(2)}) async-start(bf16[4,128,1280]{1,2,0:T(8,128)(2,1)} %copy.222), calls=%async_computation.9 | async-start | bytes 2621440 | tf_op jit(solution)/shard_map/all_to_all | solution.py:205
  361.5 10.3 %all-to-all-done.9 = bf16[4,128,1280]{1,2,0:T(8,128)(2,1)S(1)} async-done(((bf16[4,128,1280]{1,2,0:T(8,128)(2,1)}), bf16[4,128,1280]{1,2,0:T(8,128)(2,1)S(1)}, u32[]{:S(2)}, u32[]{:S(2)}) %all-to-all-start.9) | async-done | bytes 1310752 | tf_op jit(solution)/shard_map/all_to_all | solution.py:205
  (142 shorter events, 145.1 us)
Async XLA Ops:
  0.6 7.0 %copy-start.14 = (bf16[128,5120]{1,0:T(8,128)(2,1)S(1)}, bf16[128,5120]{1,0:T(8,128)(2,1)}, u32[]{:S(2)}) copy-start(bf16[128,5120]{1,0:T(8,128)(2,1)} %param.6) | copy-start | bytes 3932164
  3.2 22.4 %all-to-all-start = ((bf16[128,4,1280]{0,2,1:T(8,128)(2,1)}), bf16[128,4,1280]{0,2,1:T(8,128)(2,1)S(1)}, u32[]{:S(2)}, u32[]{:S(2)}) async-start(bf16[128,4,1280]{0,2,1:T(8,128)(2,1)} %bitcast), calls=%async_computation | async-start | bytes 2621440 | tf_op jit(solution)/shard_map/all_to_all | solution.py:59
  25.5 6.0 %copy-start.6 = (bf16[128,4,1280]{0,2,1:T(8,128)(2,1)}, bf16[128,4,1280]{0,2,1:T(8,128)(2,1)S(1)}, u32[]{:S(2)}) copy-start(bf16[128,4,1280]{0,2,1:T(8,128)(2,1)S(1)} %all-to-all-done) | copy-start | bytes 3932164
  25.5 20.6 %all-to-all-start.1 = ((bf16[128,4,1280]{0,2,1:T(8,128)(2,1)}), bf16[128,4,1280]{0,2,1:T(8,128)(2,1)S(1)}, u32[]{:S(2)}, u32[]{:S(2)}) async-start(bf16[128,4,1280]{0,2,1:T(8,128)(2,1)} %bitcast.306), calls=%async_computation.1 | async-start | bytes 2621440 | tf_op jit(solution)/shard_map/all_to_all | solution.py:60
  29.1 20.6 %copy-start.17 = (s32[10,64]{1,0:T(8,128)S(1)}, s32[10,64]{1,0:T(8,128)}, u32[]{:S(2)}) copy-start(s32[10,64]{1,0:T(8,128)} %param.9) | copy-start | bytes 7684
  46.1 19.7 %all-to-all-start.2 = ((bf16[128,4,1280]{0,2,1:T(8,128)(2,1)}), bf16[128,4,1280]{0,2,1:T(8,128)(2,1)S(1)}, u32[]{:S(2)}, u32[]{:S(2)}) async-start(bf16[128,4,1280]{0,2,1:T(8,128)(2,1)} %bitcast.303), calls=%async_computation.2 | async-start | bytes 2621440 | tf_op jit(solution)/shard_map/all_to_all | solution.py:61
  65.8 11.7 %copy-start.10 = (bf16[128,4,1280]{0,2,1:T(8,128)(2,1)}, bf16[128,4,1280]{0,2,1:T(8,128)(2,1)S(1)}, u32[]{:S(2)}) copy-start(bf16[128,4,1280]{0,2,1:T(8,128)(2,1)S(1)} %all-to-all-done.2) | copy-start | bytes 3932164
  65.8 42.9 %all-to-all-start.5 = ((bf16[128,4,1280]{0,2,1:T(8,128)(2,1)}), bf16[128,4,1280]{0,2,1:T(8,128)(2,1)}, u32[]{:S(2)}, u32[]{:S(2)}) async-start(bf16[128,4,1280]{0,2,1:T(8,128)(2,1)} %bitcast.304), calls=%async_computation.5 | async-start | bytes 2621440 | tf_op jit(solution)/shard_map/all_to_all | solution.py:62
  81.6 3.6 copy-start.11
  108.7 61.8 %all-to-all-start.3 = ((bf16[32,1,2,256,128]{4,3,2,1,0:T(8,128)(2,1)}), bf16[32,1,2,256,128]{4,3,2,1,0:T(8,128)(2,1)}, u32[]{:S(2)}, u32[]{:S(2)}) async-start(bf16[32,1,2,256,128]{4,3,2,1,0:T(8,128)(2,1)} %copy.190), calls=%async_computation.3 | async-start | bytes 8388608 | tf_op jit(solution)/shard_map/all_to_all | solution.py:99
  134.8 75.5 %copy-start = (bf16[2,256,1,10,128]{4,1,3,0,2:T(8,128)(2,1)}, bf16[2,256,1,10,128]{4,1,3,0,2:T(8,128)(2,1)S(1)}, u32[]{:S(2)}) copy-start(bf16[2,256,1,10,128]{4,1,3,0,2:T(8,128)(2,1)S(1)} %copy.172) | copy-start | bytes 3932164
  175.3 2.5 copy-start.13
  177.7 2.2 slice-start
  184.3 2.7 copy-start.7
  192.1 2.9 copy-start.5
  205.4 30.8 %all-to-all-start.6 = ((bf16[4,128,1280]{1,2,0:T(8,128)(2,1)}), bf16[4,128,1280]{1,2,0:T(8,128)(2,1)S(1)}, u32[]{:S(2)}, u32[]{:S(2)}) async-start(bf16[4,128,1280]{1,2,0:T(8,128)(2,1)} %copy.212), calls=%async_computation.6 | async-start | bytes 2621440 | tf_op jit(solution)/shard_map/all_to_all | solution.py:203
  210.4 2.7 copy-start.4
  213.1 3.1 copy-start.2
  236.1 7.6 %copy-start.16 = (bf16[2,10,128,256]{3,2,1,0:T(8,128)(2,1)S(1)}, bf16[2,10,128,256]{3,2,1,0:T(8,128)(2,1)}, u32[]{:S(2)}) copy-start(bf16[2,10,128,256]{3,2,1,0:T(8,128)(2,1)} %get-tuple-element.35) | copy-start | bytes 3932164
  237.2 59.7 %all-to-all-start.7 = ((bf16[32,1,2,256,128]{4,3,2,1,0:T(8,128)(2,1)}), bf16[32,1,2,256,128]{4,3,2,1,0:T(8,128)(2,1)}, u32[]{:S(2)}, u32[]{:S(2)}) async-start(bf16[32,1,2,256,128]{4,3,2,1,0:T(8,128)(2,1)} %convert_bitcast_fusion), calls=%async_computation.7 | async-start | bytes 8388608 | tf_op jit(solution)/shard_map/all_to_all | solution.py:187
  296.9 25.2 %all-to-all-start.4 = ((bf16[4,128,1280]{1,2,0:T(8,128)(2,1)}), bf16[4,128,1280]{1,2,0:T(8,128)(2,1)}, u32[]{:S(2)}, u32[]{:S(2)}) async-start(bf16[4,128,1280]{1,2,0:T(8,128)(2,1)} %copy.199), calls=%async_computation.4 | async-start | bytes 2621440 | tf_op jit(solution)/shard_map/all_to_all | solution.py:138
  322.0 28.4 %all-to-all-start.8 = ((bf16[4,128,1280]{1,2,0:T(8,128)(2,1)}), bf16[4,128,1280]{1,2,0:T(8,128)(2,1)}, u32[]{:S(2)}, u32[]{:S(2)}) async-start(bf16[4,128,1280]{1,2,0:T(8,128)(2,1)} %copy.219), calls=%async_computation.8 | async-start | bytes 2621440 | tf_op jit(solution)/shard_map/all_to_all | solution.py:204
  349.2 6.0 %copy-start.9 = (bf16[4,128,1280]{1,2,0:T(8,128)(2,1)S(1)}, bf16[4,128,1280]{1,2,0:T(8,128)(2,1)}, u32[]{:S(2)}) copy-start(bf16[4,128,1280]{1,2,0:T(8,128)(2,1)} %copy-done.8) | copy-start | bytes 3932164
  350.5 21.4 %all-to-all-start.9 = ((bf16[4,128,1280]{1,2,0:T(8,128)(2,1)}), bf16[4,128,1280]{1,2,0:T(8,128)(2,1)S(1)}, u32[]{:S(2)}, u32[]{:S(2)}) async-start(bf16[4,128,1280]{1,2,0:T(8,128)(2,1)} %copy.222), calls=%async_computation.9 | async-start | bytes 2621440 | tf_op jit(solution)/shard_map/all_to_all | solution.py:205
  (6 other events, 10.3 us)
where the time goes:
time: 378 us; the launch traced here: 374 us
  local copies, waits for them, and re-layouts  132 us (35%)
  waiting for transfers between devices  114 us (30%)
  starting transfers between devices  51.1 us (14%)
  other arithmetic  46.8 us (12%)
  matrix products  27.9 us (7%)
    all_to_all x1, waiting for transfers between devices, shards(): lax.all_to_all(return_pair.astype(jnp.bfloat16), 'ctx', split_axis=0, con...  40.7 us
    reshape x6, local copies, waits for them, and re-layouts, group_major(): tokens_array.reshape(blocks_here, BLOCK, per_group, GROUPS, HEAD_DIM)  21.1 us
    all_to_all x1, waiting for transfers between devices, shards(): lax.all_to_all(pack_pair(k_flat, v_flat, send_row, send_filled), 'ctx', s...  20.5 us
    unnamed x48, local copies, waits for them, and re-layouts  20.4 us
    all_to_all x1, waiting for transfers between devices, shards(): lax.all_to_all(queries, 'tp', split_axis=1, concat_axis=0, tiled=True)  16.5 us
    all_to_all x1, waiting for transfers between devices, shards(): lax.all_to_all(keys, 'tp', split_axis=1, concat_axis=0, tiled=True)  14.6 us
    all_to_all x1, waiting for transfers between devices, shards(): lax.all_to_all(values, 'tp', split_axis=1, concat_axis=0, tiled=True)  11.6 us
    all_to_all x1, waiting for transfers between devices, shards(): lax.all_to_all(grad_v_b, 'tp', split_axis=0, concat_axis=1, tiled=True)  10.3 us
  transfers between devices with their start and end apart: 10, of which 6 were waited for; matrix products, arithmetic and copies ran while one was open for 44% of the time, Pallas kernels for 0%

commit v1 on v0

v1 whole, which is shorter than its diff:
```python
import jax
import jax.numpy as jnp
from jax import lax
from jax.experimental import pallas as pl
from jax.experimental.pallas import tpu as pltpu
from jax.sharding import PartitionSpec as P


HEAD_DIM = 128
BLOCK = 256
GROUPS = 10
CTX = 32
TP = 4
TOK = 128
ROWS = TP * TOK
COLS = GROUPS * HEAD_DIM
SCALE = HEAD_DIM ** (-0.5)
F32 = jnp.float32
BF16 = jnp.bfloat16


ANY = pl.BlockSpec(memory_space=pl.ANY)
SMEM = pl.BlockSpec(memory_space=pltpu.SMEM)
VMEM = pl.BlockSpec(memory_space=pltpu.VMEM)
HBM = pl.BlockSpec(memory_space=pltpu.HBM)


ITEMS = 2 * GROUPS
PARAMS = pltpu.CompilerParams(vmem_limit_bytes=40 * 1024 * 1024)


def shape(dims, dtype=BF16):
    return jax.ShapeDtypeStruct(dims, dtype)


def peer(step):
    return lax.rem(lax.axis_index("tp") + step, TP)


def col_slice(index):
    return pl.ds(pl.multiple_of(index * COLS, COLS), COLS)


def row_slice(index):
    return pl.ds(pl.multiple_of(index * TOK, TOK), TOK)


def block_slice(index):
    return pl.ds(pl.multiple_of(index * BLOCK, BLOCK), BLOCK)


def head_slice(index):
    return pl.ds(pl.multiple_of(index * HEAD_DIM, HEAD_DIM), HEAD_DIM)


def call(kernel, out_shape, in_specs, out_specs, scratch):
    def run(*operands):
        return pl.pallas_call(
            kernel,
            out_shape=out_shape,
            in_specs=in_specs,
            out_specs=out_specs,
            scratch_shapes=scratch,
            compiler_params=PARAMS,
        )(*operands)

    return run


def run_copies(copies):
    for copy in copies:
        copy.start()
    for copy in copies:
        copy.wait()


def cut_kernel(a_ref, b_ref, p1, p2, p3, sems):
    copies = []
    for step, out in ((1, p1), (2, p2), (3, p3)):
        for which, ref in enumerate((a_ref, b_ref)):
            copies.append(
                pltpu.make_async_copy(
                    ref.at[:, col_slice(peer(step))], out.at[which], sems.at[len(copies)]
                )
            )
    run_copies(copies)


def cut(a, b):
    return call(
        cut_kernel,
        [shape((2, TOK, COLS))] * 3,
        [HBM] * 2,
        [VMEM] * 3,
        [pltpu.SemaphoreType.DMA((6,))],
    )(a, b)


def join_kernel(own, r1, r2, r3, out, sems):
    copies = []
    for step, ref in ((0, own), (1, r1), (2, r2), (3, r3)):
        copies.append(
            pltpu.make_async_copy(ref, out.at[:, col_slice(peer(TP - step))], sems.at[step])
        )
    run_copies(copies)


def join(own, received):
    return call(
        join_kernel, shape((TOK, TP * COLS)), [VMEM] * 4, HBM, [pltpu.SemaphoreType.DMA((4,))]
    )(own, *received)


def exchange(pieces):
    received = []
    for step, piece in zip((1, 2, 3), pieces):
        received.append(
            lax.ppermute(piece, "tp", [(i, (i + step) % TP) for i in range(TP)])
        )
    return tuple(received)


def gather_copies(a_ref, b_ref, received, held, sems, base):
    copies = []
    for which, ref in enumerate((a_ref, b_ref)):
        copies.append(
            pltpu.make_async_copy(
                ref.at[:, col_slice(peer(0))],
                held.at[which, row_slice(peer(0))],
                sems.at[base + len(copies)],
            )
        )
    for step, ref in zip((1, 2, 3), received):
        for which in range(2):
            copies.append(
                pltpu.make_async_copy(
                    ref.at[which],
                    held.at[which, row_slice(peer(TP - step))],
                    sems.at[base + len(copies)],
                )
            )
    return copies


def table_kernel(match, tab):
    ctx = lax.axis_index("ctx")

    def clear(d, carry):
        for row in range(5):
            tab[row, d] = 0
        return carry

    lax.fori_loop(0, CTX, clear, 0)

    def owner_side(d, carry):
        for n in range(2):
            for g in range(GROUPS):
                block = 2 * d + n
                m = match[g, block]

                @pl.when((m < block) & ((m >> 1) == ctx))
                def _():
                    tab[0, d] = m & 1
                    tab[1, d] = g
                    tab[2, d] = 1

        return carry

    lax.fori_loop(ctx + 1, CTX, owner_side, 0)
    for n in range(2):
        for g in range(GROUPS):
            block = 2 * ctx + n
            m = match[g, block]
            source = m >> 1
            item = n * GROUPS + g

            @pl.when((m < block) & (source != ctx))
            def _():
                tab[0, source] = n
                tab[1, source] = g
                tab[2, source] = 1
                tab[3, item] = 1
                tab[4, item] = source

            @pl.when((m < block) & (source == ctx))
            def _():
                tab[3, item] = 2


def make_table(match):
    return call(table_kernel, shape((8, CTX), jnp.int32), [SMEM], SMEM, [])(match)


def pack_kernel(tab, a_ref, b_ref, r1, r2, r3, out, held_out, held, sems, slot_sems):
    ctx = lax.axis_index("ctx")
    run_copies(gather_copies(a_ref, b_ref, (r1, r2, r3), held, sems, 0))
    copies = []
    for d in range(CTX):
        which = jnp.where(ctx > d, 1, 0)
        copies.append(
            pltpu.make_async_copy(
                held.at[which, block_slice(tab[0, d]), head_slice(tab[1, d])],
                out.at[d],
                slot_sems.at[d],
            )
        )
    copies.append(pltpu.make_async_copy(held, held_out, slot_sems.at[CTX]))
    run_copies(copies)


def pack(tab, a, b, received):
    return call(
        pack_kernel,
        [shape((CTX, BLOCK, HEAD_DIM)), shape((2, ROWS, COLS))],
        [SMEM] + [HBM] * 2 + [ANY] * 3,
        [HBM] * 2,
        [
            pltpu.VMEM((2, ROWS, COLS), BF16),
            pltpu.SemaphoreType.DMA((8,)),
            pltpu.SemaphoreType.DMA((CTX + 1,)),
        ],
    )(tab, a, b, *received)


def swap(slots):
    return lax.all_to_all(slots, "ctx", split_axis=0, concat_axis=0, tiled=True)


def dot(a, b):
    return lax.dot_general(a, b, (((1,), (0,)), ((), ())), preferred_element_type=F32)


def dot_t(a, b):
    return lax.dot_general(a, b, (((1,), (1,)), ((), ())), preferred_element_type=F32)


def far_copies(tab, slots, far, sems):
    return [
        pltpu.make_async_copy(slots.at[tab[4, item]], far.at[item], sems.at[item])
        for item in range(ITEMS)
    ]


def fill_local(tab, far, held):
    def local(g, carry):
        @pl.when(tab[3, GROUPS + g] == 2)
        def _():
            far[GROUPS + g] = held[pl.ds(0, BLOCK), head_slice(g)]

        return carry

    lax.fori_loop(0, GROUPS, local, 0)


def start_all(copies):
    for copy in copies:
        copy.start()


def wait_all(copies):
    for copy in copies:
        copy.wait()


def prob_kernel(tab, kq_ref, slots, prob_out, lse_out, kq, far, prob, sems, far_sems, out_sems):
    loads = [pltpu.make_async_copy(kq_ref, kq, sems.at[0])]
    loads += far_copies(tab, slots, far, far_sems)
    run_copies(loads)
    fill_local(tab, far, kq.at[0])
    causal = lax.broadcasted_iota(jnp.int32, (BLOCK, BLOCK), 0) >= lax.broadcasted_iota(
        jnp.int32, (BLOCK, BLOCK), 1
    )

    def store(item):
        return pltpu.make_async_copy(prob.at[item], prob_out.at[item], out_sems.at[item])

    def step(g, carry):
        cols = head_slice(g)
        for n in range(2):
            rows = pl.ds(n * BLOCK, BLOCK)
            item = n * GROUPS + g
            q = kq[1, rows, cols]
            s_own = jnp.where(causal, dot_t(q, kq[0, rows, cols]) * SCALE, -jnp.inf)
            s_far = jnp.where(tab[3, item] > 0, dot_t(q, far[item]) * SCALE, -jnp.inf)
            top = jnp.maximum(
                jnp.max(s_own, axis=1, keepdims=True), jnp.max(s_far, axis=1, keepdims=True)
            )
            e_own = jnp.exp(s_own - top)
            e_far = jnp.exp(s_far - top)
            total = jnp.sum(e_own, axis=1, keepdims=True) + jnp.sum(e_far, axis=1, keepdims=True)
            inverse = 1.0 / total
            prob[item, :, pl.ds(0, BLOCK)] = (e_own * inverse).astype(BF16)
            prob[item, :, pl.ds(BLOCK, BLOCK)] = (e_far * inverse).astype(BF16)
            lse = jnp.broadcast_to(top + jnp.log(total), (BLOCK, HEAD_DIM))
            lse_out[item] = jnp.transpose(lse)[0:8]
        for n in range(2):
            store(n * GROUPS + g).start()
        return carry

    lax.fori_loop(0, GROUPS, step, 0)
    wait_all([store(item) for item in range(ITEMS)])


def prob_side(tab, kq, slots):
    return call(
        prob_kernel,
        [shape((ITEMS, BLOCK, 2 * BLOCK)), shape((ITEMS, 8, BLOCK), F32)],
        [SMEM, HBM, HBM],
        [HBM, VMEM],
        [
            pltpu.VMEM((2, ROWS, COLS), BF16),
            pltpu.VMEM((ITEMS, BLOCK, HEAD_DIM), BF16),
            pltpu.VMEM((ITEMS, BLOCK, 2 * BLOCK), BF16),
            pltpu.SemaphoreType.DMA((1,)),
            pltpu.SemaphoreType.DMA((ITEMS,)),
            pltpu.SemaphoreType.DMA((ITEMS,)),
        ],
    )(tab, kq, slots)


def piece_copies(result, outs, sems):
    return [
        pltpu.make_async_copy(result.at[row_slice(peer(move))], out, sems.at[move])
        for move, out in enumerate(outs)
    ]


def prob_copy(prob_ref, prob, item, sems):
    return pltpu.make_async_copy(prob_ref.at[item], prob.at[item], sems.at[item])


def start_probs(prob_ref, prob, sems):
    for g in range(GROUPS):
        for n in range(2):
            prob_copy(prob_ref, prob, n * GROUPS + g, sems).start()


def value_kernel(
    tab, prob_ref, vd_ref, slots, own, p1, p2, p3, full,
    prob, v, far, result, sems, far_sems, prob_sems, out_sems,
):
    loads = [pltpu.make_async_copy(vd_ref.at[0], v, sems.at[0])]
    loads += far_copies(tab, slots, far, far_sems)
    start_all(loads)
    start_probs(prob_ref, prob, prob_sems)
    wait_all(loads)
    fill_local(tab, far, v)

    def step(g, carry):
        cols = head_slice(g)
        for n in range(2):
            prob_copy(prob_ref, prob, n * GROUPS + g, prob_sems).wait()
        for n in range(2):
            rows = pl.ds(n * BLOCK, BLOCK)
            item = n * GROUPS + g
            att = dot(prob[item, :, pl.ds(0, BLOCK)], v[rows, cols])
            att = att + dot(prob[item, :, pl.ds(BLOCK, BLOCK)], far[item])
            result[rows, cols] = att.astype(BF16)
        return carry

    lax.fori_loop(0, GROUPS, step, 0)
    run_copies(
        piece_copies(result, (own, p1, p2, p3), out_sems)
        + [pltpu.make_async_copy(result, full, out_sems.at[TP])]
    )


def value_side(tab, prob, vd, slots):
    return call(
        value_kernel,
        [shape((TOK, COLS))] * 4 + [shape((ROWS, COLS))],
        [SMEM, HBM, HBM, HBM],
        [HBM] * 5,
        [
            pltpu.VMEM((ITEMS, BLOCK, 2 * BLOCK), BF16),
            pltpu.VMEM((ROWS, COLS), BF16),
            pltpu.VMEM((ITEMS, BLOCK, HEAD_DIM), BF16),
            pltpu.VMEM((ROWS, COLS), BF16),
            pltpu.SemaphoreType.DMA((1,)),
            pltpu.SemaphoreType.DMA((ITEMS,)),
            pltpu.SemaphoreType.DMA((ITEMS,)),
            pltpu.SemaphoreType.DMA((TP + 1,)),
        ],
    )(tab, prob, vd, slots)


def query_kernel(
    tab, prob_ref, lse, kq_ref, vd_ref, slots1, slots2, att_ref,
    own, p1, p2, p3, stats_slots, stats,
    prob, k, vd, att, far_k, far_v, result, sems, k_sems, v_sems, prob_sems, out_sems, slot_sems,
):
    ctx = lax.axis_index("ctx")
    loads = [
        pltpu.make_async_copy(vd_ref, vd, sems.at[0]),
        pltpu.make_async_copy(att_ref, att, sems.at[1]),
        pltpu.make_async_copy(kq_ref.at[0], k, sems.at[2]),
    ]
    loads += far_copies(tab, slots2, far_v, v_sems)
    loads += far_copies(tab, slots1, far_k, k_sems)
    start_all(loads)
    start_probs(prob_ref, prob, prob_sems)
    wait_all(loads)
    fill_local(tab, far_v, vd.at[0])
    fill_local(tab, far_k, k)
    sublane = lax.broadcasted_iota(jnp.int32, (8, BLOCK), 0)

    def step(g, carry):
        cols = head_slice(g)
        for n in range(2):
            prob_copy(prob_ref, prob, n * GROUPS + g, prob_sems).wait()
        for n in range(2):
            rows = pl.ds(n * BLOCK, BLOCK)
            item = n * GROUPS + g
            do = vd[1, rows, cols]
            delta = jnp.sum(
                do.astype(F32) * att[rows, cols].astype(F32), axis=1, keepdims=True
            )
            p_own = prob[item, :, pl.ds(0, BLOCK)].astype(F32)
            p_far = prob[item, :, pl.ds(BLOCK, BLOCK)].astype(F32)
            ds_own = (p_own * (dot_t(do, vd[0, rows, cols]) - delta) * SCALE).astype(BF16)
            ds_far = (p_far * (dot_t(do, far_v[item]) - delta) * SCALE).astype(BF16)
            grad = dot(ds_own, k[rows, cols]) + dot(ds_far, far_k[item])
            result[rows, cols] = grad.astype(BF16)
            turned = jnp.transpose(jnp.broadcast_to(delta, (BLOCK, HEAD_DIM)))[0:8]
            stats[item] = jnp.where(sublane == 0, lse[item], turned)
        return carry

    lax.fori_loop(0, GROUPS, step, 0)
    copies = piece_copies(result, (own, p1, p2, p3), out_sems)
    for d in range(CTX):
        item = jnp.where(ctx > d, tab[0, d] * GROUPS + tab[1, d], 0)
        copies.append(pltpu.make_async_copy(stats.at[item], stats_slots.at[d], slot_sems.at[d]))
    run_copies(copies)


def query_side(tab, prob, lse, kq, vd, slots1, slots2, att):
    return call(
        query_kernel,
        [shape((TOK, COLS))] * 4 + [shape((CTX, 8, BLOCK), F32), shape((ITEMS, 8, BLOCK), F32)],
        [SMEM, HBM, VMEM] + [HBM] * 5,
        [HBM] * 5 + [VMEM],
        [
            pltpu.VMEM((ITEMS, BLOCK, 2 * BLOCK), BF16),
            pltpu.VMEM((ROWS, COLS), BF16),
            pltpu.VMEM((2, ROWS, COLS), BF16),
            pltpu.VMEM((ROWS, COLS), BF16),
            pltpu.VMEM((ITEMS, BLOCK, HEAD_DIM), BF16),
            pltpu.VMEM((ITEMS, BLOCK, HEAD_DIM), BF16),
            pltpu.VMEM((ROWS, COLS), BF16),
            pltpu.SemaphoreType.DMA((3,)),
            pltpu.SemaphoreType.DMA((ITEMS,)),
            pltpu.SemaphoreType.DMA((ITEMS,)),
            pltpu.SemaphoreType.DMA((ITEMS,)),
            pltpu.SemaphoreType.DMA((TP,)),
            pltpu.SemaphoreType.DMA((CTX,)),
        ],
    )(tab, prob, lse, kq, vd, slots1, slots2, att)


def key_terms(k, v, q, do, stats, causal):
    s = dot_t(k, q) * SCALE
    if causal is not None:
        s = jnp.where(causal, s, -jnp.inf)
    p = jnp.exp(s - stats[0:1])
    ds = (p * (dot_t(v, do) - stats[1:2]) * SCALE).astype(BF16)
    return dot(ds, q), dot(p.astype(BF16), do)


def near_kernel(tab, kq_ref, vd_ref, stats, gk_out, gv_out, kq, vd, gk, gv, sems, out_sems):
    run_copies(
        [
            pltpu.make_async_copy(kq_ref, kq, sems.at[0]),
            pltpu.make_async_copy(vd_ref, vd, sems.at[1]),
        ]
    )
    causal = lax.broadcasted_iota(jnp.int32, (BLOCK, BLOCK), 0) <= lax.broadcasted_iota(
        jnp.int32, (BLOCK, BLOCK), 1
    )

    def step(g, carry):
        cols = head_slice(g)
        for n in range(2):
            rows = pl.ds(n * BLOCK, BLOCK)
            gk[rows, cols], gv[rows, cols] = key_terms(
                kq[0, rows, cols], vd[0, rows, cols], kq[1, rows, cols], vd[1, rows, cols],
                stats[n * GROUPS + g], causal,
            )

        @pl.when(tab[3, GROUPS + g] == 2)
        def _():
            low, high = pl.ds(0, BLOCK), pl.ds(BLOCK, BLOCK)
            k_term, v_term = key_terms(
                kq[0, low, cols], vd[0, low, cols], kq[1, high, cols], vd[1, high, cols],
                stats[GROUPS + g], None,
            )
            gk[low, cols] += k_term
            gv[low, cols] += v_term

        return carry

    lax.fori_loop(0, GROUPS, step, 0)
    run_copies(
        [
            pltpu.make_async_copy(gk, gk_out, out_sems.at[0]),
            pltpu.make_async_copy(gv, gv_out, out_sems.at[1]),
        ]
    )


def near_side(tab, kq, vd, stats):
    return call(
        near_kernel,
        [shape((ROWS, COLS), F32)] * 2,
        [SMEM, HBM, HBM, VMEM],
        [HBM] * 2,
        [
            pltpu.VMEM((2, ROWS, COLS), BF16),
            pltpu.VMEM((2, ROWS, COLS), BF16),
            pltpu.VMEM((ROWS, COLS), F32),
            pltpu.VMEM((ROWS, COLS), F32),
            pltpu.SemaphoreType.DMA((2,)),
            pltpu.SemaphoreType.DMA((2,)),
        ],
    )(tab, kq, vd, stats)


def far_kernel(
    tab, kq_ref, vd_ref, slots1, slots2, stats, gk_ref, gv_ref,
    ko, k1, k2, k3, vo, v1, v2, v3,
    k, v, far_q, far_do, near, acc, result, sems, slot_sems, out_sems,
):
    ctx = lax.axis_index("ctx")

    def slot_copies(d):
        return [
            pltpu.make_async_copy(slots1.at[d], far_q.at[d], slot_sems.at[0, d]),
            pltpu.make_async_copy(slots2.at[d], far_do.at[d], slot_sems.at[1, d]),
        ]

    def start_slot(d, carry):
        start_all(slot_copies(d))
        return carry

    loads = [
        pltpu.make_async_copy(kq_ref.at[0], k, sems.at[0]),
        pltpu.make_async_copy(vd_ref.at[0], v, sems.at[1]),
    ]
    near_loads = [
        pltpu.make_async_copy(gk_ref, near.at[0], sems.at[2]),
        pltpu.make_async_copy(gv_ref, near.at[1], sems.at[3]),
    ]
    start_all(loads)
    pairs = (CTX - ctx) // 2
    lax.fori_loop(0, 2 * pairs, lambda j, c: start_slot((ctx + 1 + j) % CTX, c), 0)
    start_all(near_loads)
    acc[...] = jnp.zeros_like(acc)
    wait_all(loads)

    def step(pair, carry):
        picked = []
        for half in range(2):
            want = ctx + 1 + 2 * pair + half
            d = want % CTX
            wait_all(slot_copies(d))
            picked.append((d, (tab[2, d] == 1) & (want < CTX)))
        terms = []
        for d, filled in picked:
            rows, cols = block_slice(tab[0, d]), head_slice(tab[1, d])
            k_term, v_term = key_terms(
                k[rows, cols], v[rows, cols], far_q[d], far_do[d], stats[d], None
            )
            terms.append(
                (rows, cols, jnp.where(filled, k_term, 0.0), jnp.where(filled, v_term, 0.0))
            )
        for rows, cols, k_term, v_term in terms:
            acc[0, rows, cols] += k_term
            acc[1, rows, cols] += v_term
        return carry

    lax.fori_loop(0, pairs, step, 0)
    outs = ((ko, k1, k2, k3), (vo, v1, v2, v3))
    stores = []
    for which in range(2):
        near_loads[which].wait()
        result[which] = (near[which] + acc[which]).astype(BF16)
        copies = piece_copies(result.at[which], outs[which], out_sems.at[which])
        start_all(copies)
        stores += copies
    wait_all(stores)


def far_side(tab, kq, vd, slots1, slots2, stats, gk, gv):
    return call(
        far_kernel,
        [shape((TOK, COLS))] * 8,
        [SMEM] + [HBM] * 4 + [VMEM] + [HBM] * 2,
        [HBM] * 8,
        [
            pltpu.VMEM((ROWS, COLS), BF16),
            pltpu.VMEM((ROWS, COLS), BF16),
            pltpu.VMEM((CTX, BLOCK, HEAD_DIM), BF16),
            pltpu.VMEM((CTX, BLOCK, HEAD_DIM), BF16),
            pltpu.VMEM((2, ROWS, COLS), F32),
            pltpu.VMEM((2, ROWS, COLS), F32),
            pltpu.VMEM((2, ROWS, COLS), BF16),
            pltpu.SemaphoreType.DMA((4,)),
            pltpu.SemaphoreType.DMA((2, CTX)),
            pltpu.SemaphoreType.DMA((2, TP)),
        ],
    )(tab, kq, vd, slots1, slots2, stats, gk, gv)


def shards(queries, keys, values, dout, match):
    kq_in = exchange(cut(keys, queries))
    vd_in = exchange(cut(values, dout))
    tab = make_table(match)
    slots1, kq = pack(tab, keys, queries, kq_in)
    far1 = swap(slots1)
    slots2, vd = pack(tab, values, dout, vd_in)
    slots2, far1 = lax.optimization_barrier((slots2, far1))
    far2 = swap(slots2)
    prob, lse = prob_side(tab, kq, far1)
    *att, att_full = value_side(tab, prob, vd, far2)
    att_in = exchange(att[1:4])
    *gq, stats_slots, stats = query_side(tab, prob, lse, kq, vd, far1, far2, att_full)
    gq_in = exchange(gq[1:4])
    far_stats = swap(stats_slots)
    gk, gv = near_side(tab, kq, vd, stats)
    out = far_side(tab, kq, vd, far1, far2, far_stats, gk, gv)
    gk_in = exchange(out[1:4])
    gv_in = exchange(out[5:])
    return (join(att[0], att_in), join(gq[0], gq_in), join(out[0], gk_in), join(out[4], gv_in))


def solution(mesh):
    placed = P(("ctx", "tp"), None)
    return jax.shard_map(
        shards,
        mesh=mesh,
        in_specs=(placed, placed, placed, placed, P()),
        out_specs=(placed, placed, placed, placed),
        check_vma=False,
    )
```

time: 378 us -> 237 us (0.63)
  local copies, waits for them, and re-layouts: 132 us -> 27.7 us
  Pallas kernels: 0 us -> 70.3 us
  other arithmetic: 46.8 us -> 0 us
  waiting for transfers between devices: 114 us -> 83.5 us
  matrix products: 27.9 us -> 0 us
    all_to_all x10 -> x3, waiting for transfers between devices: 114 us -> 13.2 us  [swap(): return lax.all_to_all(slots, 'ctx', split_axis=0, concat_axis=0, tiled=True)]
    ppermute x0 -> x18, waiting for transfers between devices: none -> 70.3 us  [exchange(): lax.ppermute(piece, 'tp', [(i, (i + step) % TP) for i in range(TP)])]
    pallas_call x0 -> x14, Pallas kernels: none -> 70.3 us  [run(): pl.pallas_call(kernel, out_shape=out_shape, in_specs=in_specs, out_specs=...]
    all_to_all x12 -> x0, local copies, waits for them, and re-layouts: 38.8 us -> none  [the longest x1 7.82 us: shards(): lax.all_to_all(dout, 'tp', split_axis=1, concat_axis=0, tiled=True)]
    ppermute x0 -> x18, starting transfers between devices: none -> 30.1 us  [exchange(): lax.ppermute(piece, 'tp', [(i, (i + step) % TP) for i in range(TP)])]
    all_to_all x10 -> x3, starting transfers between devices: 51.1 us -> 22.1 us  [swap(): return lax.all_to_all(slots, 'ctx', split_axis=0, concat_axis=0, tiled=True)]
    dot_general x12 -> x0, matrix products: 27.9 us -> none  [the longest x1 4.15 us: shards(): jnp.einsum('ngrqk,ngqrd->ngkrd', pb_own, do_blocks, preferred_element_typ...]
    reshape x10 -> x0, local copies, waits for them, and re-layouts: 24.8 us -> none  [the longest x6 21.1 us: group_major(): tokens_array.reshape(blocks_here, BLOCK, per_group, GROUPS, HEAD_DIM)]
  transfers between devices with their start and end apart: 10 -> 21, of which waited for: 6 -> 11; matrix products, arithmetic and copies ran while one was open for 44% -> 0% of each run, Pallas kernels for 0% -> 25%
where the time goes in v1:
time: 237 us; the launch traced here: 235 us
  waiting for transfers between devices  83.5 us (35%)
  Pallas kernels  70.3 us (30%)
  starting transfers between devices  52.2 us (22%)
  local copies, waits for them, and re-layouts  27.7 us (12%)
    ppermute x18, waiting for transfers between devices, exchange(): lax.ppermute(piece, 'tp', [(i, (i + step) % TP) for i in range(TP)])  70.3 us
    pallas_call x14, Pallas kernels, run(): pl.pallas_call(kernel, out_shape=out_shape, in_specs=in_specs, out_specs=...  70.3 us
    ppermute x18, starting transfers between devices, exchange(): lax.ppermute(piece, 'tp', [(i, (i + step) % TP) for i in range(TP)])  30.1 us
    unnamed x56, local copies, waits for them, and re-layouts  27.7 us
    all_to_all x3, starting transfers between devices, swap(): return lax.all_to_all(slots, 'ctx', split_axis=0, concat_axis=0, tiled=True)  22.1 us
    all_to_all x3, waiting for transfers between devices, swap(): return lax.all_to_all(slots, 'ctx', split_axis=0, concat_axis=0, tiled=True)  13.2 us
  transfers between devices with their start and end apart: 21, of which 11 were waited for; matrix products, arithmetic and copies ran while one was open for 0% of the time, Pallas kernels for 25%

profile of v1, /device:TPU:32, one launch (start us, length us, event | category | flops | bytes accessed | tf_op | source)
XLA Modules:
  0.0 234.8 jit_solution(584511743299369141)
XLA Ops:
  5.2 2.9 %collective-permute-start.1 = (bf16[2,128,1280]{2,1,0:T(8,128)(2,1)S(1)}, bf16[2,128,1280]{2,1,0:T(8,128)(2,1)S(1)}, u32[]{:S(2)}, u32[]{:S(2)}) collective-permute-start(bf16[2,128,1280]{2,1,0:T(8,128)(2,1)S(1)} %get-tuple-element.40), channel_id=1, source_target_pairs={{0,2},{1,3},{2,0},{3,1},{4,6},{5,7},{6,4},{7,5},{8,10},{9,11},{10,... | collective-permute-start | bytes 1966088 | tf_op jit(solution)/shard_map/ppermute | solution.py:118
  9.4 3.7 %shard_map.84.tab = s32[8,32]{1,0:T(8,128)S(1)} custom-call(s32[10,64]{1,0:T(8,128)S(1)} %copy-done.22), custom_call_target="tpu_custom_call" | custom-call | tf_op jit(solution)/shard_map/pallas_call | solution.py:58
  13.2 8.2 %collective-permute-done.r1 = bf16[2,128,1280]{2,1,0:T(8,128)(2,1)S(1)} collective-permute-done((bf16[2,128,1280]{2,1,0:T(8,128)(2,1)S(1)}, bf16[2,128,1280]{2,1,0:T(8,128)(2,1)S(1)}, u32[]{:S(2)}, u32[]{:S(2)}) %collective-permute-start) | collective-permute-done | bytes 655392 | tf_op jit(solution)/shard_map/ppermute | solution.py:118
  21.3 15.2 %collective-permute-done.1.r2 = bf16[2,128,1280]{2,1,0:T(8,128)(2,1)S(1)} collective-permute-done((bf16[2,128,1280]{2,1,0:T(8,128)(2,1)S(1)}, bf16[2,128,1280]{2,1,0:T(8,128)(2,1)S(1)}, u32[]{:S(2)}, u32[]{:S(2)}) %collective-permute-start.1) | collective-permute-done | bytes 655392 | tf_op jit(solution)/shard_map/ppermute | solution.py:118
  36.5 2.6 %shard_map.86 = (bf16[32,256,128]{2,1,0:T(8,128)(2,1)S(1)}, bf16[2,512,1280]{2,1,0:T(8,128)(2,1)S(1)}) custom-call(s32[8,32]{1,0:T(8,128)S(1)} %shard_map.84.tab, bf16[128,5120]{1,0:T(8,128)(2,1)S(1)} %copy-done.8, bf16[128,5120]{1,0:T(8,128)(2,1)S(1)} %copy-done.9, bf16[2,128,1280]{2,1,0:T(8,128)(2,1)S(1)} %collective-permute-done.r1, ...), custom_call_target="tpu_custom_call" | custom-call | tf_op jit(solution)/shard_map/pallas_call | solution.py:58
  40.5 8.1 %all-to-all-start = ((bf16[32,256,128]{2,1,0:T(8,128)(2,1)}), bf16[32,256,128]{2,1,0:T(8,128)(2,1)}, u32[]{:S(2)}, u32[]{:S(2)}) async-start(bf16[32,256,128]{2,1,0:T(8,128)(2,1)} %copy-done.15), calls=%async_computation | async-start | bytes 4194304 | tf_op jit(solution)/shard_map/all_to_all | solution.py:226
  52.7 2.4 %collective-permute-start.4 = (bf16[2,128,1280]{2,1,0:T(8,128)(2,1)S(1)}, bf16[2,128,1280]{2,1,0:T(8,128)(2,1)S(1)}, u32[]{:S(2)}, u32[]{:S(2)}) collective-permute-start(bf16[2,128,1280]{2,1,0:T(8,128)(2,1)S(1)} %get-tuple-element.44), channel_id=1, source_target_pairs={{0,2},{1,3},{2,0},{3,1},{4,6},{5,7},{6,4},{7,5},{8,10},{9,11},{10,... | collective-permute-start | bytes 1966088 | tf_op jit(solution)/shard_map/ppermute | solution.py:118
  56.7 13.2 %collective-permute-done.3.r1 = bf16[2,128,1280]{2,1,0:T(8,128)(2,1)S(1)} collective-permute-done((bf16[2,128,1280]{2,1,0:T(8,128)(2,1)S(1)}, bf16[2,128,1280]{2,1,0:T(8,128)(2,1)S(1)}, u32[]{:S(2)}, u32[]{:S(2)}) %collective-permute-start.3) | collective-permute-done | bytes 655392 | tf_op jit(solution)/shard_map/ppermute | solution.py:118
  69.9 14.0 %collective-permute-done.4.r2 = bf16[2,128,1280]{2,1,0:T(8,128)(2,1)S(1)} collective-permute-done((bf16[2,128,1280]{2,1,0:T(8,128)(2,1)S(1)}, bf16[2,128,1280]{2,1,0:T(8,128)(2,1)S(1)}, u32[]{:S(2)}, u32[]{:S(2)}) %collective-permute-start.4) | collective-permute-done | bytes 655392 | tf_op jit(solution)/shard_map/ppermute | solution.py:118
  84.1 2.6 %shard_map.88 = (bf16[32,256,128]{2,1,0:T(8,128)(2,1)S(1)}, bf16[2,512,1280]{2,1,0:T(8,128)(2,1)S(1)}) custom-call(s32[8,32]{1,0:T(8,128)S(1)} %shard_map.84.tab, bf16[128,5120]{1,0:T(8,128)(2,1)S(1)} %copy-done.11, bf16[128,5120]{1,0:T(8,128)(2,1)S(1)} %copy-done.12, bf16[2,128,1280]{2,1,0:T(8,128)(2,1)S(1)} %collective-permute-done.3.r1, ...), custom_call_target="tpu_custom_call" | custom-call | tf_op jit(solution)/shard_map/pallas_call | solution.py:58
  89.6 7.4 %all-to-all-start.1 = ((bf16[32,256,128]{2,1,0:T(8,128)(2,1)}), bf16[32,256,128]{2,1,0:T(8,128)(2,1)}, u32[]{:S(2)}, u32[]{:S(2)}) async-start(bf16[32,256,128]{2,1,0:T(8,128)(2,1)} %copy-done.16), calls=%async_computation.1 | async-start | bytes 4194304 | tf_op jit(solution)/shard_map/all_to_all | solution.py:226
  97.0 11.2 %shard_map.89 = (bf16[20,256,512]{2,1,0:T(8,128)(2,1)S(1)}, f32[20,8,256]{2,1,0:T(8,128)S(1)}) custom-call(s32[8,32]{1,0:T(8,128)S(1)} %shard_map.84.tab, bf16[2,512,1280]{2,1,0:T(8,128)(2,1)S(1)} %get-tuple-element.42.kq_ref, bf16[32,256,128]{2,1,0:T(8,128)(2,1)} %all-to-all-done.slots.slots1), custom_call_target="tpu_custom_call" | custom-call | tf_op jit(solution)/shard_map/pallas_call | solution.py:58
  110.6 13.2 %all-to-all-done.1.slots.slots2 = bf16[32,256,128]{2,1,0:T(8,128)(2,1)} async-done(((bf16[32,256,128]{2,1,0:T(8,128)(2,1)}), bf16[32,256,128]{2,1,0:T(8,128)(2,1)}, u32[]{:S(2)}, u32[]{:S(2)}) %all-to-all-start.1) | async-done | bytes 2097184 | tf_op jit(solution)/shard_map/all_to_all | solution.py:226
  125.6 2.5 %copy-done.6 = bf16[20,256,512]{2,1,0:T(8,128)(2,1)S(1)} copy-done((bf16[20,256,512]{2,1,0:T(8,128)(2,1)S(1)}, bf16[20,256,512]{2,1,0:T(8,128)(2,1)}, u32[]{:S(2)}) %copy-start.6) | copy-done | bytes 5242904
  128.0 7.8 %shard_map.90 = (bf16[128,1280]{1,0:T(8,128)(2,1)S(1)}, bf16[128,1280]{1,0:T(8,128)(2,1)}, bf16[128,1280]{1,0:T(8,128)(2,1)}, bf16[128,1280]{1,0:T(8,128)(2,1)S(1)}, bf16[512,1280]{1,0:T(8,128)(2,1)S(1)}) custom-call(s32[8,32]{1,0:T(8,128)S(1)} %shard_map.84.tab, bf16[20,256,512]{2,1,0:T(8,128)(2,1)S(1)} %copy-done.6, bf16[2,512,1280]{2,1,0:T(8,128)(2,1)S(1)} %copy-done.1, ...), custom_call_target="tpu_custom_call" | custom-call | tf_op jit(solution)/shard_map/pallas_call | solution.py:58
  137.7 2.4 %collective-permute-start.7 = (bf16[128,1280]{1,0:T(8,128)(2,1)}, bf16[128,1280]{1,0:T(8,128)(2,1)}, u32[]{:S(2)}, u32[]{:S(2)}) collective-permute-start(bf16[128,1280]{1,0:T(8,128)(2,1)} %get-tuple-element.54), channel_id=1, source_target_pairs={{0,2},{1,3},{2,0},{3,1},{4,6},{5,7},{6,4},{7,5},{8,10},{9,11},{10,... | collective-permute-start | bytes 983048 | tf_op jit(solution)/shard_map/ppermute | solution.py:118
  140.0 14.4 %shard_map.92 = (bf16[128,1280]{1,0:T(8,128)(2,1)S(1)}, bf16[128,1280]{1,0:T(8,128)(2,1)S(1)}, bf16[128,1280]{1,0:T(8,128)(2,1)S(1)}, bf16[128,1280]{1,0:T(8,128...) custom-call(s32[8,32]{1,0:T(8,128)S(1)} %shard_map.84.tab, bf16[20,256,512]{2,1,0:T(8,128)(2,1)} %copy-done.5, ...), custom_call_target="tpu_custom_call" | custom-call | tf_op jit(solution)/shard_map/pallas_call | solution.py:58
  158.7 6.5 %all-to-all-start.2 = ((f32[32,8,256]{2,1,0:T(8,128)}), f32[32,8,256]{2,1,0:T(8,128)S(1)}, u32[]{:S(2)}, u32[]{:S(2)}) async-start(f32[32,8,256]{2,1,0:T(8,128)} %copy-done.19), calls=%async_computation.2 | async-start | bytes 524288 | tf_op jit(solution)/shard_map/all_to_all | solution.py:226
  171.2 8.2 %shard_map.94 = (f32[512,1280]{1,0:T(8,128)S(1)}, f32[512,1280]{1,0:T(8,128)S(1)}) custom-call(s32[8,32]{1,0:T(8,128)S(1)} %shard_map.84.tab, bf16[2,512,1280]{2,1,0:T(8,128)(2,1)S(1)} %get-tuple-element.42.kq_ref, bf16[2,512,1280]{2,1,0:T(8,128)(2,1)S(1)} %copy-done.3, f32[20,8,256]{2,1,0:T(8,128)S(1)} %copy-done.21), custom_call_target="tpu_custom_call" | custom-call | tf_op jit(solution)/shard_map/pallas_call | solution.py:58
  184.1 12.9 %shard_map.95 = (bf16[128,1280]{1,0:T(8,128)(2,1)S(1)}, bf16[128,1280]{1,0:T(8,128)(2,1)S(1)}, bf16[128,1280]{1,0:T(8,128)(2,1)S(1)}, bf16[128,1280]{1,0:T(8,128...) custom-call(s32[8,32]{1,0:T(8,128)S(1)} %shard_map.84.tab, ...), custom_call_target="tpu_custom_call" | custom-call | tf_op jit(solution)/shard_map/pallas_call | solution.py:58
  203.9 9.4 %collective-permute-done.11.r3 = bf16[128,1280]{1,0:T(8,128)(2,1)S(1)} collective-permute-done((bf16[128,1280]{1,0:T(8,128)(2,1)S(1)}, bf16[128,1280]{1,0:T(8,128)(2,1)S(1)}, u32[]{:S(2)}, u32[]{:S(2)}) %collective-permute-start.11) | collective-permute-done | bytes 327712 | tf_op jit(solution)/shard_map/ppermute | solution.py:118
  213.3 2.8 %collective-permute-start.16 = (bf16[128,1280]{1,0:T(8,128)(2,1)S(1)}, bf16[128,1280]{1,0:T(8,128)(2,1)S(1)}, u32[]{:S(2)}, u32[]{:S(2)}) collective-permute-start(bf16[128,1280]{1,0:T(8,128)(2,1)S(1)} %get-tuple-element.72), channel_id=1, source_target_pairs={{0,2},{1,3},{2,0},{3,1},{4,6},{5,7},{6,4},{7,5},{8,10},{9,11},{10,... | collective-permute-start | bytes 983048 | tf_op jit(solution)/shard_map/ppermute | solution.py:118
  223.8 3.5 %collective-permute-done.14.r3 = bf16[128,1280]{1,0:T(8,128)(2,1)S(1)} collective-permute-done((bf16[128,1280]{1,0:T(8,128)(2,1)S(1)}, bf16[128,1280]{1,0:T(8,128)(2,1)S(1)}, u32[]{:S(2)}, u32[]{:S(2)}) %collective-permute-start.14) | collective-permute-done | bytes 327712 | tf_op jit(solution)/shard_map/ppermute | solution.py:118
  228.9 4.7 %collective-permute-done.17.r3 = bf16[128,1280]{1,0:T(8,128)(2,1)S(1)} collective-permute-done((bf16[128,1280]{1,0:T(8,128)(2,1)S(1)}, bf16[128,1280]{1,0:T(8,128)(2,1)S(1)}, u32[]{:S(2)}, u32[]{:S(2)}) %collective-permute-start.17) | collective-permute-done | bytes 327712 | tf_op jit(solution)/shard_map/ppermute | solution.py:118
  (88 shorter events, 54.0 us)
Async XLA Ops:
  3.3 33.3 %copy-start.8 = (bf16[128,5120]{1,0:T(8,128)(2,1)S(1)}, bf16[128,5120]{1,0:T(8,128)(2,1)}, u32[]{:S(2)}) copy-start(bf16[128,5120]{1,0:T(8,128)(2,1)} %a_ref.5) | copy-start | bytes 3932164
  3.5 17.8 %collective-permute-start = (bf16[2,128,1280]{2,1,0:T(8,128)(2,1)S(1)}, bf16[2,128,1280]{2,1,0:T(8,128)(2,1)S(1)}, u32[]{:S(2)}, u32[]{:S(2)}) collective-permute-start(bf16[2,128,1280]{2,1,0:T(8,128)(2,1)S(1)} %get-tuple-element.39), channel_id=1, source_target_pairs={{0,1},{1,2},{2,3},{3,0},{4,5},{5,6},{6,7},{7,4},{8,9},{9,10},{10,1... | collective-permute-start | bytes 1966088 | tf_op jit(solution)/shard_map/ppermute | solution.py:118
  5.2 31.4 %collective-permute-start.1 = (bf16[2,128,1280]{2,1,0:T(8,128)(2,1)S(1)}, bf16[2,128,1280]{2,1,0:T(8,128)(2,1)S(1)}, u32[]{:S(2)}, u32[]{:S(2)}) collective-permute-start(bf16[2,128,1280]{2,1,0:T(8,128)(2,1)S(1)} %get-tuple-element.40), channel_id=1, source_target_pairs={{0,2},{1,3},{2,0},{3,1},{4,6},{5,7},{6,4},{7,5},{8,10},{9,11},{10,... | collective-permute-start | bytes 1966088 | tf_op jit(solution)/shard_map/ppermute | solution.py:118
  8.1 28.5 %collective-permute-start.2 = (bf16[2,128,1280]{2,1,0:T(8,128)(2,1)S(1)}, bf16[2,128,1280]{2,1,0:T(8,128)(2,1)S(1)}, u32[]{:S(2)}, u32[]{:S(2)}) collective-permute-start(bf16[2,128,1280]{2,1,0:T(8,128)(2,1)S(1)} %get-tuple-element.41), channel_id=1, source_target_pairs={{0,3},{1,0},{2,1},{3,2},{4,7},{5,4},{6,5},{7,6},{8,11},{9,8},{10,9... | collective-permute-start | bytes 1966088 | tf_op jit(solution)/shard_map/ppermute | solution.py:118
  40.5 49.1 %all-to-all-start = ((bf16[32,256,128]{2,1,0:T(8,128)(2,1)}), bf16[32,256,128]{2,1,0:T(8,128)(2,1)}, u32[]{:S(2)}, u32[]{:S(2)}) async-start(bf16[32,256,128]{2,1,0:T(8,128)(2,1)} %copy-done.15), calls=%async_computation | async-start | bytes 4194304 | tf_op jit(solution)/shard_map/all_to_all | solution.py:226
  51.2 32.9 %copy-start.11 = (bf16[128,5120]{1,0:T(8,128)(2,1)S(1)}, bf16[128,5120]{1,0:T(8,128)(2,1)}, u32[]{:S(2)}) copy-start(bf16[128,5120]{1,0:T(8,128)(2,1)} %a_ref.7) | copy-start | bytes 3932164
  51.4 18.5 %collective-permute-start.3 = (bf16[2,128,1280]{2,1,0:T(8,128)(2,1)S(1)}, bf16[2,128,1280]{2,1,0:T(8,128)(2,1)S(1)}, u32[]{:S(2)}, u32[]{:S(2)}) collective-permute-start(bf16[2,128,1280]{2,1,0:T(8,128)(2,1)S(1)} %get-tuple-element.43), channel_id=1, source_target_pairs={{0,1},{1,2},{2,3},{3,0},{4,5},{5,6},{6,7},{7,4},{8,9},{9,10},{10,1... | collective-permute-start | bytes 1966088 | tf_op jit(solution)/shard_map/ppermute | solution.py:118
  52.7 31.2 %collective-permute-start.4 = (bf16[2,128,1280]{2,1,0:T(8,128)(2,1)S(1)}, bf16[2,128,1280]{2,1,0:T(8,128)(2,1)S(1)}, u32[]{:S(2)}, u32[]{:S(2)}) collective-permute-start(bf16[2,128,1280]{2,1,0:T(8,128)(2,1)S(1)} %get-tuple-element.44), channel_id=1, source_target_pairs={{0,2},{1,3},{2,0},{3,1},{4,6},{5,7},{6,4},{7,5},{8,10},{9,11},{10,... | collective-permute-start | bytes 1966088 | tf_op jit(solution)/shard_map/ppermute | solution.py:118
  55.1 29.0 %collective-permute-start.5 = (bf16[2,128,1280]{2,1,0:T(8,128)(2,1)S(1)}, bf16[2,128,1280]{2,1,0:T(8,128)(2,1)S(1)}, u32[]{:S(2)}, u32[]{:S(2)}) collective-permute-start(bf16[2,128,1280]{2,1,0:T(8,128)(2,1)S(1)} %get-tuple-element.45), channel_id=1, source_target_pairs={{0,3},{1,0},{2,1},{3,2},{4,7},{5,4},{6,5},{7,6},{8,11},{9,8},{10,9... | collective-permute-start | bytes 1966088 | tf_op jit(solution)/shard_map/ppermute | solution.py:118
  89.6 34.2 %all-to-all-start.1 = ((bf16[32,256,128]{2,1,0:T(8,128)(2,1)}), bf16[32,256,128]{2,1,0:T(8,128)(2,1)}, u32[]{:S(2)}, u32[]{:S(2)}) async-start(bf16[32,256,128]{2,1,0:T(8,128)(2,1)} %copy-done.16), calls=%async_computation.1 | async-start | bytes 4194304 | tf_op jit(solution)/shard_map/all_to_all | solution.py:226
  135.9 61.2 %collective-permute-start.6 = (bf16[128,1280]{1,0:T(8,128)(2,1)}, bf16[128,1280]{1,0:T(8,128)(2,1)S(1)}, u32[]{:S(2)}, u32[]{:S(2)}) collective-permute-start(bf16[128,1280]{1,0:T(8,128)(2,1)} %get-tuple-element.53), channel_id=1, source_target_pairs={{0,1},{1,2},{2,3},{3,0},{4,5},{5,6},{6,7},{7,4},{8,9},{9,10},{10,1... | collective-permute-start | bytes 983048 | tf_op jit(solution)/shard_map/ppermute | solution.py:118
  137.7 61.0 %collective-permute-start.7 = (bf16[128,1280]{1,0:T(8,128)(2,1)}, bf16[128,1280]{1,0:T(8,128)(2,1)}, u32[]{:S(2)}, u32[]{:S(2)}) collective-permute-start(bf16[128,1280]{1,0:T(8,128)(2,1)} %get-tuple-element.54), channel_id=1, source_target_pairs={{0,2},{1,3},{2,0},{3,1},{4,6},{5,7},{6,4},{7,5},{8,10},{9,11},{10,... | collective-permute-start | bytes 983048 | tf_op jit(solution)/shard_map/ppermute | solution.py:118
  158.7 23.6 %all-to-all-start.2 = ((f32[32,8,256]{2,1,0:T(8,128)}), f32[32,8,256]{2,1,0:T(8,128)S(1)}, u32[]{:S(2)}, u32[]{:S(2)}) async-start(f32[32,8,256]{2,1,0:T(8,128)} %copy-done.19), calls=%async_computation.2 | async-start | bytes 524288 | tf_op jit(solution)/shard_map/all_to_all | solution.py:226
  165.3 34.0 %collective-permute-start.8 = (bf16[128,1280]{1,0:T(8,128)(2,1)}, bf16[128,1280]{1,0:T(8,128)(2,1)}, u32[]{:S(2)}, u32[]{:S(2)}) collective-permute-start(bf16[128,1280]{1,0:T(8,128)(2,1)} %copy-done.26), channel_id=1, source_target_pairs={{0,3},{1,0},{2,1},{3,2},{4,7},{5,4},{6,5},{7,6},{8,11},{9,8},{10,9... | collective-permute-start | bytes 983048 | tf_op jit(solution)/shard_map/ppermute | solution.py:118
  166.5 35.1 %collective-permute-start.9 = (bf16[128,1280]{1,0:T(8,128)(2,1)}, bf16[128,1280]{1,0:T(8,128)(2,1)}, u32[]{:S(2)}, u32[]{:S(2)}) collective-permute-start(bf16[128,1280]{1,0:T(8,128)(2,1)} %copy-done.27), channel_id=1, source_target_pairs={{0,1},{1,2},{2,3},{3,0},{4,5},{5,6},{6,7},{7,4},{8,9},{9,10},{10,1... | collective-permute-start | bytes 983048 | tf_op jit(solution)/shard_map/ppermute | solution.py:118
  167.4 36.5 %collective-permute-start.10 = (bf16[128,1280]{1,0:T(8,128)(2,1)}, bf16[128,1280]{1,0:T(8,128)(2,1)}, u32[]{:S(2)}, u32[]{:S(2)}) collective-permute-start(bf16[128,1280]{1,0:T(8,128)(2,1)} %copy-done.25), channel_id=1, source_target_pairs={{0,2},{1,3},{2,0},{3,1},{4,6},{5,7},{6,4},{7,5},{8,10},{9,11},{10,... | collective-permute-start | bytes 983048 | tf_op jit(solution)/shard_map/ppermute | solution.py:118
  197.0 24.6 %copy-start.18 = (bf16[128,1280]{1,0:T(8,128)(2,1)S(1)}, bf16[128,1280]{1,0:T(8,128)(2,1)}, u32[]{:S(2)}) copy-start(bf16[128,1280]{1,0:T(8,128)(2,1)} %copy-done.17) | copy-start | bytes 983044
  197.1 16.2 %collective-permute-start.11 = (bf16[128,1280]{1,0:T(8,128)(2,1)S(1)}, bf16[128,1280]{1,0:T(8,128)(2,1)S(1)}, u32[]{:S(2)}, u32[]{:S(2)}) collective-permute-start(bf16[128,1280]{1,0:T(8,128)(2,1)S(1)} %copy-done.24), channel_id=1, source_target_pairs={{0,3},{1,0},{2,1},{3,2},{4,7},{5,4},{6,5},{7,6},{8,11},{9,8},{10,9... | collective-permute-start | bytes 983048 | tf_op jit(solution)/shard_map/ppermute | solution.py:118
  198.7 18.8 %collective-permute-start.12 = (bf16[128,1280]{1,0:T(8,128)(2,1)S(1)}, bf16[128,1280]{1,0:T(8,128)(2,1)S(1)}, u32[]{:S(2)}, u32[]{:S(2)}) collective-permute-start(bf16[128,1280]{1,0:T(8,128)(2,1)S(1)} %get-tuple-element.67), channel_id=1, source_target_pairs={{0,1},{1,2},{2,3},{3,0},{4,5},{5,6},{6,7},{7,4},{8,9},{9,10},{10,1... | collective-permute-start | bytes 983048 | tf_op jit(solution)/shard_map/ppermute | solution.py:118
  199.3 24.5 %collective-permute-start.13 = (bf16[128,1280]{1,0:T(8,128)(2,1)S(1)}, bf16[128,1280]{1,0:T(8,128)(2,1)S(1)}, u32[]{:S(2)}, u32[]{:S(2)}) collective-permute-start(bf16[128,1280]{1,0:T(8,128)(2,1)S(1)} %get-tuple-element.68), channel_id=1, source_target_pairs={{0,2},{1,3},{2,0},{3,1},{4,6},{5,7},{6,4},{7,5},{8,10},{9,11},{10,... | collective-permute-start | bytes 983048 | tf_op jit(solution)/shard_map/ppermute | solution.py:118
  201.5 25.7 %collective-permute-start.14 = (bf16[128,1280]{1,0:T(8,128)(2,1)S(1)}, bf16[128,1280]{1,0:T(8,128)(2,1)S(1)}, u32[]{:S(2)}, u32[]{:S(2)}) collective-permute-start(bf16[128,1280]{1,0:T(8,128)(2,1)S(1)} %get-tuple-element.69), channel_id=1, source_target_pairs={{0,3},{1,0},{2,1},{3,2},{4,7},{5,4},{6,5},{7,6},{8,11},{9,8},{10,9... | collective-permute-start | bytes 983048 | tf_op jit(solution)/shard_map/ppermute | solution.py:118
  203.9 25.0 %collective-permute-start.15 = (bf16[128,1280]{1,0:T(8,128)(2,1)S(1)}, bf16[128,1280]{1,0:T(8,128)(2,1)S(1)}, u32[]{:S(2)}, u32[]{:S(2)}) collective-permute-start(bf16[128,1280]{1,0:T(8,128)(2,1)S(1)} %get-tuple-element.71), channel_id=1, source_target_pairs={{0,1},{1,2},{2,3},{3,0},{4,5},{5,6},{6,7},{7,4},{8,9},{9,10},{10,1... | collective-permute-start | bytes 983048 | tf_op jit(solution)/shard_map/ppermute | solution.py:118
  213.3 15.6 %collective-permute-start.16 = (bf16[128,1280]{1,0:T(8,128)(2,1)S(1)}, bf16[128,1280]{1,0:T(8,128)(2,1)S(1)}, u32[]{:S(2)}, u32[]{:S(2)}) collective-permute-start(bf16[128,1280]{1,0:T(8,128)(2,1)S(1)} %get-tuple-element.72), channel_id=1, source_target_pairs={{0,2},{1,3},{2,0},{3,1},{4,6},{5,7},{6,4},{7,5},{8,10},{9,11},{10,... | collective-permute-start | bytes 983048 | tf_op jit(solution)/shard_map/ppermute | solution.py:118
  217.5 16.1 %collective-permute-start.17 = (bf16[128,1280]{1,0:T(8,128)(2,1)S(1)}, bf16[128,1280]{1,0:T(8,128)(2,1)S(1)}, u32[]{:S(2)}, u32[]{:S(2)}) collective-permute-start(bf16[128,1280]{1,0:T(8,128)(2,1)S(1)} %get-tuple-element.73), channel_id=1, source_target_pairs={{0,3},{1,0},{2,1},{3,2},{4,7},{5,4},{6,5},{7,6},{8,11},{9,8},{10,9... | collective-permute-start | bytes 983048 | tf_op jit(solution)/shard_map/ppermute | solution.py:118
  (25 other events, 77.3 us)

commit v2 on v1

v2 whole, which is shorter than its diff:
```python
import jax
import jax.numpy as jnp
from jax import lax
from jax.experimental import pallas as pl
from jax.experimental.pallas import tpu as pltpu
from jax.sharding import PartitionSpec as P


HEAD_DIM = 128
BLOCK = 256
GROUPS = 10
CTX = 32
TP = 4
TOK = 128
ROWS = TP * TOK
COLS = GROUPS * HEAD_DIM
SCALE = HEAD_DIM ** (-0.5)
F32 = jnp.float32
BF16 = jnp.bfloat16


ANY = pl.BlockSpec(memory_space=pl.ANY)
SMEM = pl.BlockSpec(memory_space=pltpu.SMEM)
VMEM = pl.BlockSpec(memory_space=pltpu.VMEM)
HBM = pl.BlockSpec(memory_space=pltpu.HBM)


ITEMS = 2 * GROUPS
PARAMS = pltpu.CompilerParams(vmem_limit_bytes=40 * 1024 * 1024)


def shape(dims, dtype=BF16):
    return jax.ShapeDtypeStruct(dims, dtype)


def peer(step):
    return lax.rem(lax.axis_index("tp") + step, TP)


def col_slice(index):
    return pl.ds(pl.multiple_of(index * COLS, COLS), COLS)


def row_slice(index):
    return pl.ds(pl.multiple_of(index * TOK, TOK), TOK)


def block_slice(index):
    return pl.ds(pl.multiple_of(index * BLOCK, BLOCK), BLOCK)


def head_slice(index):
    return pl.ds(pl.multiple_of(index * HEAD_DIM, HEAD_DIM), HEAD_DIM)


def call(kernel, out_shape, in_specs, out_specs, scratch):
    many = isinstance(out_shape, list)
    outs = out_shape if many else [out_shape]
    specs = out_specs if many else [out_specs]
    outs = [
        pltpu.HBM(out.shape, out.dtype) if spec is HBM else out for out, spec in zip(outs, specs)
    ]

    def run(*operands):
        operands = [
            pltpu.with_memory_space_constraint(operand, pltpu.HBM) if spec is HBM else operand
            for operand, spec in zip(operands, in_specs)
        ]
        return pl.pallas_call(
            kernel,
            out_shape=outs if many else outs[0],
            in_specs=in_specs,
            out_specs=out_specs,
            scratch_shapes=scratch,
            compiler_params=PARAMS,
        )(*operands)

    return run


def run_copies(copies):
    for copy in copies:
        copy.start()
    for copy in copies:
        copy.wait()


def cut_kernel(a_ref, b_ref, p1, p2, p3, sems):
    copies = []
    for step, out in ((1, p1), (2, p2), (3, p3)):
        for which, ref in enumerate((a_ref, b_ref)):
            copies.append(
                pltpu.make_async_copy(
                    ref.at[:, col_slice(peer(step))], out.at[which], sems.at[len(copies)]
                )
            )
    run_copies(copies)


def cut(a, b):
    return call(
        cut_kernel,
        [shape((2, TOK, COLS))] * 3,
        [HBM] * 2,
        [VMEM] * 3,
        [pltpu.SemaphoreType.DMA((6,))],
    )(a, b)


def join_kernel(own, r1, r2, r3, out, sems):
    copies = []
    for step, ref in ((0, own), (1, r1), (2, r2), (3, r3)):
        copies.append(
            pltpu.make_async_copy(ref, out.at[:, col_slice(peer(TP - step))], sems.at[step])
        )
    run_copies(copies)


def join(own, received):
    return call(
        join_kernel, shape((TOK, TP * COLS)), [VMEM] * 4, HBM, [pltpu.SemaphoreType.DMA((4,))]
    )(own, *received)


def exchange(pieces):
    received = []
    for step, piece in zip((1, 2, 3), pieces):
        received.append(
            lax.ppermute(piece, "tp", [(i, (i + step) % TP) for i in range(TP)])
        )
    return tuple(received)


def gather_copies(a_ref, b_ref, received, held, sems, base):
    copies = []
    for which, ref in enumerate((a_ref, b_ref)):
        copies.append(
            pltpu.make_async_copy(
                ref.at[:, col_slice(peer(0))],
                held.at[which, row_slice(peer(0))],
                sems.at[base + len(copies)],
            )
        )
    for step, ref in zip((1, 2, 3), received):
        for which in range(2):
            copies.append(
                pltpu.make_async_copy(
                    ref.at[which],
                    held.at[which, row_slice(peer(TP - step))],
                    sems.at[base + len(copies)],
                )
            )
    return copies


def table_kernel(match, tab):
    ctx = lax.axis_index("ctx")

    def clear(d, carry):
        for row in range(5):
            tab[row, d] = 0
        return carry

    lax.fori_loop(0, CTX, clear, 0)

    def owner_side(d, carry):
        for n in range(2):
            for g in range(GROUPS):
                block = 2 * d + n
                m = match[g, block]

                @pl.when((m < block) & ((m >> 1) == ctx))
                def _():
                    tab[0, d] = m & 1
                    tab[1, d] = g
                    tab[2, d] = 1

        return carry

    lax.fori_loop(ctx + 1, CTX, owner_side, 0)
    for n in range(2):
        for g in range(GROUPS):
            block = 2 * ctx + n
            m = match[g, block]
            source = m >> 1
            item = n * GROUPS + g

            @pl.when((m < block) & (source != ctx))
            def _():
                tab[0, source] = n
                tab[1, source] = g
                tab[2, source] = 1
                tab[3, item] = 1
                tab[4, item] = source

            @pl.when((m < block) & (source == ctx))
            def _():
                tab[3, item] = 2


def make_table(match):
    return call(table_kernel, shape((8, CTX), jnp.int32), [SMEM], SMEM, [])(match)


def pack_kernel(tab, a_ref, b_ref, r1, r2, r3, out, held_out, held, sems, slot_sems):
    ctx = lax.axis_index("ctx")
    run_copies(gather_copies(a_ref, b_ref, (r1, r2, r3), held, sems, 0))
    copies = []
    for d in range(CTX):
        which = jnp.where(ctx > d, 1, 0)
        copies.append(
            pltpu.make_async_copy(
                held.at[which, block_slice(tab[0, d]), head_slice(tab[1, d])],
                out.at[d],
                slot_sems.at[d],
            )
        )
    copies.append(pltpu.make_async_copy(held, held_out, slot_sems.at[CTX]))
    run_copies(copies)


def pack(tab, a, b, received):
    return call(
        pack_kernel,
        [shape((CTX, BLOCK, HEAD_DIM)), shape((2, ROWS, COLS))],
        [SMEM] + [HBM] * 2 + [ANY] * 3,
        [HBM] * 2,
        [
            pltpu.VMEM((2, ROWS, COLS), BF16),
            pltpu.SemaphoreType.DMA((8,)),
            pltpu.SemaphoreType.DMA((CTX + 1,)),
        ],
    )(tab, a, b, *received)


def swap(slots):
    return lax.all_to_all(slots, "ctx", split_axis=0, concat_axis=0, tiled=True)


def dot(a, b):
    return lax.dot_general(a, b, (((1,), (0,)), ((), ())), preferred_element_type=F32)


def dot_t(a, b):
    return lax.dot_general(a, b, (((1,), (1,)), ((), ())), preferred_element_type=F32)


def dot_n(a, b):
    return lax.dot_general(a, b, (((0,), (0,)), ((), ())), preferred_element_type=F32)


STEP = 2
WIDE = STEP * HEAD_DIM
PAIR = pl.BlockSpec((2, ROWS, WIDE), lambda j, tab: (0, 0, j))
SECOND = pl.BlockSpec((1, ROWS, WIDE), lambda j, tab: (1, 0, j))
HEADS_ONE = pl.BlockSpec((ROWS, WIDE), lambda j, tab: (0, j))
PIECE = pl.BlockSpec((TOK, WIDE), lambda j, tab: (0, j))
PROBS = pl.BlockSpec((2, STEP, BLOCK, 2 * BLOCK), lambda j, tab: (0, j, 0, 0))
STATS = pl.BlockSpec((2, STEP, 8, BLOCK), lambda j, tab: (0, j, 0, 0))


def far_spec(n, u):
    return pl.BlockSpec(
        (1, BLOCK, HEAD_DIM), lambda j, tab: (tab[4, n * GROUPS + j * STEP + u], 0, 0)
    )


LANES = [(u, n) for u in range(STEP) for n in range(2)]
FAR = [far_spec(n, u) for u, n in LANES]
LOW, HIGH = pl.ds(0, BLOCK), pl.ds(BLOCK, BLOCK)


def lanes(j):
    for index, (u, n) in enumerate(LANES):
        yield index, u, n, j * STEP + u, pl.ds(n * BLOCK, BLOCK), pl.ds(u * HEAD_DIM, HEAD_DIM)


def by_group(kernel, out_shape, in_specs, out_specs, scratch, free=()):
    def run(tab, *operands):
        outs = [pltpu.HBM(out.shape, out.dtype) for out in out_shape]
        operands = [
            x if index in free else pltpu.with_memory_space_constraint(x, pltpu.HBM)
            for index, x in enumerate(operands)
        ]
        return pl.pallas_call(
            kernel,
            out_shape=outs,
            grid_spec=pltpu.PrefetchScalarGridSpec(
                num_scalar_prefetch=1,
                grid=(GROUPS // STEP,),
                in_specs=in_specs,
                out_specs=out_specs,
                scratch_shapes=scratch,
            ),
            compiler_params=PARAMS,
        )(tab, *operands)

    return run


def matched(tab, g, n, received, low):
    if n == 0:
        return received[0]
    return jnp.where(tab[3, GROUPS + g] == 2, low, received[0])


def prob_kernel(tab, kq, dout, *refs):
    far, (prob, lse_out, gv) = refs[: len(FAR)], refs[len(FAR) :]
    causal = lax.broadcasted_iota(jnp.int32, (BLOCK, BLOCK), 0) >= lax.broadcasted_iota(
        jnp.int32, (BLOCK, BLOCK), 1
    )
    for index, u, n, g, rows, cols in lanes(pl.program_id(0)):
        q = kq[1, rows, cols]
        kf = matched(tab, g, n, far[index], kq[0, LOW, cols])
        s_own = jnp.where(causal, dot_t(q, kq[0, rows, cols]) * SCALE, -jnp.inf)
        s_far = jnp.where(tab[3, n * GROUPS + g] > 0, dot_t(q, kf) * SCALE, -jnp.inf)
        top = jnp.maximum(
            jnp.max(s_own, axis=1, keepdims=True), jnp.max(s_far, axis=1, keepdims=True)
        )
        e_own = jnp.exp(s_own - top)
        e_far = jnp.exp(s_far - top)
        total = jnp.sum(e_own, axis=1, keepdims=True) + jnp.sum(e_far, axis=1, keepdims=True)
        inverse = 1.0 / total
        p_own = (e_own * inverse).astype(BF16)
        prob[n, u, :, LOW] = p_own
        prob[n, u, :, HIGH] = (e_far * inverse).astype(BF16)
        gv[rows, cols] = dot_n(p_own, dout[0, rows, cols])
        lse = jnp.broadcast_to(top + jnp.log(total), (BLOCK, HEAD_DIM))
        lse_out[n, u] = jnp.transpose(lse)[0:8]
    for index, u, n, g, rows, cols in lanes(pl.program_id(0)):
        if n == 1:

            @pl.when(tab[3, GROUPS + g] == 2)
            def _():
                gv[LOW, cols] += dot_n(prob[1, u, :, HIGH], dout[0, HIGH, cols])


def prob_side(tab, kq, vd, slots):
    return by_group(
        prob_kernel,
        [
            shape((2, GROUPS, BLOCK, 2 * BLOCK)),
            shape((2, GROUPS, 8, BLOCK), F32),
            shape((ROWS, COLS), F32),
        ],
        [PAIR, SECOND] + FAR,
        [PROBS, STATS, HEADS_ONE],
        [],
    )(tab, kq, vd, *[slots] * len(FAR))


def piece_copies(result, outs, sems):
    return [
        pltpu.make_async_copy(result.at[row_slice(peer(move))], out, sems.at[move])
        for move, out in enumerate(outs)
    ]


def start_all(copies):
    for copy in copies:
        copy.start()


def wait_all(copies):
    for copy in copies:
        copy.wait()


def value_kernel(tab, prob, lse, vd, *refs):
    far, (own, p1, p2, p3, full, stats_slots, stats, slot_sems) = (
        refs[: len(FAR)],
        refs[len(FAR) :],
    )
    j = pl.program_id(0)
    ctx = lax.axis_index("ctx")
    sublane = lax.broadcasted_iota(jnp.int32, (8, BLOCK), 0)
    for index, u, n, g, rows, cols in lanes(j):
        vf = matched(tab, g, n, far[index], vd[0, LOW, cols])
        att = dot(prob[n, u, :, LOW], vd[0, rows, cols]) + dot(prob[n, u, :, HIGH], vf)
        att = att.astype(BF16)
        full[rows, cols] = att
        delta = jnp.sum(vd[1, rows, cols].astype(F32) * att.astype(F32), axis=1, keepdims=True)
        turned = jnp.transpose(jnp.broadcast_to(delta, (BLOCK, HEAD_DIM)))[0:8]
        stats[n * GROUPS + g] = jnp.where(sublane == 0, lse[n, u], turned)
    for move, out in enumerate((own, p1, p2, p3)):
        out[...] = full[row_slice(peer(move))]

    @pl.when(j == GROUPS // STEP - 1)
    def _():
        copies = []
        for d in range(CTX):
            item = jnp.where(ctx > d, tab[0, d] * GROUPS + tab[1, d], 0)
            copies.append(
                pltpu.make_async_copy(stats.at[item], stats_slots.at[d], slot_sems.at[d])
            )
        run_copies(copies)


def value_side(tab, prob, lse, vd, slots):
    return by_group(
        value_kernel,
        [shape((TOK, COLS))] * 4 + [shape((ROWS, COLS)), shape((CTX, 8, BLOCK), F32)],
        [PROBS, STATS, PAIR] + FAR,
        [PIECE] * 4 + [HEADS_ONE, HBM],
        [pltpu.VMEM((ITEMS, 8, BLOCK), F32), pltpu.SemaphoreType.DMA((CTX,))],
        free=range(3, 3 + len(FAR)),
    )(tab, prob, lse, vd, *[slots] * len(FAR))


def query_kernel(tab, prob, kq, vd, att, *refs):
    count = len(FAR)
    far_k, far_v = refs[:count], refs[count : 2 * count]
    own, p1, p2, p3, gk, result, ds_last = refs[2 * count :]
    for index, u, n, g, rows, cols in lanes(pl.program_id(0)):
        do = vd[1, rows, cols]
        kf = matched(tab, g, n, far_k[index], kq[0, LOW, cols])
        vf = matched(tab, g, n, far_v[index], vd[0, LOW, cols])
        delta = jnp.sum(do.astype(F32) * att[rows, cols].astype(F32), axis=1, keepdims=True)
        p_own = prob[n, u, :, LOW].astype(F32)
        p_far = prob[n, u, :, HIGH].astype(F32)
        ds_own = (p_own * (dot_t(do, vd[0, rows, cols]) - delta) * SCALE).astype(BF16)
        ds_far = (p_far * (dot_t(do, vf) - delta) * SCALE).astype(BF16)
        result[rows, cols] = (dot(ds_own, kq[0, rows, cols]) + dot(ds_far, kf)).astype(BF16)
        gk[rows, cols] = dot_n(ds_own, kq[1, rows, cols])
        if n == 1:
            ds_last[u] = ds_far
    for move, out in enumerate((own, p1, p2, p3)):
        out[...] = result[row_slice(peer(move))]
    for index, u, n, g, rows, cols in lanes(pl.program_id(0)):
        if n == 1:

            @pl.when(tab[3, GROUPS + g] == 2)
            def _():
                gk[LOW, cols] += dot_n(ds_last[u], kq[1, HIGH, cols])


def query_side(tab, prob, kq, vd, att, slots1, slots2):
    return by_group(
        query_kernel,
        [shape((TOK, COLS))] * 4 + [shape((ROWS, COLS), F32)],
        [PROBS, PAIR, PAIR, HEADS_ONE] + FAR + FAR,
        [PIECE] * 4 + [HEADS_ONE],
        [pltpu.VMEM((ROWS, WIDE), BF16), pltpu.VMEM((STEP, BLOCK, BLOCK), BF16)],
    )(tab, prob, kq, vd, att, *[slots1] * len(FAR), *[slots2] * len(FAR))


def key_terms(k, v, q, do, stats):
    p = jnp.exp(dot_t(k, q) * SCALE - stats[0:1])
    ds = (p * (dot_t(v, do) - stats[1:2]) * SCALE).astype(BF16)
    return dot(ds, q), dot(p.astype(BF16), do)


def far_kernel(
    tab, kq_ref, vd_ref, slots1, slots2, stats, gk_ref, gv_ref,
    ko, k1, k2, k3, vo, v1, v2, v3,
    k, v, far_q, far_do, near, acc, result, sems, slot_sems, out_sems,
):
    ctx = lax.axis_index("ctx")

    def slot_copies(d):
        return [
            pltpu.make_async_copy(slots1.at[d], far_q.at[d], slot_sems.at[0, d]),
            pltpu.make_async_copy(slots2.at[d], far_do.at[d], slot_sems.at[1, d]),
        ]

    def start_slot(d, carry):
        start_all(slot_copies(d))
        return carry

    loads = [
        pltpu.make_async_copy(kq_ref.at[0], k, sems.at[0]),
        pltpu.make_async_copy(vd_ref.at[0], v, sems.at[1]),
    ]
    near_loads = [
        pltpu.make_async_copy(gk_ref, near.at[0], sems.at[2]),
        pltpu.make_async_copy(gv_ref, near.at[1], sems.at[3]),
    ]
    start_all(loads)
    pairs = (CTX - ctx) // 2
    lax.fori_loop(0, 2 * pairs, lambda j, c: start_slot((ctx + 1 + j) % CTX, c), 0)
    start_all(near_loads)
    acc[...] = jnp.zeros_like(acc)
    wait_all(loads)

    def step(pair, carry):
        picked = []
        for half in range(2):
            want = ctx + 1 + 2 * pair + half
            d = want % CTX
            wait_all(slot_copies(d))
            picked.append((d, (tab[2, d] == 1) & (want < CTX)))
        terms = []
        for d, filled in picked:
            rows, cols = block_slice(tab[0, d]), head_slice(tab[1, d])
            k_term, v_term = key_terms(
                k[rows, cols], v[rows, cols], far_q[d], far_do[d], stats[d]
            )
            terms.append(
                (rows, cols, jnp.where(filled, k_term, 0.0), jnp.where(filled, v_term, 0.0))
            )
        for rows, cols, k_term, v_term in terms:
            acc[0, rows, cols] += k_term
            acc[1, rows, cols] += v_term
        return carry

    lax.fori_loop(0, pairs, step, 0)
    outs = ((ko, k1, k2, k3), (vo, v1, v2, v3))
    stores = []
    for which in range(2):
        near_loads[which].wait()
        result[which] = (near[which] + acc[which]).astype(BF16)
        copies = piece_copies(result.at[which], outs[which], out_sems.at[which])
        start_all(copies)
        stores += copies
    wait_all(stores)


def far_side(tab, kq, vd, slots1, slots2, stats, gk, gv):
    return call(
        far_kernel,
        [shape((TOK, COLS))] * 8,
        [SMEM] + [HBM] * 4 + [VMEM] + [HBM] * 2,
        [HBM] * 8,
        [
            pltpu.VMEM((ROWS, COLS), BF16),
            pltpu.VMEM((ROWS, COLS), BF16),
            pltpu.VMEM((CTX, BLOCK, HEAD_DIM), BF16),
            pltpu.VMEM((CTX, BLOCK, HEAD_DIM), BF16),
            pltpu.VMEM((2, ROWS, COLS), F32),
            pltpu.VMEM((2, ROWS, COLS), F32),
            pltpu.VMEM((2, ROWS, COLS), BF16),
            pltpu.SemaphoreType.DMA((4,)),
            pltpu.SemaphoreType.DMA((2, CTX)),
            pltpu.SemaphoreType.DMA((2, TP)),
        ],
    )(tab, kq, vd, slots1, slots2, stats, gk, gv)


def shards(queries, keys, values, dout, match):
    kq_in = exchange(cut(keys, queries))
    vd_in = exchange(cut(values, dout))
    tab = make_table(match)
    slots1, kq = pack(tab, keys, queries, kq_in)
    far1 = swap(slots1)
    slots2, vd = pack(tab, values, dout, vd_in)
    slots2, far1 = lax.optimization_barrier((slots2, far1))
    far2 = swap(slots2)
    prob, lse, gv = prob_side(tab, kq, vd, far1)
    *att, att_full, stats_slots = value_side(tab, prob, lse, vd, far2)
    att_in = exchange(att[1:4])
    far_stats = swap(stats_slots)
    *gq, gk = query_side(tab, prob, kq, vd, att_full, far1, far2)
    gq_in = exchange(gq[1:4])
    out = far_side(tab, kq, vd, far1, far2, far_stats, gk, gv)
    gk_in = exchange(out[1:4])
    gv_in = exchange(out[5:])
    return (join(att[0], att_in), join(gq[0], gq_in), join(out[0], gk_in), join(out[4], gv_in))


def solution(mesh):
    placed = P(("ctx", "tp"), None)
    return jax.shard_map(
        shards,
        mesh=mesh,
        in_specs=(placed, placed, placed, placed, P()),
        out_specs=(placed, placed, placed, placed),
        check_vma=False,
    )
```

time: 237 us -> 210 us (0.89)
  local copies, waits for them, and re-layouts: 27.7 us -> 1.33 us
    unnamed x56 -> x16, local copies, waits for them, and re-layouts: 27.7 us -> 1.33 us
    ppermute x18, waiting for transfers between devices: 70.3 us -> 73 us  [exchange(): lax.ppermute(piece, 'tp', [(i, (i + step) % TP) for i in range(TP)])]
    pallas_call x14 -> x13, Pallas kernels: 70.3 us -> 69.5 us  [the longest x3 35.9 us: run(): pl.pallas_call(kernel, out_shape=outs, grid_spec=pltpu.PrefetchScalarGrid...]
  transfers between devices with their start and end apart: 21 -> 21, of which waited for: 11 -> 11; matrix products, arithmetic and copies ran while one was open for 0% -> 0% of each run, Pallas kernels for 25% -> 26%
where the time goes in v2:
time: 210 us; the launch traced here: 208 us
  waiting for transfers between devices  85.3 us (41%)
  Pallas kernels  69.5 us (33%)
  starting transfers between devices  51.2 us (24%)
    ppermute x18, waiting for transfers between devices, exchange(): lax.ppermute(piece, 'tp', [(i, (i + step) % TP) for i in range(TP)])  73 us
    pallas_call x3, Pallas kernels, run(): pl.pallas_call(kernel, out_shape=outs, grid_spec=pltpu.PrefetchScalarGrid...  35.9 us
    pallas_call x10, Pallas kernels, run(): pl.pallas_call(kernel, out_shape=outs if many else outs[0], in_specs=in_s...  33.6 us
    ppermute x18, starting transfers between devices, exchange(): lax.ppermute(piece, 'tp', [(i, (i + step) % TP) for i in range(TP)])  29.8 us
    all_to_all x3, starting transfers between devices, swap(): return lax.all_to_all(slots, 'ctx', split_axis=0, concat_axis=0, tiled=True)  21.4 us
    all_to_all x3, waiting for transfers between devices, swap(): return lax.all_to_all(slots, 'ctx', split_axis=0, concat_axis=0, tiled=True)  12.3 us
  transfers between devices with their start and end apart: 21, of which 11 were waited for; matrix products, arithmetic and copies ran while one was open for 0% of the time, Pallas kernels for 26%

profile of v2, /device:TPU:32, one launch (start us, length us, event | category | flops | bytes accessed | tf_op | source)
XLA Modules:
  0.0 208.3 jit_solution(13533445269021806052)
XLA Ops:
  3.8 2.9 %collective-permute-start.1 = (bf16[2,128,1280]{2,1,0:T(8,128)(2,1)S(1)}, bf16[2,128,1280]{2,1,0:T(8,128)(2,1)S(1)}, u32[]{:S(2)}, u32[]{:S(2)}) collective-permute-start(bf16[2,128,1280]{2,1,0:T(8,128)(2,1)S(1)} %get-tuple-element.39), channel_id=1, source_target_pairs={{0,2},{1,3},{2,0},{3,1},{4,6},{5,7},{6,4},{7,5},{8,10},{9,11},{10,... | collective-permute-start | bytes 1966088 | tf_op jit(solution)/shard_map/ppermute | solution.py:129
  8.1 3.7 %shard_map.84.tab = s32[8,32]{1,0:T(8,128)S(1)} custom-call(s32[10,64]{1,0:T(8,128)S(1)} %copy-done.5), custom_call_target="tpu_custom_call" | custom-call | tf_op jit(solution)/shard_map/pallas_call | solution.py:69
  11.8 8.2 %collective-permute-done.r1 = bf16[2,128,1280]{2,1,0:T(8,128)(2,1)S(1)} collective-permute-done((bf16[2,128,1280]{2,1,0:T(8,128)(2,1)S(1)}, bf16[2,128,1280]{2,1,0:T(8,128)(2,1)S(1)}, u32[]{:S(2)}, u32[]{:S(2)}) %collective-permute-start) | collective-permute-done | bytes 655392 | tf_op jit(solution)/shard_map/ppermute | solution.py:129
  20.0 15.2 %collective-permute-done.1.r2 = bf16[2,128,1280]{2,1,0:T(8,128)(2,1)S(1)} collective-permute-done((bf16[2,128,1280]{2,1,0:T(8,128)(2,1)S(1)}, bf16[2,128,1280]{2,1,0:T(8,128)(2,1)S(1)}, u32[]{:S(2)}, u32[]{:S(2)}) %collective-permute-start.1) | collective-permute-done | bytes 655392 | tf_op jit(solution)/shard_map/ppermute | solution.py:129
  35.2 4.2 %shard_map.86 = (bf16[32,256,128]{2,1,0:T(8,128)(2,1)}, bf16[2,512,1280]{2,1,0:T(8,128)(2,1)}) custom-call(s32[8,32]{1,0:T(8,128)S(1)} %shard_map.84.tab, bf16[128,5120]{1,0:T(8,128)(2,1)} %a_ref.5, bf16[128,5120]{1,0:T(8,128)(2,1)} %b_ref.5, bf16[2,128,1280]{2,1,0:T(8,128)(2,1)S(1)} %collective-permute-done.r1, ...), custom_call_target="tpu_custom_call" | custom-call | tf_op jit(solution)/shard_map/pallas_call | solution.py:69
  39.4 8.0 %all-to-all-start = ((bf16[32,256,128]{2,1,0:T(8,128)(2,1)}), bf16[32,256,128]{2,1,0:T(8,128)(2,1)S(1)}, u32[]{:S(2)}, u32[]{:S(2)}) async-start(bf16[32,256,128]{2,1,0:T(8,128)(2,1)} %get-tuple-element.47), calls=%async_computation | async-start | bytes 4194304 | tf_op jit(solution)/shard_map/all_to_all | solution.py:237
  50.3 2.4 %collective-permute-start.4 = (bf16[2,128,1280]{2,1,0:T(8,128)(2,1)S(1)}, bf16[2,128,1280]{2,1,0:T(8,128)(2,1)S(1)}, u32[]{:S(2)}, u32[]{:S(2)}) collective-permute-start(bf16[2,128,1280]{2,1,0:T(8,128)(2,1)S(1)} %get-tuple-element.43), channel_id=1, source_target_pairs={{0,2},{1,3},{2,0},{3,1},{4,6},{5,7},{6,4},{7,5},{8,10},{9,11},{10,... | collective-permute-start | bytes 1966088 | tf_op jit(solution)/shard_map/ppermute | solution.py:129
  54.3 13.2 %collective-permute-done.3.r1 = bf16[2,128,1280]{2,1,0:T(8,128)(2,1)S(1)} collective-permute-done((bf16[2,128,1280]{2,1,0:T(8,128)(2,1)S(1)}, bf16[2,128,1280]{2,1,0:T(8,128)(2,1)S(1)}, u32[]{:S(2)}, u32[]{:S(2)}) %collective-permute-start.3) | collective-permute-done | bytes 655392 | tf_op jit(solution)/shard_map/ppermute | solution.py:129
  67.5 14.0 %collective-permute-done.4.r2 = bf16[2,128,1280]{2,1,0:T(8,128)(2,1)S(1)} collective-permute-done((bf16[2,128,1280]{2,1,0:T(8,128)(2,1)S(1)}, bf16[2,128,1280]{2,1,0:T(8,128)(2,1)S(1)}, u32[]{:S(2)}, u32[]{:S(2)}) %collective-permute-start.4) | collective-permute-done | bytes 655392 | tf_op jit(solution)/shard_map/ppermute | solution.py:129
  81.7 4.3 %shard_map.88 = (bf16[32,256,128]{2,1,0:T(8,128)(2,1)}, bf16[2,512,1280]{2,1,0:T(8,128)(2,1)}) custom-call(s32[8,32]{1,0:T(8,128)S(1)} %shard_map.84.tab, bf16[128,5120]{1,0:T(8,128)(2,1)} %a_ref.7, bf16[128,5120]{1,0:T(8,128)(2,1)} %b_ref.7, bf16[2,128,1280]{2,1,0:T(8,128)(2,1)S(1)} %collective-permute-done.3.r1, ...), custom_call_target="tpu_custom_call" | custom-call | tf_op jit(solution)/shard_map/pallas_call | solution.py:69
  87.3 7.4 %all-to-all-start.1 = ((bf16[32,256,128]{2,1,0:T(8,128)(2,1)}), bf16[32,256,128]{2,1,0:T(8,128)(2,1)S(1)}, u32[]{:S(2)}, u32[]{:S(2)}) async-start(bf16[32,256,128]{2,1,0:T(8,128)(2,1)} %get-tuple-element.51), calls=%async_computation.1 | async-start | bytes 4194304 | tf_op jit(solution)/shard_map/all_to_all | solution.py:237
  94.7 14.5 %shard_map.89 = (bf16[2,10,256,512]{3,2,1,0:T(8,128)(2,1)}, f32[2,10,8,256]{3,2,1,0:T(8,128)}, f32[512,1280]{1,0:T(8,128)}) custom-call(s32[8,32]{1,0:T(8,128)S(1)} %shard_map.84.tab, bf16[2,512,1280]{2,1,0:T(8,128)(2,1)} %get-tuple-element.41.kq.kq_ref, bf16[2,512,1280]{2,1,0:T(8,128)(2,1)} %get-tuple-element.45.dout.vd.vd_ref, ...), custom_call_target="tpu_custom_call" | custom-call | tf_op jit(solution)/shard_map/pallas_call | solution.py:285
  109.2 12.3 %all-to-all-done.1.refs_0_.refs_1_.refs_2_.refs_3_.refs_4_.refs_5_.refs_6_.refs_7_.slots2 = bf16[32,256,128]{2,1,0:T(8,128)(2,1)S(1)} async-done(((bf16[32,256,128]{2,1,0:T(8,128)(2,1)}), bf16[32,256,128]{2,1,0:T(8,128)(2,1)S(1)}, u32[]{:S(2)}, u32[]{:S(2)}) %all-to-all-start.1) | async-done | bytes 2097184 | tf_op jit(solution)/shard_map/all_to_all | solution.py:237
  121.5 9.2 %shard_map.90 = (bf16[128,1280]{1,0:T(8,128)(2,1)}, bf16[128,1280]{1,0:T(8,128)(2,1)}, bf16[128,1280]{1,0:T(8,128)(2,1)}, bf16[128,1280]{1,0:T(8,128)(2,1)}, bf1...) custom-call(s32[8,32]{1,0:T(8,128)S(1)} %shard_map.84.tab, bf16[2,10,256,512]{3,2,1,0:T(8,128)(2,1)} %get-tuple-element.49.prob, ...), custom_call_target="tpu_custom_call" | custom-call | tf_op jit(solution)/shard_map/pallas_call | solution.py:285
  132.5 2.4 %collective-permute-start.7 = (bf16[128,1280]{1,0:T(8,128)(2,1)}, bf16[128,1280]{1,0:T(8,128)(2,1)S(1)}, u32[]{:S(2)}, u32[]{:S(2)}) collective-permute-start(bf16[128,1280]{1,0:T(8,128)(2,1)} %get-tuple-element.54), channel_id=1, source_target_pairs={{0,2},{1,3},{2,0},{3,1},{4,6},{5,7},{6,4},{7,5},{8,10},{9,11},{10,... | collective-permute-start | bytes 983048 | tf_op jit(solution)/shard_map/ppermute | solution.py:129
  134.9 5.9 %all-to-all-start.2 = ((f32[32,8,256]{2,1,0:T(8,128)}), f32[32,8,256]{2,1,0:T(8,128)S(1)}, u32[]{:S(2)}, u32[]{:S(2)}) async-start(f32[32,8,256]{2,1,0:T(8,128)} %get-tuple-element.61), calls=%async_computation.2 | async-start | bytes 524288 | tf_op jit(solution)/shard_map/all_to_all | solution.py:237
  142.0 12.2 %shard_map.92 = (bf16[128,1280]{1,0:T(8,128)(2,1)}, bf16[128,1280]{1,0:T(8,128)(2,1)}, bf16[128,1280]{1,0:T(8,128)(2,1)}, bf16[128,1280]{1,0:T(8,128)(2,1)}, f32[512,1280]{1,0:T(8,128)}) custom-call(s32[8,32]{1,0:T(8,128)S(1)} %shard_map.84.tab, bf16[2,10,256,512]{3,2,1,0:T(8,128)(2,1)} %get-tuple-element.49.prob, ...), custom_call_target="tpu_custom_call" | custom-call | tf_op jit(solution)/shard_map/pallas_call | solution.py:285
  156.3 14.0 %shard_map.94 = (bf16[128,1280]{1,0:T(8,128)(2,1)}, bf16[128,1280]{1,0:T(8,128)(2,1)}, bf16[128,1280]{1,0:T(8,128)(2,1)}, bf16[128,1280]{1,0:T(8,128)(2,1)}, bf1...) custom-call(s32[8,32]{1,0:T(8,128)S(1)} %shard_map.84.tab, ...), custom_call_target="tpu_custom_call" | custom-call | tf_op jit(solution)/shard_map/pallas_call | solution.py:69
  172.5 2.3 %collective-permute-start.13 = (bf16[128,1280]{1,0:T(8,128)(2,1)}, bf16[128,1280]{1,0:T(8,128)(2,1)S(1)}, u32[]{:S(2)}, u32[]{:S(2)}) collective-permute-start(bf16[128,1280]{1,0:T(8,128)(2,1)} %get-tuple-element.66), channel_id=1, source_target_pairs={{0,2},{1,3},{2,0},{3,1},{4,6},{5,7},{6,4},{7,5},{8,10},{9,11},{10,... | collective-permute-start | bytes 983048 | tf_op jit(solution)/shard_map/ppermute | solution.py:129
  174.8 2.3 %collective-permute-start.14 = (bf16[128,1280]{1,0:T(8,128)(2,1)}, bf16[128,1280]{1,0:T(8,128)(2,1)S(1)}, u32[]{:S(2)}, u32[]{:S(2)}) collective-permute-start(bf16[128,1280]{1,0:T(8,128)(2,1)} %get-tuple-element.67), channel_id=1, source_target_pairs={{0,3},{1,0},{2,1},{3,2},{4,7},{5,4},{6,5},{7,6},{8,11},{9,8},{10,9... | collective-permute-start | bytes 983048 | tf_op jit(solution)/shard_map/ppermute | solution.py:129
  177.2 9.6 %collective-permute-done.11.r3 = bf16[128,1280]{1,0:T(8,128)(2,1)S(1)} collective-permute-done((bf16[128,1280]{1,0:T(8,128)(2,1)S(1)}, bf16[128,1280]{1,0:T(8,128)(2,1)S(1)}, u32[]{:S(2)}, u32[]{:S(2)}) %collective-permute-start.11) | collective-permute-done | bytes 327712 | tf_op jit(solution)/shard_map/ppermute | solution.py:129
  186.7 2.6 %collective-permute-start.16 = (bf16[128,1280]{1,0:T(8,128)(2,1)}, bf16[128,1280]{1,0:T(8,128)(2,1)S(1)}, u32[]{:S(2)}, u32[]{:S(2)}) collective-permute-start(bf16[128,1280]{1,0:T(8,128)(2,1)} %get-tuple-element.70), channel_id=1, source_target_pairs={{0,2},{1,3},{2,0},{3,1},{4,6},{5,7},{6,4},{7,5},{8,10},{9,11},{10,... | collective-permute-start | bytes 983048 | tf_op jit(solution)/shard_map/ppermute | solution.py:129
  195.0 5.9 %collective-permute-done.14.r3 = bf16[128,1280]{1,0:T(8,128)(2,1)S(1)} collective-permute-done((bf16[128,1280]{1,0:T(8,128)(2,1)}, bf16[128,1280]{1,0:T(8,128)(2,1)S(1)}, u32[]{:S(2)}, u32[]{:S(2)}) %collective-permute-start.14) | collective-permute-done | bytes 327712 | tf_op jit(solution)/shard_map/ppermute | solution.py:129
  202.6 4.4 %collective-permute-done.17.r3 = bf16[128,1280]{1,0:T(8,128)(2,1)S(1)} collective-permute-done((bf16[128,1280]{1,0:T(8,128)(2,1)}, bf16[128,1280]{1,0:T(8,128)(2,1)S(1)}, u32[]{:S(2)}, u32[]{:S(2)}) %collective-permute-start.17) | collective-permute-done | bytes 327712 | tf_op jit(solution)/shard_map/ppermute | solution.py:129
  (47 shorter events, 26.3 us)
Async XLA Ops:
  2.2 17.8 %collective-permute-start = (bf16[2,128,1280]{2,1,0:T(8,128)(2,1)S(1)}, bf16[2,128,1280]{2,1,0:T(8,128)(2,1)S(1)}, u32[]{:S(2)}, u32[]{:S(2)}) collective-permute-start(bf16[2,128,1280]{2,1,0:T(8,128)(2,1)S(1)} %get-tuple-element.38), channel_id=1, source_target_pairs={{0,1},{1,2},{2,3},{3,0},{4,5},{5,6},{6,7},{7,4},{8,9},{9,10},{10,1... | collective-permute-start | bytes 1966088 | tf_op jit(solution)/shard_map/ppermute | solution.py:129
  3.8 31.4 %collective-permute-start.1 = (bf16[2,128,1280]{2,1,0:T(8,128)(2,1)S(1)}, bf16[2,128,1280]{2,1,0:T(8,128)(2,1)S(1)}, u32[]{:S(2)}, u32[]{:S(2)}) collective-permute-start(bf16[2,128,1280]{2,1,0:T(8,128)(2,1)S(1)} %get-tuple-element.39), channel_id=1, source_target_pairs={{0,2},{1,3},{2,0},{3,1},{4,6},{5,7},{6,4},{7,5},{8,10},{9,11},{10,... | collective-permute-start | bytes 1966088 | tf_op jit(solution)/shard_map/ppermute | solution.py:129
  6.7 28.5 %collective-permute-start.2 = (bf16[2,128,1280]{2,1,0:T(8,128)(2,1)S(1)}, bf16[2,128,1280]{2,1,0:T(8,128)(2,1)S(1)}, u32[]{:S(2)}, u32[]{:S(2)}) collective-permute-start(bf16[2,128,1280]{2,1,0:T(8,128)(2,1)S(1)} %get-tuple-element.40), channel_id=1, source_target_pairs={{0,3},{1,0},{2,1},{3,2},{4,7},{5,4},{6,5},{7,6},{8,11},{9,8},{10,9... | collective-permute-start | bytes 1966088 | tf_op jit(solution)/shard_map/ppermute | solution.py:129
  39.4 46.6 %all-to-all-start = ((bf16[32,256,128]{2,1,0:T(8,128)(2,1)}), bf16[32,256,128]{2,1,0:T(8,128)(2,1)S(1)}, u32[]{:S(2)}, u32[]{:S(2)}) async-start(bf16[32,256,128]{2,1,0:T(8,128)(2,1)} %get-tuple-element.47), calls=%async_computation | async-start | bytes 4194304 | tf_op jit(solution)/shard_map/all_to_all | solution.py:237
  49.0 18.5 %collective-permute-start.3 = (bf16[2,128,1280]{2,1,0:T(8,128)(2,1)S(1)}, bf16[2,128,1280]{2,1,0:T(8,128)(2,1)S(1)}, u32[]{:S(2)}, u32[]{:S(2)}) collective-permute-start(bf16[2,128,1280]{2,1,0:T(8,128)(2,1)S(1)} %get-tuple-element.42), channel_id=1, source_target_pairs={{0,1},{1,2},{2,3},{3,0},{4,5},{5,6},{6,7},{7,4},{8,9},{9,10},{10,1... | collective-permute-start | bytes 1966088 | tf_op jit(solution)/shard_map/ppermute | solution.py:129
  50.3 31.2 %collective-permute-start.4 = (bf16[2,128,1280]{2,1,0:T(8,128)(2,1)S(1)}, bf16[2,128,1280]{2,1,0:T(8,128)(2,1)S(1)}, u32[]{:S(2)}, u32[]{:S(2)}) collective-permute-start(bf16[2,128,1280]{2,1,0:T(8,128)(2,1)S(1)} %get-tuple-element.43), channel_id=1, source_target_pairs={{0,2},{1,3},{2,0},{3,1},{4,6},{5,7},{6,4},{7,5},{8,10},{9,11},{10,... | collective-permute-start | bytes 1966088 | tf_op jit(solution)/shard_map/ppermute | solution.py:129
  52.7 29.0 %collective-permute-start.5 = (bf16[2,128,1280]{2,1,0:T(8,128)(2,1)S(1)}, bf16[2,128,1280]{2,1,0:T(8,128)(2,1)S(1)}, u32[]{:S(2)}, u32[]{:S(2)}) collective-permute-start(bf16[2,128,1280]{2,1,0:T(8,128)(2,1)S(1)} %get-tuple-element.44), channel_id=1, source_target_pairs={{0,3},{1,0},{2,1},{3,2},{4,7},{5,4},{6,5},{7,6},{8,11},{9,8},{10,9... | collective-permute-start | bytes 1966088 | tf_op jit(solution)/shard_map/ppermute | solution.py:129
  87.3 34.1 %all-to-all-start.1 = ((bf16[32,256,128]{2,1,0:T(8,128)(2,1)}), bf16[32,256,128]{2,1,0:T(8,128)(2,1)S(1)}, u32[]{:S(2)}, u32[]{:S(2)}) async-start(bf16[32,256,128]{2,1,0:T(8,128)(2,1)} %get-tuple-element.51), calls=%async_computation.1 | async-start | bytes 4194304 | tf_op jit(solution)/shard_map/all_to_all | solution.py:237
  130.7 39.6 %collective-permute-start.6 = (bf16[128,1280]{1,0:T(8,128)(2,1)}, bf16[128,1280]{1,0:T(8,128)(2,1)S(1)}, u32[]{:S(2)}, u32[]{:S(2)}) collective-permute-start(bf16[128,1280]{1,0:T(8,128)(2,1)} %get-tuple-element.53), channel_id=1, source_target_pairs={{0,1},{1,2},{2,3},{3,0},{4,5},{5,6},{6,7},{7,4},{8,9},{9,10},{10,1... | collective-permute-start | bytes 983048 | tf_op jit(solution)/shard_map/ppermute | solution.py:129
  132.5 39.5 %collective-permute-start.7 = (bf16[128,1280]{1,0:T(8,128)(2,1)}, bf16[128,1280]{1,0:T(8,128)(2,1)S(1)}, u32[]{:S(2)}, u32[]{:S(2)}) collective-permute-start(bf16[128,1280]{1,0:T(8,128)(2,1)} %get-tuple-element.54), channel_id=1, source_target_pairs={{0,2},{1,3},{2,0},{3,1},{4,6},{5,7},{6,4},{7,5},{8,10},{9,11},{10,... | collective-permute-start | bytes 983048 | tf_op jit(solution)/shard_map/ppermute | solution.py:129
  134.9 21.4 %all-to-all-start.2 = ((f32[32,8,256]{2,1,0:T(8,128)}), f32[32,8,256]{2,1,0:T(8,128)S(1)}, u32[]{:S(2)}, u32[]{:S(2)}) async-start(f32[32,8,256]{2,1,0:T(8,128)} %get-tuple-element.61), calls=%async_computation.2 | async-start | bytes 524288 | tf_op jit(solution)/shard_map/all_to_all | solution.py:237
  140.8 31.7 %collective-permute-start.8 = (bf16[128,1280]{1,0:T(8,128)(2,1)}, bf16[128,1280]{1,0:T(8,128)(2,1)S(1)}, u32[]{:S(2)}, u32[]{:S(2)}) collective-permute-start(bf16[128,1280]{1,0:T(8,128)(2,1)} %get-tuple-element.55), channel_id=1, source_target_pairs={{0,3},{1,0},{2,1},{3,2},{4,7},{5,4},{6,5},{7,6},{8,11},{9,8},{10,9... | collective-permute-start | bytes 983048 | tf_op jit(solution)/shard_map/ppermute | solution.py:129
  154.2 20.6 %collective-permute-start.9 = (bf16[128,1280]{1,0:T(8,128)(2,1)}, bf16[128,1280]{1,0:T(8,128)(2,1)S(1)}, u32[]{:S(2)}, u32[]{:S(2)}) collective-permute-start(bf16[128,1280]{1,0:T(8,128)(2,1)} %get-tuple-element.58), channel_id=1, source_target_pairs={{0,1},{1,2},{2,3},{3,0},{4,5},{5,6},{6,7},{7,4},{8,9},{9,10},{10,1... | collective-permute-start | bytes 983048 | tf_op jit(solution)/shard_map/ppermute | solution.py:129
  155.2 22.0 %collective-permute-start.10 = (bf16[128,1280]{1,0:T(8,128)(2,1)}, bf16[128,1280]{1,0:T(8,128)(2,1)S(1)}, u32[]{:S(2)}, u32[]{:S(2)}) collective-permute-start(bf16[128,1280]{1,0:T(8,128)(2,1)} %get-tuple-element.59), channel_id=1, source_target_pairs={{0,2},{1,3},{2,0},{3,1},{4,6},{5,7},{6,4},{7,5},{8,10},{9,11},{10,... | collective-permute-start | bytes 983048 | tf_op jit(solution)/shard_map/ppermute | solution.py:129
  156.3 14.0 %copy-start.7 = (bf16[128,1280]{1,0:T(8,128)(2,1)S(1)}, bf16[128,1280]{1,0:T(8,128)(2,1)}, u32[]{:S(2)}) copy-start(bf16[128,1280]{1,0:T(8,128)(2,1)} %get-tuple-element.60) | copy-start | bytes 983044
  156.3 36.4 %copy-start.1 = (bf16[128,1280]{1,0:T(8,128)(2,1)S(1)}, bf16[128,1280]{1,0:T(8,128)(2,1)}, u32[]{:S(2)}) copy-start(bf16[128,1280]{1,0:T(8,128)(2,1)} %get-tuple-element.52.own) | copy-start | bytes 983044
  170.3 23.5 %copy-start.3 = (bf16[128,1280]{1,0:T(8,128)(2,1)S(1)}, bf16[128,1280]{1,0:T(8,128)(2,1)}, u32[]{:S(2)}) copy-start(bf16[128,1280]{1,0:T(8,128)(2,1)} %get-tuple-element.57.own) | copy-start | bytes 983044
  170.3 16.4 %collective-permute-start.11 = (bf16[128,1280]{1,0:T(8,128)(2,1)S(1)}, bf16[128,1280]{1,0:T(8,128)(2,1)S(1)}, u32[]{:S(2)}, u32[]{:S(2)}) collective-permute-start(bf16[128,1280]{1,0:T(8,128)(2,1)S(1)} %copy-done.7), channel_id=1, source_target_pairs={{0,3},{1,0},{2,1},{3,2},{4,7},{5,4},{6,5},{7,6},{8,11},{9,8},{10,9... | collective-permute-start | bytes 983048 | tf_op jit(solution)/shard_map/ppermute | solution.py:129
  172.0 19.0 %collective-permute-start.12 = (bf16[128,1280]{1,0:T(8,128)(2,1)}, bf16[128,1280]{1,0:T(8,128)(2,1)S(1)}, u32[]{:S(2)}, u32[]{:S(2)}) collective-permute-start(bf16[128,1280]{1,0:T(8,128)(2,1)} %get-tuple-element.65), channel_id=1, source_target_pairs={{0,1},{1,2},{2,3},{3,0},{4,5},{5,6},{6,7},{7,4},{8,9},{9,10},{10,1... | collective-permute-start | bytes 983048 | tf_op jit(solution)/shard_map/ppermute | solution.py:129
  172.5 22.4 %collective-permute-start.13 = (bf16[128,1280]{1,0:T(8,128)(2,1)}, bf16[128,1280]{1,0:T(8,128)(2,1)S(1)}, u32[]{:S(2)}, u32[]{:S(2)}) collective-permute-start(bf16[128,1280]{1,0:T(8,128)(2,1)} %get-tuple-element.66), channel_id=1, source_target_pairs={{0,2},{1,3},{2,0},{3,1},{4,6},{5,7},{6,4},{7,5},{8,10},{9,11},{10,... | collective-permute-start | bytes 983048 | tf_op jit(solution)/shard_map/ppermute | solution.py:129
  174.8 26.0 %collective-permute-start.14 = (bf16[128,1280]{1,0:T(8,128)(2,1)}, bf16[128,1280]{1,0:T(8,128)(2,1)S(1)}, u32[]{:S(2)}, u32[]{:S(2)}) collective-permute-start(bf16[128,1280]{1,0:T(8,128)(2,1)} %get-tuple-element.67), channel_id=1, source_target_pairs={{0,3},{1,0},{2,1},{3,2},{4,7},{5,4},{6,5},{7,6},{8,11},{9,8},{10,9... | collective-permute-start | bytes 983048 | tf_op jit(solution)/shard_map/ppermute | solution.py:129
  177.2 25.5 %collective-permute-start.15 = (bf16[128,1280]{1,0:T(8,128)(2,1)}, bf16[128,1280]{1,0:T(8,128)(2,1)S(1)}, u32[]{:S(2)}, u32[]{:S(2)}) collective-permute-start(bf16[128,1280]{1,0:T(8,128)(2,1)} %get-tuple-element.69), channel_id=1, source_target_pairs={{0,1},{1,2},{2,3},{3,0},{4,5},{5,6},{6,7},{7,4},{8,9},{9,10},{10,1... | collective-permute-start | bytes 983048 | tf_op jit(solution)/shard_map/ppermute | solution.py:129
  186.7 15.9 %collective-permute-start.16 = (bf16[128,1280]{1,0:T(8,128)(2,1)}, bf16[128,1280]{1,0:T(8,128)(2,1)S(1)}, u32[]{:S(2)}, u32[]{:S(2)}) collective-permute-start(bf16[128,1280]{1,0:T(8,128)(2,1)} %get-tuple-element.70), channel_id=1, source_target_pairs={{0,2},{1,3},{2,0},{3,1},{4,6},{5,7},{6,4},{7,5},{8,10},{9,11},{10,... | collective-permute-start | bytes 983048 | tf_op jit(solution)/shard_map/ppermute | solution.py:129
  191.0 16.0 %collective-permute-start.17 = (bf16[128,1280]{1,0:T(8,128)(2,1)}, bf16[128,1280]{1,0:T(8,128)(2,1)S(1)}, u32[]{:S(2)}, u32[]{:S(2)}) collective-permute-start(bf16[128,1280]{1,0:T(8,128)(2,1)} %get-tuple-element.71), channel_id=1, source_target_pairs={{0,3},{1,0},{2,1},{3,2},{4,7},{5,4},{6,5},{7,6},{8,11},{9,8},{10,9... | collective-permute-start | bytes 983048 | tf_op jit(solution)/shard_map/ppermute | solution.py:129
  (5 other events, 39.3 us)

commit v3 on v2

--- a/solution.py
+++ b/solution.py
@@ -12,6 +12,7 @@
 CTX = 32
 TP = 4
 TOK = 128
+HALF = TOK // 2
 ROWS = TP * TOK
 COLS = GROUPS * HEAD_DIM
 SCALE = HEAD_DIM ** (-0.5)
@@ -85,25 +86,22 @@
         copy.wait()
 
 
-def cut_kernel(a_ref, b_ref, p1, p2, p3, sems):
-    copies = []
-    for step, out in ((1, p1), (2, p2), (3, p3)):
-        for which, ref in enumerate((a_ref, b_ref)):
-            copies.append(
-                pltpu.make_async_copy(
-                    ref.at[:, col_slice(peer(step))], out.at[which], sems.at[len(copies)]
+def cut(a, b, base, size):
+    def kernel(a_ref, b_ref, p1, p2, p3, sems):
+        copies = []
+        for step, out in ((1, p1), (2, p2), (3, p3)):
+            for which, ref in enumerate((a_ref, b_ref)):
+                copies.append(
+                    pltpu.make_async_copy(
+                        ref.at[pl.ds(base, size), col_slice(peer(step))],
+                        out.at[which],
+                        sems.at[len(copies)],
+                    )
                 )
-            )
-    run_copies(copies)
-
-
-def cut(a, b):
+        run_copies(copies)
+
     return call(
-        cut_kernel,
-        [shape((2, TOK, COLS))] * 3,
-        [HBM] * 2,
-        [VMEM] * 3,
-        [pltpu.SemaphoreType.DMA((6,))],
+        kernel, [shape((2, size, COLS))] * 3, [HBM] * 2, [VMEM] * 3, [pltpu.SemaphoreType.DMA((6,))]
     )(a, b)
 
 
@@ -131,23 +129,25 @@
     return tuple(received)
 
 
-def gather_copies(a_ref, b_ref, received, held, sems, base):
+def gather_copies(a_ref, b_ref, received, held, sems, base, size, at, stride):
+    def place(index):
+        start = pl.multiple_of(index * stride + at, size)
+        return pl.ds(start, size)
+
     copies = []
     for which, ref in enumerate((a_ref, b_ref)):
         copies.append(
             pltpu.make_async_copy(
-                ref.at[:, col_slice(peer(0))],
-                held.at[which, row_slice(peer(0))],
-                sems.at[base + len(copies)],
+                ref.at[pl.ds(base, size), col_slice(peer(0))],
+                held.at[which, place(peer(0))],
+                sems.at[len(copies)],
             )
         )
     for step, ref in zip((1, 2, 3), received):
         for which in range(2):
             copies.append(
                 pltpu.make_async_copy(
-                    ref.at[which],
-                    held.at[which, row_slice(peer(TP - step))],
-                    sems.at[base + len(copies)],
+                    ref.at[which], held.at[which, place(peer(TP - step))], sems.at[len(copies)]
                 )
             )
     return copies
@@ -202,35 +202,62 @@
     return call(table_kernel, shape((8, CTX), jnp.int32), [SMEM], SMEM, [])(match)
 
 
-def pack_kernel(tab, a_ref, b_ref, r1, r2, r3, out, held_out, held, sems, slot_sems):
-    ctx = lax.axis_index("ctx")
-    run_copies(gather_copies(a_ref, b_ref, (r1, r2, r3), held, sems, 0))
-    copies = []
-    for d in range(CTX):
-        which = jnp.where(ctx > d, 1, 0)
-        copies.append(
-            pltpu.make_async_copy(
-                held.at[which, block_slice(tab[0, d]), head_slice(tab[1, d])],
-                out.at[d],
-                slot_sems.at[d],
+def pack(tab, a, b, received, base, size):
+    def kernel(tab, a_ref, b_ref, r1, r2, r3, out, held_out, held, sems, slot_sems):
+        ctx = lax.axis_index("ctx")
+        run_copies(gather_copies(a_ref, b_ref, (r1, r2, r3), held, sems, base, size, 0, size))
+        copies = []
+        for d in range(CTX):
+            which = jnp.where(ctx > d, 1, 0)
+            rows = pl.ds(pl.multiple_of(tab[0, d] * 2 * size, 2 * size), 2 * size)
+            copies.append(
+                pltpu.make_async_copy(
+                    held.at[which, rows, head_slice(tab[1, d])], out.at[d], slot_sems.at[d]
+                )
             )
-        )
-    copies.append(pltpu.make_async_copy(held, held_out, slot_sems.at[CTX]))
-    run_copies(copies)
-
-
-def pack(tab, a, b, received):
+        copies.append(pltpu.make_async_copy(held, held_out, slot_sems.at[CTX]))
+        run_copies(copies)
+
     return call(
-        pack_kernel,
-        [shape((CTX, BLOCK, HEAD_DIM)), shape((2, ROWS, COLS))],
+        kernel,
+        [shape((CTX, 2 * size, HEAD_DIM)), shape((2, TP * size, COLS))],
         [SMEM] + [HBM] * 2 + [ANY] * 3,
         [HBM] * 2,
         [
-            pltpu.VMEM((2, ROWS, COLS), BF16),
+            pltpu.VMEM((2, TP * size, COLS), BF16),
             pltpu.SemaphoreType.DMA((8,)),
             pltpu.SemaphoreType.DMA((CTX + 1,)),
         ],
     )(tab, a, b, *received)
+
+
+def hold_kernel(a_ref, b_ref, out, held, sems, out_sem):
+    copies = []
+    for part, ref in enumerate((a_ref, b_ref)):
+        for index in range(TP):
+            copies.append(
+                pltpu.make_async_copy(
+                    ref.at[:, pl.ds(index * HALF, HALF)],
+                    held.at[:, pl.ds(index * TOK + part * HALF, HALF)],
+                    sems.at[len(copies)],
+                )
+            )
+    run_copies(copies)
+    run_copies([pltpu.make_async_copy(held, out, out_sem.at[0])])
+
+
+def hold(a, b):
+    return call(
+        hold_kernel,
+        shape((2, ROWS, COLS)),
+        [HBM] * 2,
+        HBM,
+        [
+            pltpu.VMEM((2, ROWS, COLS), BF16),
+            pltpu.SemaphoreType.DMA((2 * TP,)),
+            pltpu.SemaphoreType.DMA((1,)),
+        ],
+    )(a, b)
 
 
 def swap(slots):
@@ -265,8 +292,19 @@
     )
 
 
+def half_spec(n, u):
+    return pl.BlockSpec(
+        (1, 2, HALF, HEAD_DIM), lambda j, tab: (tab[4, n * GROUPS + j * STEP + u], 0, 0, 0)
+    )
+
+
+def woven(first, second):
+    return jnp.concatenate([first[0, 0], second[0, 0], first[0, 1], second[0, 1]], axis=0)
+
+
 LANES = [(u, n) for u in range(STEP) for n in range(2)]
 FAR = [far_spec(n, u) for u, n in LANES]
+HALVES = [half_spec(n, u) for u, n in LANES]
 LOW, HIGH = pl.ds(0, BLOCK), pl.ds(BLOCK, BLOCK)
 
 
@@ -300,18 +338,19 @@
 
 def matched(tab, g, n, received, low):
     if n == 0:
-        return received[0]
-    return jnp.where(tab[3, GROUPS + g] == 2, low, received[0])
+        return received
+    return jnp.where(tab[3, GROUPS + g] == 2, low, received)
 
 
 def prob_kernel(tab, kq, dout, *refs):
-    far, (prob, lse_out, gv) = refs[: len(FAR)], refs[len(FAR) :]
+    count = len(FAR)
+    first, second, (prob, lse_out, gv) = refs[:count], refs[count : 2 * count], refs[2 * count :]
     causal = lax.broadcasted_iota(jnp.int32, (BLOCK, BLOCK), 0) >= lax.broadcasted_iota(
         jnp.int32, (BLOCK, BLOCK), 1
     )
     for index, u, n, g, rows, cols in lanes(pl.program_id(0)):
         q = kq[1, rows, cols]
-        kf = matched(tab, g, n, far[index], kq[0, LOW, cols])
+        kf = matched(tab, g, n, woven(first[index], second[index]), kq[0, LOW, cols])
         s_own = jnp.where(causal, dot_t(q, kq[0, rows, cols]) * SCALE, -jnp.inf)
         s_far = jnp.where(tab[3, n * GROUPS + g] > 0, dot_t(q, kf) * SCALE, -jnp.inf)
         top = jnp.maximum(
@@ -335,7 +374,7 @@
                 gv[LOW, cols] += dot_n(prob[1, u, :, HIGH], dout[0, HIGH, cols])
 
 
-def prob_side(tab, kq, vd, slots):
+def prob_side(tab, kq, vd, slots_a, slots_b):
     return by_group(
         prob_kernel,
         [
@@ -343,10 +382,10 @@
             shape((2, GROUPS, 8, BLOCK), F32),
             shape((ROWS, COLS), F32),
         ],
-        [PAIR, SECOND] + FAR,
+        [PAIR, SECOND] + HALVES * 2,
         [PROBS, STATS, HEADS_ONE],
         [],
-    )(tab, kq, vd, *[slots] * len(FAR))
+    )(tab, kq, vd, *[slots_a] * len(FAR), *[slots_b] * len(FAR))
 
 
 def piece_copies(result, outs, sems):
@@ -375,7 +414,7 @@
     ctx = lax.axis_index("ctx")
     sublane = lax.broadcasted_iota(jnp.int32, (8, BLOCK), 0)
     for index, u, n, g, rows, cols in lanes(j):
-        vf = matched(tab, g, n, far[index], vd[0, LOW, cols])
+        vf = matched(tab, g, n, far[index][0], vd[0, LOW, cols])
         att = dot(prob[n, u, :, LOW], vd[0, rows, cols]) + dot(prob[n, u, :, HIGH], vf)
         att = att.astype(BF16)
         full[rows, cols] = att
@@ -409,12 +448,12 @@
 
 def query_kernel(tab, prob, kq, vd, att, *refs):
     count = len(FAR)
-    far_k, far_v = refs[:count], refs[count : 2 * count]
-    own, p1, p2, p3, gk, result, ds_last = refs[2 * count :]
+    first, second, far_v = refs[:count], refs[count : 2 * count], refs[2 * count : 3 * count]
+    own, p1, p2, p3, gk, result, ds_last = refs[3 * count :]
     for index, u, n, g, rows, cols in lanes(pl.program_id(0)):
         do = vd[1, rows, cols]
-        kf = matched(tab, g, n, far_k[index], kq[0, LOW, cols])
-        vf = matched(tab, g, n, far_v[index], vd[0, LOW, cols])
+        kf = matched(tab, g, n, woven(first[index], second[index]), kq[0, LOW, cols])
+        vf = matched(tab, g, n, far_v[index][0], vd[0, LOW, cols])
         delta = jnp.sum(do.astype(F32) * att[rows, cols].astype(F32), axis=1, keepdims=True)
         p_own = prob[n, u, :, LOW].astype(F32)
         p_far = prob[n, u, :, HIGH].astype(F32)
@@ -434,14 +473,17 @@
                 gk[LOW, cols] += dot_n(ds_last[u], kq[1, HIGH, cols])
 
 
-def query_side(tab, prob, kq, vd, att, slots1, slots2):
+def query_side(tab, prob, kq, vd, att, slots_a, slots_b, slots2):
     return by_group(
         query_kernel,
         [shape((TOK, COLS))] * 4 + [shape((ROWS, COLS), F32)],
-        [PROBS, PAIR, PAIR, HEADS_ONE] + FAR + FAR,
+        [PROBS, PAIR, PAIR, HEADS_ONE] + HALVES * 2 + FAR,
         [PIECE] * 4 + [HEADS_ONE],
         [pltpu.VMEM((ROWS, WIDE), BF16), pltpu.VMEM((STEP, BLOCK, BLOCK), BF16)],
-    )(tab, prob, kq, vd, att, *[slots1] * len(FAR), *[slots2] * len(FAR))
+    )(
+        tab, prob, kq, vd, att,
+        *[slots_a] * len(FAR), *[slots_b] * len(FAR), *[slots2] * len(FAR),
+    )
 
 
 def key_terms(k, v, q, do, stats):
@@ -450,8 +492,11 @@
     return dot(ds, q), dot(p.astype(BF16), do)
 
 
+JOBS = 4
+
+
 def far_kernel(
-    tab, kq_ref, vd_ref, slots1, slots2, stats, gk_ref, gv_ref,
+    tab, kq_ref, vd_ref, slots_a, slots_b, slots2, stats, gk_ref, gv_ref,
     ko, k1, k2, k3, vo, v1, v2, v3,
     k, v, far_q, far_do, near, acc, result, sems, slot_sems, out_sems,
 ):
@@ -459,8 +504,9 @@
 
     def slot_copies(d):
         return [
-            pltpu.make_async_copy(slots1.at[d], far_q.at[d], slot_sems.at[0, d]),
-            pltpu.make_async_copy(slots2.at[d], far_do.at[d], slot_sems.at[1, d]),
+            pltpu.make_async_copy(slots_a.at[d], far_q.at[d, :, 0], slot_sems.at[0, d]),
+            pltpu.make_async_copy(slots_b.at[d], far_q.at[d, :, 1], slot_sems.at[1, d]),
+            pltpu.make_async_copy(slots2.at[d], far_do.at[d], slot_sems.at[2, d]),
         ]
 
     def start_slot(d, carry):
@@ -476,16 +522,16 @@
         pltpu.make_async_copy(gv_ref, near.at[1], sems.at[3]),
     ]
     start_all(loads)
-    pairs = (CTX - ctx) // 2
-    lax.fori_loop(0, 2 * pairs, lambda j, c: start_slot((ctx + 1 + j) % CTX, c), 0)
+    rounds = (CTX - 1 - ctx + JOBS - 1) // JOBS
+    lax.fori_loop(0, JOBS * rounds, lambda j, c: start_slot((ctx + 1 + j) % CTX, c), 0)
     start_all(near_loads)
     acc[...] = jnp.zeros_like(acc)
     wait_all(loads)
 
-    def step(pair, carry):
+    def step(turn, carry):
         picked = []
-        for half in range(2):
-            want = ctx + 1 + 2 * pair + half
+        for job in range(JOBS):
+            want = ctx + 1 + JOBS * turn + job
             d = want % CTX
             wait_all(slot_copies(d))
             picked.append((d, (tab[2, d] == 1) & (want < CTX)))
@@ -493,7 +539,7 @@
         for d, filled in picked:
             rows, cols = block_slice(tab[0, d]), head_slice(tab[1, d])
             k_term, v_term = key_terms(
-                k[rows, cols], v[rows, cols], far_q[d], far_do[d], stats[d]
+                k[rows, cols], v[rows, cols], far_q[d].reshape(BLOCK, HEAD_DIM), far_do[d], stats[d]
             )
             terms.append(
                 (rows, cols, jnp.where(filled, k_term, 0.0), jnp.where(filled, v_term, 0.0))
@@ -503,7 +549,7 @@
             acc[1, rows, cols] += v_term
         return carry
 
-    lax.fori_loop(0, pairs, step, 0)
+    lax.fori_loop(0, rounds, step, 0)
     outs = ((ko, k1, k2, k3), (vo, v1, v2, v3))
     stores = []
     for which in range(2):
@@ -515,43 +561,50 @@
     wait_all(stores)
 
 
-def far_side(tab, kq, vd, slots1, slots2, stats, gk, gv):
+def far_side(tab, kq, vd, slots_a, slots_b, slots2, stats, gk, gv):
     return call(
         far_kernel,
         [shape((TOK, COLS))] * 8,
-        [SMEM] + [HBM] * 4 + [VMEM] + [HBM] * 2,
+        [SMEM] + [HBM] * 5 + [VMEM] + [HBM] * 2,
         [HBM] * 8,
         [
             pltpu.VMEM((ROWS, COLS), BF16),
             pltpu.VMEM((ROWS, COLS), BF16),
-            pltpu.VMEM((CTX, BLOCK, HEAD_DIM), BF16),
+            pltpu.VMEM((CTX, 2, 2, HALF, HEAD_DIM), BF16),
             pltpu.VMEM((CTX, BLOCK, HEAD_DIM), BF16),
             pltpu.VMEM((2, ROWS, COLS), F32),
             pltpu.VMEM((2, ROWS, COLS), F32),
             pltpu.VMEM((2, ROWS, COLS), BF16),
             pltpu.SemaphoreType.DMA((4,)),
-            pltpu.SemaphoreType.DMA((2, CTX)),
+            pltpu.SemaphoreType.DMA((3, CTX)),
             pltpu.SemaphoreType.DMA((2, TP)),
         ],
-    )(tab, kq, vd, slots1, slots2, stats, gk, gv)
+    )(tab, kq, vd, slots_a, slots_b, slots2, stats, gk, gv)
 
 
 def shards(queries, keys, values, dout, match):
-    kq_in = exchange(cut(keys, queries))
-    vd_in = exchange(cut(values, dout))
+    ka_in = exchange(cut(keys, queries, 0, HALF))
+    kb_in = exchange(cut(keys, queries, HALF, HALF))
+    vd_in = exchange(cut(values, dout, 0, TOK))
     tab = make_table(match)
-    slots1, kq = pack(tab, keys, queries, kq_in)
-    far1 = swap(slots1)
-    slots2, vd = pack(tab, values, dout, vd_in)
-    slots2, far1 = lax.optimization_barrier((slots2, far1))
+    slots_a, held_a = pack(tab, keys, queries, ka_in, 0, HALF)
+    far_a = swap(slots_a)
+    slots_b, held_b = pack(tab, keys, queries, kb_in, HALF, HALF)
+    slots_b, far_a = lax.optimization_barrier((slots_b, far_a))
+    far_b = swap(slots_b)
+    slots2, vd = pack(tab, values, dout, vd_in, 0, TOK)
+    slots2, far_b = lax.optimization_barrier((slots2, far_b))
     far2 = swap(slots2)
-    prob, lse, gv = prob_side(tab, kq, vd, far1)
+    kq = hold(held_a, held_b)
+    far_a = far_a.reshape(CTX, 2, HALF, HEAD_DIM)
+    far_b = far_b.reshape(CTX, 2, HALF, HEAD_DIM)
+    prob, lse, gv = prob_side(tab, kq, vd, far_a, far_b)
     *att, att_full, stats_slots = value_side(tab, prob, lse, vd, far2)
     att_in = exchange(att[1:4])
     far_stats = swap(stats_slots)
-    *gq, gk = query_side(tab, prob, kq, vd, att_full, far1, far2)
+    *gq, gk = query_side(tab, prob, kq, vd, att_full, far_a, far_b, far2)
     gq_in = exchange(gq[1:4])
-    out = far_side(tab, kq, vd, far1, far2, far_stats, gk, gv)
+    out = far_side(tab, kq, vd, far_a, far_b, far2, far_stats, gk, gv)
     gk_in = exchange(out[1:4])
     gv_in = exchange(out[5:])
     return (join(att[0], att_in), join(gq[0], gq_in), join(out[0], gk_in), join(out[4], gv_in))

time: 210 us -> 226 us (1.076)
  starting transfers between devices: 51.2 us -> 63.4 us
  Pallas kernels: 69.5 us -> 77.2 us
  waiting for transfers between devices: 85.3 us -> 81 us
    pallas_call x10 -> x13, Pallas kernels: 33.6 us -> 41 us  [run(): pl.pallas_call(kernel, out_shape=outs if many else outs[0], in_specs=in_s...]
    all_to_all x3 -> x4, starting transfers between devices: 21.4 us -> 28.8 us  [swap(): return lax.all_to_all(slots, 'ctx', split_axis=0, concat_axis=0, tiled=True)]
    ppermute x18 -> x21, starting transfers between devices: 29.8 us -> 34.6 us  [exchange(): lax.ppermute(piece, 'tp', [(i, (i + step) % TP) for i in range(TP)])]
    all_to_all x3 -> x4, waiting for transfers between devices: 12.3 us -> 8.64 us  [swap(): return lax.all_to_all(slots, 'ctx', split_axis=0, concat_axis=0, tiled=True)]
    ppermute x18 -> x21, waiting for transfers between devices: 73 us -> 72.3 us  [exchange(): lax.ppermute(piece, 'tp', [(i, (i + step) % TP) for i in range(TP)])]
  transfers between devices with their start and end apart: 21 -> 25, of which waited for: 11 -> 12; matrix products, arithmetic and copies ran while one was open for 0% -> 0% of each run, Pallas kernels for 26% -> 28%
where the time goes in v3:
time: 226 us; the launch traced here: 224 us
  waiting for transfers between devices  81 us (36%)
  Pallas kernels  77.2 us (34%)
  starting transfers between devices  63.4 us (28%)
    ppermute x21, waiting for transfers between devices, exchange(): lax.ppermute(piece, 'tp', [(i, (i + step) % TP) for i in range(TP)])  72.3 us
    pallas_call x13, Pallas kernels, run(): pl.pallas_call(kernel, out_shape=outs if many else outs[0], in_specs=in_s...  41 us
    pallas_call x3, Pallas kernels, run(): pl.pallas_call(kernel, out_shape=outs, grid_spec=pltpu.PrefetchScalarGrid...  36.2 us
    ppermute x21, starting transfers between devices, exchange(): lax.ppermute(piece, 'tp', [(i, (i + step) % TP) for i in range(TP)])  34.6 us
    all_to_all x4, starting transfers between devices, swap(): return lax.all_to_all(slots, 'ctx', split_axis=0, concat_axis=0, tiled=True)  28.8 us
    all_to_all x4, waiting for transfers between devices, swap(): return lax.all_to_all(slots, 'ctx', split_axis=0, concat_axis=0, tiled=True)  8.64 us
  transfers between devices with their start and end apart: 25, of which 12 were waited for; matrix products, arithmetic and copies ran while one was open for 0% of the time, Pallas kernels for 28%

profile of v3, /device:TPU:32, one launch (start us, length us, event | category | flops | bytes accessed | tf_op | source)
XLA Modules:
  0.0 223.7 jit_solution(16103738711774598576)
XLA Ops:
  3.6 2.9 %collective-permute-start.1 = (bf16[2,64,1280]{2,1,0:T(8,128)(2,1)S(1)}, bf16[2,64,1280]{2,1,0:T(8,128)(2,1)S(1)}, u32[]{:S(2)}, u32[]{:S(2)}) collective-permute-start(bf16[2,64,1280]{2,1,0:T(8,128)(2,1)S(1)} %get-tuple-element.46), channel_id=1, source_target_pairs={{0,2},{1,3},{2,0},{3,1},{4,6},{5,7},{6,4},{7,5},{8,10},{9,11},{10,... | collective-permute-start | bytes 983048 | tf_op jit(solution)/shard_map/ppermute | solution.py:127
  7.9 3.7 %shard_map.84.tab = s32[8,32]{1,0:T(8,128)S(1)} custom-call(s32[10,64]{1,0:T(8,128)S(1)} %copy-done.5), custom_call_target="tpu_custom_call" | custom-call | tf_op jit(solution)/shard_map/pallas_call | solution.py:70
  12.8 8.2 %collective-permute-done.1.r2 = bf16[2,64,1280]{2,1,0:T(8,128)(2,1)S(1)} collective-permute-done((bf16[2,64,1280]{2,1,0:T(8,128)(2,1)S(1)}, bf16[2,64,1280]{2,1,0:T(8,128)(2,1)S(1)}, u32[]{:S(2)}, u32[]{:S(2)}) %collective-permute-start.1) | collective-permute-done | bytes 327712 | tf_op jit(solution)/shard_map/ppermute | solution.py:127
  21.0 3.7 %shard_map.86 = (bf16[32,128,128]{2,1,0:T(8,128)(2,1)}, bf16[2,256,1280]{2,1,0:T(8,128)(2,1)}) custom-call(s32[8,32]{1,0:T(8,128)S(1)} %shard_map.84.tab, bf16[128,5120]{1,0:T(8,128)(2,1)} %a_ref.9, bf16[128,5120]{1,0:T(8,128)(2,1)} %b_ref.9, bf16[2,64,1280]{2,1,0:T(8,128)(2,1)S(1)} %collective-permute-done.r1, ...), custom_call_target="tpu_custom_call" | custom-call | tf_op jit(solution)/shard_map/pallas_call | solution.py:70
  24.7 8.0 %all-to-all-start = ((bf16[32,128,128]{2,1,0:T(8,128)(2,1)}), bf16[32,128,128]{2,1,0:T(8,128)(2,1)S(1)}, u32[]{:S(2)}, u32[]{:S(2)}) async-start(bf16[32,128,128]{2,1,0:T(8,128)(2,1)} %get-tuple-element.58), calls=%async_computation | async-start | bytes 2097152 | tf_op jit(solution)/shard_map/all_to_all | solution.py:264
  39.4 6.2 %collective-permute-done.3.r1 = bf16[2,64,1280]{2,1,0:T(8,128)(2,1)S(1)} collective-permute-done((bf16[2,64,1280]{2,1,0:T(8,128)(2,1)S(1)}, bf16[2,64,1280]{2,1,0:T(8,128)(2,1)S(1)}, u32[]{:S(2)}, u32[]{:S(2)}) %collective-permute-start.3) | collective-permute-done | bytes 327712 | tf_op jit(solution)/shard_map/ppermute | solution.py:127
  45.6 6.9 %collective-permute-done.4.r2 = bf16[2,64,1280]{2,1,0:T(8,128)(2,1)S(1)} collective-permute-done((bf16[2,64,1280]{2,1,0:T(8,128)(2,1)S(1)}, bf16[2,64,1280]{2,1,0:T(8,128)(2,1)S(1)}, u32[]{:S(2)}, u32[]{:S(2)}) %collective-permute-start.4) | collective-permute-done | bytes 327712 | tf_op jit(solution)/shard_map/ppermute | solution.py:127
  52.7 3.7 %shard_map.88 = (bf16[32,128,128]{2,1,0:T(8,128)(2,1)}, bf16[2,256,1280]{2,1,0:T(8,128)(2,1)}) custom-call(s32[8,32]{1,0:T(8,128)S(1)} %shard_map.84.tab, bf16[128,5120]{1,0:T(8,128)(2,1)} %a_ref.9, bf16[128,5120]{1,0:T(8,128)(2,1)} %b_ref.9, bf16[2,64,1280]{2,1,0:T(8,128)(2,1)S(1)} %collective-permute-done.3.r1, ...), custom_call_target="tpu_custom_call" | custom-call | tf_op jit(solution)/shard_map/pallas_call | solution.py:70
  56.4 7.4 %all-to-all-start.1 = ((bf16[32,128,128]{2,1,0:T(8,128)(2,1)}), bf16[32,128,128]{2,1,0:T(8,128)(2,1)S(1)}, u32[]{:S(2)}, u32[]{:S(2)}) async-start(bf16[32,128,128]{2,1,0:T(8,128)(2,1)} %get-tuple-element.61), calls=%async_computation.1 | async-start | bytes 2097152 | tf_op jit(solution)/shard_map/all_to_all | solution.py:264
  70.7 12.8 %collective-permute-done.6.r1 = bf16[2,128,1280]{2,1,0:T(8,128)(2,1)S(1)} collective-permute-done((bf16[2,128,1280]{2,1,0:T(8,128)(2,1)S(1)}, bf16[2,128,1280]{2,1,0:T(8,128)(2,1)S(1)}, u32[]{:S(2)}, u32[]{:S(2)}) %collective-permute-start.6) | collective-permute-done | bytes 655392 | tf_op jit(solution)/shard_map/ppermute | solution.py:127
  83.4 14.9 %collective-permute-done.7.r2 = bf16[2,128,1280]{2,1,0:T(8,128)(2,1)S(1)} collective-permute-done((bf16[2,128,1280]{2,1,0:T(8,128)(2,1)S(1)}, bf16[2,128,1280]{2,1,0:T(8,128)(2,1)S(1)}, u32[]{:S(2)}, u32[]{:S(2)}) %collective-permute-start.7) | collective-permute-done | bytes 655392 | tf_op jit(solution)/shard_map/ppermute | solution.py:127
  98.3 4.2 %shard_map.91 = (bf16[32,256,128]{2,1,0:T(8,128)(2,1)}, bf16[2,512,1280]{2,1,0:T(8,128)(2,1)}) custom-call(s32[8,32]{1,0:T(8,128)S(1)} %shard_map.84.tab, bf16[128,5120]{1,0:T(8,128)(2,1)} %a_ref.11, bf16[128,5120]{1,0:T(8,128)(2,1)} %b_ref.11, bf16[2,128,1280]{2,1,0:T(8,128)(2,1)S(1)} %collective-permute-done.6.r1, ...), custom_call_target="tpu_custom_call" | custom-call | tf_op jit(solution)/shard_map/pallas_call | solution.py:70
  103.6 7.4 %all-to-all-start.2 = ((bf16[32,256,128]{2,1,0:T(8,128)(2,1)}), bf16[32,256,128]{2,1,0:T(8,128)(2,1)S(1)}, u32[]{:S(2)}, u32[]{:S(2)}) async-start(bf16[32,256,128]{2,1,0:T(8,128)(2,1)} %get-tuple-element.65), calls=%async_computation.2 | async-start | bytes 4194304 | tf_op jit(solution)/shard_map/all_to_all | solution.py:264
  111.0 3.2 %shard_map.89.kq.kq_ref = bf16[2,512,1280]{2,1,0:T(8,128)(2,1)} custom-call(bf16[2,256,1280]{2,1,0:T(8,128)(2,1)} %get-tuple-element.48.a_ref, bf16[2,256,1280]{2,1,0:T(8,128)(2,1)} %get-tuple-element.52.b_ref), custom_call_target="tpu_custom_call" | custom-call | tf_op jit(solution)/shard_map/pallas_call | solution.py:70
  114.2 14.9 %shard_map.92 = (bf16[2,10,256,512]{3,2,1,0:T(8,128)(2,1)}, f32[2,10,8,256]{3,2,1,0:T(8,128)}, f32[512,1280]{1,0:T(8,128)}) custom-call(s32[8,32]{1,0:T(8,128)S(1)} %shard_map.84.tab, bf16[2,512,1280]{2,1,0:T(8,128)(2,1)} %shard_map.89.kq.kq_ref, bf16[2,512,1280]{2,1,0:T(8,128)(2,1)} %get-tuple-element.56.dout.vd.vd_ref, bf16[32,2,64,128]{3,2,1,0:T(8,128)(2,1)} %bitcast.2, ...), custom_call_target="tpu_custom_call" | custom-call | tf_op jit(solution)/shard_map/pallas_call | solution.py:323
  129.1 8.6 %all-to-all-done.2.refs_0_.refs_1_.refs_2_.refs_3_.refs_8_.refs_9_.refs_10_.refs_11_.slots2 = bf16[32,256,128]{2,1,0:T(8,128)(2,1)S(1)} async-done(((bf16[32,256,128]{2,1,0:T(8,128)(2,1)}), bf16[32,256,128]{2,1,0:T(8,128)(2,1)S(1)}, u32[]{:S(2)}, u32[]{:S(2)}) %all-to-all-start.2) | async-done | bytes 2097184 | tf_op jit(solution)/shard_map/all_to_all | solution.py:264
  137.7 9.2 %shard_map.93 = (bf16[128,1280]{1,0:T(8,128)(2,1)}, bf16[128,1280]{1,0:T(8,128)(2,1)}, bf16[128,1280]{1,0:T(8,128)(2,1)}, bf16[128,1280]{1,0:T(8,128)(2,1)}, bf1...) custom-call(s32[8,32]{1,0:T(8,128)S(1)} %shard_map.84.tab, bf16[2,10,256,512]{3,2,1,0:T(8,128)(2,1)} %get-tuple-element.63.prob, ...), custom_call_target="tpu_custom_call" | custom-call | tf_op jit(solution)/shard_map/pallas_call | solution.py:323
  150.8 6.0 %all-to-all-start.3 = ((f32[32,8,256]{2,1,0:T(8,128)}), f32[32,8,256]{2,1,0:T(8,128)S(1)}, u32[]{:S(2)}, u32[]{:S(2)}) async-start(f32[32,8,256]{2,1,0:T(8,128)} %get-tuple-element.75), calls=%async_computation.3 | async-start | bytes 524288 | tf_op jit(solution)/shard_map/all_to_all | solution.py:264
  158.2 12.1 %shard_map.95 = (bf16[128,1280]{1,0:T(8,128)(2,1)}, bf16[128,1280]{1,0:T(8,128)(2,1)}, bf16[128,1280]{1,0:T(8,128)(2,1)}, bf16[128,1280]{1,0:T(8,128)(2,1)}, f32[512,1280]{1,0:T(8,128)}) custom-call(s32[8,32]{1,0:T(8,128)S(1)} %shard_map.84.tab, bf16[2,10,256,512]{3,2,1,0:T(8,128)(2,1)} %get-tuple-element.63.prob, ...), custom_call_target="tpu_custom_call" | custom-call | tf_op jit(solution)/shard_map/pallas_call | solution.py:323
  172.4 13.9 %shard_map.97 = (bf16[128,1280]{1,0:T(8,128)(2,1)}, bf16[128,1280]{1,0:T(8,128)(2,1)}, bf16[128,1280]{1,0:T(8,128)(2,1)}, bf16[128,1280]{1,0:T(8,128)(2,1)}, bf1...) custom-call(s32[8,32]{1,0:T(8,128)S(1)} %shard_map.84.tab, ...), custom_call_target="tpu_custom_call" | custom-call | tf_op jit(solution)/shard_map/pallas_call | solution.py:70
  193.2 9.8 %collective-permute-done.14.r3 = bf16[128,1280]{1,0:T(8,128)(2,1)S(1)} collective-permute-done((bf16[128,1280]{1,0:T(8,128)(2,1)S(1)}, bf16[128,1280]{1,0:T(8,128)(2,1)S(1)}, u32[]{:S(2)}, u32[]{:S(2)}) %collective-permute-start.14) | collective-permute-done | bytes 327712 | tf_op jit(solution)/shard_map/ppermute | solution.py:127
  202.9 2.4 %collective-permute-start.19 = (bf16[128,1280]{1,0:T(8,128)(2,1)}, bf16[128,1280]{1,0:T(8,128)(2,1)S(1)}, u32[]{:S(2)}, u32[]{:S(2)}) collective-permute-start(bf16[128,1280]{1,0:T(8,128)(2,1)} %get-tuple-element.84), channel_id=1, source_target_pairs={{0,2},{1,3},{2,0},{3,1},{4,6},{5,7},{6,4},{7,5},{8,10},{9,11},{10,... | collective-permute-start | bytes 983048 | tf_op jit(solution)/shard_map/ppermute | solution.py:127
  211.0 6.0 %collective-permute-done.17.r3 = bf16[128,1280]{1,0:T(8,128)(2,1)S(1)} collective-permute-done((bf16[128,1280]{1,0:T(8,128)(2,1)}, bf16[128,1280]{1,0:T(8,128)(2,1)S(1)}, u32[]{:S(2)}, u32[]{:S(2)}) %collective-permute-start.17) | collective-permute-done | bytes 327712 | tf_op jit(solution)/shard_map/ppermute | solution.py:127
  218.2 4.3 %collective-permute-done.20.r3 = bf16[128,1280]{1,0:T(8,128)(2,1)S(1)} collective-permute-done((bf16[128,1280]{1,0:T(8,128)(2,1)}, bf16[128,1280]{1,0:T(8,128)(2,1)S(1)}, u32[]{:S(2)}, u32[]{:S(2)}) %collective-permute-start.20) | collective-permute-done | bytes 327712 | tf_op jit(solution)/shard_map/ppermute | solution.py:127
  (60 shorter events, 42.2 us)
Async XLA Ops:
  3.6 17.3 %collective-permute-start.1 = (bf16[2,64,1280]{2,1,0:T(8,128)(2,1)S(1)}, bf16[2,64,1280]{2,1,0:T(8,128)(2,1)S(1)}, u32[]{:S(2)}, u32[]{:S(2)}) collective-permute-start(bf16[2,64,1280]{2,1,0:T(8,128)(2,1)S(1)} %get-tuple-element.46), channel_id=1, source_target_pairs={{0,2},{1,3},{2,0},{3,1},{4,6},{5,7},{6,4},{7,5},{8,10},{9,11},{10,... | collective-permute-start | bytes 983048 | tf_op jit(solution)/shard_map/ppermute | solution.py:127
  6.5 14.4 %collective-permute-start.2 = (bf16[2,64,1280]{2,1,0:T(8,128)(2,1)S(1)}, bf16[2,64,1280]{2,1,0:T(8,128)(2,1)S(1)}, u32[]{:S(2)}, u32[]{:S(2)}) collective-permute-start(bf16[2,64,1280]{2,1,0:T(8,128)(2,1)S(1)} %get-tuple-element.47), channel_id=1, source_target_pairs={{0,3},{1,0},{2,1},{3,2},{4,7},{5,4},{6,5},{7,6},{8,11},{9,8},{10,9... | collective-permute-start | bytes 983048 | tf_op jit(solution)/shard_map/ppermute | solution.py:127
  24.7 31.7 %all-to-all-start = ((bf16[32,128,128]{2,1,0:T(8,128)(2,1)}), bf16[32,128,128]{2,1,0:T(8,128)(2,1)S(1)}, u32[]{:S(2)}, u32[]{:S(2)}) async-start(bf16[32,128,128]{2,1,0:T(8,128)(2,1)} %get-tuple-element.58), calls=%async_computation | async-start | bytes 2097152 | tf_op jit(solution)/shard_map/all_to_all | solution.py:264
  34.1 11.5 %collective-permute-start.3 = (bf16[2,64,1280]{2,1,0:T(8,128)(2,1)S(1)}, bf16[2,64,1280]{2,1,0:T(8,128)(2,1)S(1)}, u32[]{:S(2)}, u32[]{:S(2)}) collective-permute-start(bf16[2,64,1280]{2,1,0:T(8,128)(2,1)S(1)} %get-tuple-element.49), channel_id=1, source_target_pairs={{0,1},{1,2},{2,3},{3,0},{4,5},{5,6},{6,7},{7,4},{8,9},{9,10},{10,1... | collective-permute-start | bytes 983048 | tf_op jit(solution)/shard_map/ppermute | solution.py:127
  35.4 17.1 %collective-permute-start.4 = (bf16[2,64,1280]{2,1,0:T(8,128)(2,1)S(1)}, bf16[2,64,1280]{2,1,0:T(8,128)(2,1)S(1)}, u32[]{:S(2)}, u32[]{:S(2)}) collective-permute-start(bf16[2,64,1280]{2,1,0:T(8,128)(2,1)S(1)} %get-tuple-element.50), channel_id=1, source_target_pairs={{0,2},{1,3},{2,0},{3,1},{4,6},{5,7},{6,4},{7,5},{8,10},{9,11},{10,... | collective-permute-start | bytes 983048 | tf_op jit(solution)/shard_map/ppermute | solution.py:127
  37.8 15.0 %collective-permute-start.5 = (bf16[2,64,1280]{2,1,0:T(8,128)(2,1)S(1)}, bf16[2,64,1280]{2,1,0:T(8,128)(2,1)S(1)}, u32[]{:S(2)}, u32[]{:S(2)}) collective-permute-start(bf16[2,64,1280]{2,1,0:T(8,128)(2,1)S(1)} %get-tuple-element.51), channel_id=1, source_target_pairs={{0,3},{1,0},{2,1},{3,2},{4,7},{5,4},{6,5},{7,6},{8,11},{9,8},{10,9... | collective-permute-start | bytes 983048 | tf_op jit(solution)/shard_map/ppermute | solution.py:127
  56.4 46.2 %all-to-all-start.1 = ((bf16[32,128,128]{2,1,0:T(8,128)(2,1)}), bf16[32,128,128]{2,1,0:T(8,128)(2,1)S(1)}, u32[]{:S(2)}, u32[]{:S(2)}) async-start(bf16[32,128,128]{2,1,0:T(8,128)(2,1)} %get-tuple-element.61), calls=%async_computation.1 | async-start | bytes 2097152 | tf_op jit(solution)/shard_map/all_to_all | solution.py:264
  65.4 18.0 %collective-permute-start.6 = (bf16[2,128,1280]{2,1,0:T(8,128)(2,1)S(1)}, bf16[2,128,1280]{2,1,0:T(8,128)(2,1)S(1)}, u32[]{:S(2)}, u32[]{:S(2)}) collective-permute-start(bf16[2,128,1280]{2,1,0:T(8,128)(2,1)S(1)} %get-tuple-element.53), channel_id=1, source_target_pairs={{0,1},{1,2},{2,3},{3,0},{4,5},{5,6},{6,7},{7,4},{8,9},{9,10},{10,1... | collective-permute-start | bytes 1966088 | tf_op jit(solution)/shard_map/ppermute | solution.py:127
  67.2 31.2 %collective-permute-start.7 = (bf16[2,128,1280]{2,1,0:T(8,128)(2,1)S(1)}, bf16[2,128,1280]{2,1,0:T(8,128)(2,1)S(1)}, u32[]{:S(2)}, u32[]{:S(2)}) collective-permute-start(bf16[2,128,1280]{2,1,0:T(8,128)(2,1)S(1)} %get-tuple-element.54), channel_id=1, source_target_pairs={{0,2},{1,3},{2,0},{3,1},{4,6},{5,7},{6,4},{7,5},{8,10},{9,11},{10,... | collective-permute-start | bytes 1966088 | tf_op jit(solution)/shard_map/ppermute | solution.py:127
  69.6 28.8 %collective-permute-start.8 = (bf16[2,128,1280]{2,1,0:T(8,128)(2,1)S(1)}, bf16[2,128,1280]{2,1,0:T(8,128)(2,1)S(1)}, u32[]{:S(2)}, u32[]{:S(2)}) collective-permute-start(bf16[2,128,1280]{2,1,0:T(8,128)(2,1)S(1)} %get-tuple-element.55), channel_id=1, source_target_pairs={{0,3},{1,0},{2,1},{3,2},{4,7},{5,4},{6,5},{7,6},{8,11},{9,8},{10,9... | collective-permute-start | bytes 1966088 | tf_op jit(solution)/shard_map/ppermute | solution.py:127
  103.6 34.1 %all-to-all-start.2 = ((bf16[32,256,128]{2,1,0:T(8,128)(2,1)}), bf16[32,256,128]{2,1,0:T(8,128)(2,1)S(1)}, u32[]{:S(2)}, u32[]{:S(2)}) async-start(bf16[32,256,128]{2,1,0:T(8,128)(2,1)} %get-tuple-element.65), calls=%async_computation.2 | async-start | bytes 4194304 | tf_op jit(solution)/shard_map/all_to_all | solution.py:264
  146.9 39.4 %collective-permute-start.9 = (bf16[128,1280]{1,0:T(8,128)(2,1)}, bf16[128,1280]{1,0:T(8,128)(2,1)S(1)}, u32[]{:S(2)}, u32[]{:S(2)}) collective-permute-start(bf16[128,1280]{1,0:T(8,128)(2,1)} %get-tuple-element.67), channel_id=1, source_target_pairs={{0,1},{1,2},{2,3},{3,0},{4,5},{5,6},{6,7},{7,4},{8,9},{9,10},{10,1... | collective-permute-start | bytes 983048 | tf_op jit(solution)/shard_map/ppermute | solution.py:127
  148.5 39.7 %collective-permute-start.10 = (bf16[128,1280]{1,0:T(8,128)(2,1)}, bf16[128,1280]{1,0:T(8,128)(2,1)S(1)}, u32[]{:S(2)}, u32[]{:S(2)}) collective-permute-start(bf16[128,1280]{1,0:T(8,128)(2,1)} %get-tuple-element.68), channel_id=1, source_target_pairs={{0,2},{1,3},{2,0},{3,1},{4,6},{5,7},{6,4},{7,5},{8,10},{9,11},{10,... | collective-permute-start | bytes 983048 | tf_op jit(solution)/shard_map/ppermute | solution.py:127
  150.8 21.6 %all-to-all-start.3 = ((f32[32,8,256]{2,1,0:T(8,128)}), f32[32,8,256]{2,1,0:T(8,128)S(1)}, u32[]{:S(2)}, u32[]{:S(2)}) async-start(f32[32,8,256]{2,1,0:T(8,128)} %get-tuple-element.75), calls=%async_computation.3 | async-start | bytes 524288 | tf_op jit(solution)/shard_map/all_to_all | solution.py:264
  156.8 31.7 %collective-permute-start.11 = (bf16[128,1280]{1,0:T(8,128)(2,1)}, bf16[128,1280]{1,0:T(8,128)(2,1)S(1)}, u32[]{:S(2)}, u32[]{:S(2)}) collective-permute-start(bf16[128,1280]{1,0:T(8,128)(2,1)} %get-tuple-element.69), channel_id=1, source_target_pairs={{0,3},{1,0},{2,1},{3,2},{4,7},{5,4},{6,5},{7,6},{8,11},{9,8},{10,9... | collective-permute-start | bytes 983048 | tf_op jit(solution)/shard_map/ppermute | solution.py:127
  170.3 20.5 %collective-permute-start.12 = (bf16[128,1280]{1,0:T(8,128)(2,1)}, bf16[128,1280]{1,0:T(8,128)(2,1)S(1)}, u32[]{:S(2)}, u32[]{:S(2)}) collective-permute-start(bf16[128,1280]{1,0:T(8,128)(2,1)} %get-tuple-element.72), channel_id=1, source_target_pairs={{0,1},{1,2},{2,3},{3,0},{4,5},{5,6},{6,7},{7,4},{8,9},{9,10},{10,1... | collective-permute-start | bytes 983048 | tf_op jit(solution)/shard_map/ppermute | solution.py:127
  171.3 21.9 %collective-permute-start.13 = (bf16[128,1280]{1,0:T(8,128)(2,1)}, bf16[128,1280]{1,0:T(8,128)(2,1)S(1)}, u32[]{:S(2)}, u32[]{:S(2)}) collective-permute-start(bf16[128,1280]{1,0:T(8,128)(2,1)} %get-tuple-element.73), channel_id=1, source_target_pairs={{0,2},{1,3},{2,0},{3,1},{4,6},{5,7},{6,4},{7,5},{8,10},{9,11},{10,... | collective-permute-start | bytes 983048 | tf_op jit(solution)/shard_map/ppermute | solution.py:127
  186.3 16.6 %collective-permute-start.14 = (bf16[128,1280]{1,0:T(8,128)(2,1)S(1)}, bf16[128,1280]{1,0:T(8,128)(2,1)S(1)}, u32[]{:S(2)}, u32[]{:S(2)}) collective-permute-start(bf16[128,1280]{1,0:T(8,128)(2,1)S(1)} %copy-done.8), channel_id=1, source_target_pairs={{0,3},{1,0},{2,1},{3,2},{4,7},{5,4},{6,5},{7,6},{8,11},{9,8},{10,9... | collective-permute-start | bytes 983048 | tf_op jit(solution)/shard_map/ppermute | solution.py:127
  188.2 19.0 %collective-permute-start.15 = (bf16[128,1280]{1,0:T(8,128)(2,1)}, bf16[128,1280]{1,0:T(8,128)(2,1)S(1)}, u32[]{:S(2)}, u32[]{:S(2)}) collective-permute-start(bf16[128,1280]{1,0:T(8,128)(2,1)} %get-tuple-element.79), channel_id=1, source_target_pairs={{0,1},{1,2},{2,3},{3,0},{4,5},{5,6},{6,7},{7,4},{8,9},{9,10},{10,1... | collective-permute-start | bytes 983048 | tf_op jit(solution)/shard_map/ppermute | solution.py:127
  188.6 22.4 %collective-permute-start.16 = (bf16[128,1280]{1,0:T(8,128)(2,1)}, bf16[128,1280]{1,0:T(8,128)(2,1)S(1)}, u32[]{:S(2)}, u32[]{:S(2)}) collective-permute-start(bf16[128,1280]{1,0:T(8,128)(2,1)} %get-tuple-element.80), channel_id=1, source_target_pairs={{0,2},{1,3},{2,0},{3,1},{4,6},{5,7},{6,4},{7,5},{8,10},{9,11},{10,... | collective-permute-start | bytes 983048 | tf_op jit(solution)/shard_map/ppermute | solution.py:127
  190.8 26.2 %collective-permute-start.17 = (bf16[128,1280]{1,0:T(8,128)(2,1)}, bf16[128,1280]{1,0:T(8,128)(2,1)S(1)}, u32[]{:S(2)}, u32[]{:S(2)}) collective-permute-start(bf16[128,1280]{1,0:T(8,128)(2,1)} %get-tuple-element.81), channel_id=1, source_target_pairs={{0,3},{1,0},{2,1},{3,2},{4,7},{5,4},{6,5},{7,6},{8,11},{9,8},{10,9... | collective-permute-start | bytes 983048 | tf_op jit(solution)/shard_map/ppermute | solution.py:127
  193.2 25.0 %collective-permute-start.18 = (bf16[128,1280]{1,0:T(8,128)(2,1)}, bf16[128,1280]{1,0:T(8,128)(2,1)S(1)}, u32[]{:S(2)}, u32[]{:S(2)}) collective-permute-start(bf16[128,1280]{1,0:T(8,128)(2,1)} %get-tuple-element.83), channel_id=1, source_target_pairs={{0,1},{1,2},{2,3},{3,0},{4,5},{5,6},{6,7},{7,4},{8,9},{9,10},{10,1... | collective-permute-start | bytes 983048 | tf_op jit(solution)/shard_map/ppermute | solution.py:127
  202.9 15.2 %collective-permute-start.19 = (bf16[128,1280]{1,0:T(8,128)(2,1)}, bf16[128,1280]{1,0:T(8,128)(2,1)S(1)}, u32[]{:S(2)}, u32[]{:S(2)}) collective-permute-start(bf16[128,1280]{1,0:T(8,128)(2,1)} %get-tuple-element.84), channel_id=1, source_target_pairs={{0,2},{1,3},{2,0},{3,1},{4,6},{5,7},{6,4},{7,5},{8,10},{9,11},{10,... | collective-permute-start | bytes 983048 | tf_op jit(solution)/shard_map/ppermute | solution.py:127
  207.2 15.3 %collective-permute-start.20 = (bf16[128,1280]{1,0:T(8,128)(2,1)}, bf16[128,1280]{1,0:T(8,128)(2,1)S(1)}, u32[]{:S(2)}, u32[]{:S(2)}) collective-permute-start(bf16[128,1280]{1,0:T(8,128)(2,1)} %get-tuple-element.85), channel_id=1, source_target_pairs={{0,3},{1,0},{2,1},{3,2},{4,7},{5,4},{6,5},{7,6},{8,11},{9,8},{10,9... | collective-permute-start | bytes 983048 | tf_op jit(solution)/shard_map/ppermute | solution.py:127
  (10 other events, 101.1 us)

commit v4 on v3

--- a/solution.py
+++ b/solution.py
@@ -164,17 +164,16 @@
     lax.fori_loop(0, CTX, clear, 0)
 
     def owner_side(d, carry):
+        code = jnp.int32(0)
         for n in range(2):
             for g in range(GROUPS):
                 block = 2 * d + n
                 m = match[g, block]
-
-                @pl.when((m < block) & ((m >> 1) == ctx))
-                def _():
-                    tab[0, d] = m & 1
-                    tab[1, d] = g
-                    tab[2, d] = 1
-
+                hit = (m < block) & ((m >> 1) == ctx)
+                code = jnp.where(hit, 32 + g + 16 * (m & 1), code)
+        tab[0, d] = (code >> 4) & 1
+        tab[1, d] = code & 15
+        tab[2, d] = code >> 5
         return carry
 
     lax.fori_loop(ctx + 1, CTX, owner_side, 0)

time: 226 us -> 226 us (level)
  no operation moved by 1% of the time
where the time goes in v4:
time: 226 us; the launch traced here: 224 us
  waiting for transfers between devices  81.1 us (36%)
  Pallas kernels  77 us (34%)
  starting transfers between devices  63.4 us (28%)
    ppermute x21, waiting for transfers between devices, exchange(): lax.ppermute(piece, 'tp', [(i, (i + step) % TP) for i in range(TP)])  72.5 us
    pallas_call x13, Pallas kernels, run(): pl.pallas_call(kernel, out_shape=outs if many else outs[0], in_specs=in_s...  40.9 us
    pallas_call x3, Pallas kernels, run(): pl.pallas_call(kernel, out_shape=outs, grid_spec=pltpu.PrefetchScalarGrid...  36.2 us
    ppermute x21, starting transfers between devices, exchange(): lax.ppermute(piece, 'tp', [(i, (i + step) % TP) for i in range(TP)])  34.6 us
    all_to_all x4, starting transfers between devices, swap(): return lax.all_to_all(slots, 'ctx', split_axis=0, concat_axis=0, tiled=True)  28.8 us
    all_to_all x4, waiting for transfers between devices, swap(): return lax.all_to_all(slots, 'ctx', split_axis=0, concat_axis=0, tiled=True)  8.64 us
  transfers between devices with their start and end apart: 25, of which 12 were waited for; matrix products, arithmetic and copies ran while one was open for 0% of the time, Pallas kernels for 28%

profile of v4, /device:TPU:32, one launch (start us, length us, event | category | flops | bytes accessed | tf_op | source)
XLA Modules:
  0.0 223.7 jit_solution(3550858195873397170)
XLA Ops:
  3.6 2.9 %collective-permute-start.1 = (bf16[2,64,1280]{2,1,0:T(8,128)(2,1)S(1)}, bf16[2,64,1280]{2,1,0:T(8,128)(2,1)S(1)}, u32[]{:S(2)}, u32[]{:S(2)}) collective-permute-start(bf16[2,64,1280]{2,1,0:T(8,128)(2,1)S(1)} %get-tuple-element.46), channel_id=1, source_target_pairs={{0,2},{1,3},{2,0},{3,1},{4,6},{5,7},{6,4},{7,5},{8,10},{9,11},{10,... | collective-permute-start | bytes 983048 | tf_op jit(solution)/shard_map/ppermute | solution.py:127
  7.9 3.6 %shard_map.84.tab = s32[8,32]{1,0:T(8,128)S(1)} custom-call(s32[10,64]{1,0:T(8,128)S(1)} %copy-done.5), custom_call_target="tpu_custom_call" | custom-call | tf_op jit(solution)/shard_map/pallas_call | solution.py:70
  12.8 8.2 %collective-permute-done.1.r2 = bf16[2,64,1280]{2,1,0:T(8,128)(2,1)S(1)} collective-permute-done((bf16[2,64,1280]{2,1,0:T(8,128)(2,1)S(1)}, bf16[2,64,1280]{2,1,0:T(8,128)(2,1)S(1)}, u32[]{:S(2)}, u32[]{:S(2)}) %collective-permute-start.1) | collective-permute-done | bytes 327712 | tf_op jit(solution)/shard_map/ppermute | solution.py:127
  21.0 3.7 %shard_map.86 = (bf16[32,128,128]{2,1,0:T(8,128)(2,1)}, bf16[2,256,1280]{2,1,0:T(8,128)(2,1)}) custom-call(s32[8,32]{1,0:T(8,128)S(1)} %shard_map.84.tab, bf16[128,5120]{1,0:T(8,128)(2,1)} %a_ref.9, bf16[128,5120]{1,0:T(8,128)(2,1)} %b_ref.9, bf16[2,64,1280]{2,1,0:T(8,128)(2,1)S(1)} %collective-permute-done.r1, ...), custom_call_target="tpu_custom_call" | custom-call | tf_op jit(solution)/shard_map/pallas_call | solution.py:70
  24.7 8.0 %all-to-all-start = ((bf16[32,128,128]{2,1,0:T(8,128)(2,1)}), bf16[32,128,128]{2,1,0:T(8,128)(2,1)S(1)}, u32[]{:S(2)}, u32[]{:S(2)}) async-start(bf16[32,128,128]{2,1,0:T(8,128)(2,1)} %get-tuple-element.58), calls=%async_computation | async-start | bytes 2097152 | tf_op jit(solution)/shard_map/all_to_all | solution.py:263
  39.4 6.2 %collective-permute-done.3.r1 = bf16[2,64,1280]{2,1,0:T(8,128)(2,1)S(1)} collective-permute-done((bf16[2,64,1280]{2,1,0:T(8,128)(2,1)S(1)}, bf16[2,64,1280]{2,1,0:T(8,128)(2,1)S(1)}, u32[]{:S(2)}, u32[]{:S(2)}) %collective-permute-start.3) | collective-permute-done | bytes 327712 | tf_op jit(solution)/shard_map/ppermute | solution.py:127
  45.6 6.9 %collective-permute-done.4.r2 = bf16[2,64,1280]{2,1,0:T(8,128)(2,1)S(1)} collective-permute-done((bf16[2,64,1280]{2,1,0:T(8,128)(2,1)S(1)}, bf16[2,64,1280]{2,1,0:T(8,128)(2,1)S(1)}, u32[]{:S(2)}, u32[]{:S(2)}) %collective-permute-start.4) | collective-permute-done | bytes 327712 | tf_op jit(solution)/shard_map/ppermute | solution.py:127
  52.7 3.7 %shard_map.88 = (bf16[32,128,128]{2,1,0:T(8,128)(2,1)}, bf16[2,256,1280]{2,1,0:T(8,128)(2,1)}) custom-call(s32[8,32]{1,0:T(8,128)S(1)} %shard_map.84.tab, bf16[128,5120]{1,0:T(8,128)(2,1)} %a_ref.9, bf16[128,5120]{1,0:T(8,128)(2,1)} %b_ref.9, bf16[2,64,1280]{2,1,0:T(8,128)(2,1)S(1)} %collective-permute-done.3.r1, ...), custom_call_target="tpu_custom_call" | custom-call | tf_op jit(solution)/shard_map/pallas_call | solution.py:70
  56.4 7.4 %all-to-all-start.1 = ((bf16[32,128,128]{2,1,0:T(8,128)(2,1)}), bf16[32,128,128]{2,1,0:T(8,128)(2,1)S(1)}, u32[]{:S(2)}, u32[]{:S(2)}) async-start(bf16[32,128,128]{2,1,0:T(8,128)(2,1)} %get-tuple-element.61), calls=%async_computation.1 | async-start | bytes 2097152 | tf_op jit(solution)/shard_map/all_to_all | solution.py:263
  70.7 12.8 %collective-permute-done.6.r1 = bf16[2,128,1280]{2,1,0:T(8,128)(2,1)S(1)} collective-permute-done((bf16[2,128,1280]{2,1,0:T(8,128)(2,1)S(1)}, bf16[2,128,1280]{2,1,0:T(8,128)(2,1)S(1)}, u32[]{:S(2)}, u32[]{:S(2)}) %collective-permute-start.6) | collective-permute-done | bytes 655392 | tf_op jit(solution)/shard_map/ppermute | solution.py:127
  83.4 14.9 %collective-permute-done.7.r2 = bf16[2,128,1280]{2,1,0:T(8,128)(2,1)S(1)} collective-permute-done((bf16[2,128,1280]{2,1,0:T(8,128)(2,1)S(1)}, bf16[2,128,1280]{2,1,0:T(8,128)(2,1)S(1)}, u32[]{:S(2)}, u32[]{:S(2)}) %collective-permute-start.7) | collective-permute-done | bytes 655392 | tf_op jit(solution)/shard_map/ppermute | solution.py:127
  98.3 4.2 %shard_map.91 = (bf16[32,256,128]{2,1,0:T(8,128)(2,1)}, bf16[2,512,1280]{2,1,0:T(8,128)(2,1)}) custom-call(s32[8,32]{1,0:T(8,128)S(1)} %shard_map.84.tab, bf16[128,5120]{1,0:T(8,128)(2,1)} %a_ref.11, bf16[128,5120]{1,0:T(8,128)(2,1)} %b_ref.11, bf16[2,128,1280]{2,1,0:T(8,128)(2,1)S(1)} %collective-permute-done.6.r1, ...), custom_call_target="tpu_custom_call" | custom-call | tf_op jit(solution)/shard_map/pallas_call | solution.py:70
  103.6 7.4 %all-to-all-start.2 = ((bf16[32,256,128]{2,1,0:T(8,128)(2,1)}), bf16[32,256,128]{2,1,0:T(8,128)(2,1)S(1)}, u32[]{:S(2)}, u32[]{:S(2)}) async-start(bf16[32,256,128]{2,1,0:T(8,128)(2,1)} %get-tuple-element.65), calls=%async_computation.2 | async-start | bytes 4194304 | tf_op jit(solution)/shard_map/all_to_all | solution.py:263
  111.0 3.2 %shard_map.89.kq.kq_ref = bf16[2,512,1280]{2,1,0:T(8,128)(2,1)} custom-call(bf16[2,256,1280]{2,1,0:T(8,128)(2,1)} %get-tuple-element.48.a_ref, bf16[2,256,1280]{2,1,0:T(8,128)(2,1)} %get-tuple-element.52.b_ref), custom_call_target="tpu_custom_call" | custom-call | tf_op jit(solution)/shard_map/pallas_call | solution.py:70
  114.2 14.9 %shard_map.92 = (bf16[2,10,256,512]{3,2,1,0:T(8,128)(2,1)}, f32[2,10,8,256]{3,2,1,0:T(8,128)}, f32[512,1280]{1,0:T(8,128)}) custom-call(s32[8,32]{1,0:T(8,128)S(1)} %shard_map.84.tab, bf16[2,512,1280]{2,1,0:T(8,128)(2,1)} %shard_map.89.kq.kq_ref, bf16[2,512,1280]{2,1,0:T(8,128)(2,1)} %get-tuple-element.56.dout.vd.vd_ref, bf16[32,2,64,128]{3,2,1,0:T(8,128)(2,1)} %bitcast.2, ...), custom_call_target="tpu_custom_call" | custom-call | tf_op jit(solution)/shard_map/pallas_call | solution.py:322
  129.1 8.6 %all-to-all-done.2.refs_0_.refs_1_.refs_2_.refs_3_.refs_8_.refs_9_.refs_10_.refs_11_.slots2 = bf16[32,256,128]{2,1,0:T(8,128)(2,1)S(1)} async-done(((bf16[32,256,128]{2,1,0:T(8,128)(2,1)}), bf16[32,256,128]{2,1,0:T(8,128)(2,1)S(1)}, u32[]{:S(2)}, u32[]{:S(2)}) %all-to-all-start.2) | async-done | bytes 2097184 | tf_op jit(solution)/shard_map/all_to_all | solution.py:263
  137.7 9.2 %shard_map.93 = (bf16[128,1280]{1,0:T(8,128)(2,1)}, bf16[128,1280]{1,0:T(8,128)(2,1)}, bf16[128,1280]{1,0:T(8,128)(2,1)}, bf16[128,1280]{1,0:T(8,128)(2,1)}, bf1...) custom-call(s32[8,32]{1,0:T(8,128)S(1)} %shard_map.84.tab, bf16[2,10,256,512]{3,2,1,0:T(8,128)(2,1)} %get-tuple-element.63.prob, ...), custom_call_target="tpu_custom_call" | custom-call | tf_op jit(solution)/shard_map/pallas_call | solution.py:322
  150.8 6.0 %all-to-all-start.3 = ((f32[32,8,256]{2,1,0:T(8,128)}), f32[32,8,256]{2,1,0:T(8,128)S(1)}, u32[]{:S(2)}, u32[]{:S(2)}) async-start(f32[32,8,256]{2,1,0:T(8,128)} %get-tuple-element.75), calls=%async_computation.3 | async-start | bytes 524288 | tf_op jit(solution)/shard_map/all_to_all | solution.py:263
  158.2 12.1 %shard_map.95 = (bf16[128,1280]{1,0:T(8,128)(2,1)}, bf16[128,1280]{1,0:T(8,128)(2,1)}, bf16[128,1280]{1,0:T(8,128)(2,1)}, bf16[128,1280]{1,0:T(8,128)(2,1)}, f32[512,1280]{1,0:T(8,128)}) custom-call(s32[8,32]{1,0:T(8,128)S(1)} %shard_map.84.tab, bf16[2,10,256,512]{3,2,1,0:T(8,128)(2,1)} %get-tuple-element.63.prob, ...), custom_call_target="tpu_custom_call" | custom-call | tf_op jit(solution)/shard_map/pallas_call | solution.py:322
  172.4 13.9 %shard_map.97 = (bf16[128,1280]{1,0:T(8,128)(2,1)}, bf16[128,1280]{1,0:T(8,128)(2,1)}, bf16[128,1280]{1,0:T(8,128)(2,1)}, bf16[128,1280]{1,0:T(8,128)(2,1)}, bf1...) custom-call(s32[8,32]{1,0:T(8,128)S(1)} %shard_map.84.tab, ...), custom_call_target="tpu_custom_call" | custom-call | tf_op jit(solution)/shard_map/pallas_call | solution.py:70
  193.2 9.8 %collective-permute-done.14.r3 = bf16[128,1280]{1,0:T(8,128)(2,1)S(1)} collective-permute-done((bf16[128,1280]{1,0:T(8,128)(2,1)S(1)}, bf16[128,1280]{1,0:T(8,128)(2,1)S(1)}, u32[]{:S(2)}, u32[]{:S(2)}) %collective-permute-start.14) | collective-permute-done | bytes 327712 | tf_op jit(solution)/shard_map/ppermute | solution.py:127
  202.9 2.4 %collective-permute-start.19 = (bf16[128,1280]{1,0:T(8,128)(2,1)}, bf16[128,1280]{1,0:T(8,128)(2,1)S(1)}, u32[]{:S(2)}, u32[]{:S(2)}) collective-permute-start(bf16[128,1280]{1,0:T(8,128)(2,1)} %get-tuple-element.84), channel_id=1, source_target_pairs={{0,2},{1,3},{2,0},{3,1},{4,6},{5,7},{6,4},{7,5},{8,10},{9,11},{10,... | collective-permute-start | bytes 983048 | tf_op jit(solution)/shard_map/ppermute | solution.py:127
  211.0 6.0 %collective-permute-done.17.r3 = bf16[128,1280]{1,0:T(8,128)(2,1)S(1)} collective-permute-done((bf16[128,1280]{1,0:T(8,128)(2,1)}, bf16[128,1280]{1,0:T(8,128)(2,1)S(1)}, u32[]{:S(2)}, u32[]{:S(2)}) %collective-permute-start.17) | collective-permute-done | bytes 327712 | tf_op jit(solution)/shard_map/ppermute | solution.py:127
  218.2 4.3 %collective-permute-done.20.r3 = bf16[128,1280]{1,0:T(8,128)(2,1)S(1)} collective-permute-done((bf16[128,1280]{1,0:T(8,128)(2,1)}, bf16[128,1280]{1,0:T(8,128)(2,1)S(1)}, u32[]{:S(2)}, u32[]{:S(2)}) %collective-permute-start.20) | collective-permute-done | bytes 327712 | tf_op jit(solution)/shard_map/ppermute | solution.py:127
  (60 shorter events, 42.3 us)
Async XLA Ops:
  3.6 17.3 %collective-permute-start.1 = (bf16[2,64,1280]{2,1,0:T(8,128)(2,1)S(1)}, bf16[2,64,1280]{2,1,0:T(8,128)(2,1)S(1)}, u32[]{:S(2)}, u32[]{:S(2)}) collective-permute-start(bf16[2,64,1280]{2,1,0:T(8,128)(2,1)S(1)} %get-tuple-element.46), channel_id=1, source_target_pairs={{0,2},{1,3},{2,0},{3,1},{4,6},{5,7},{6,4},{7,5},{8,10},{9,11},{10,... | collective-permute-start | bytes 983048 | tf_op jit(solution)/shard_map/ppermute | solution.py:127
  6.5 14.4 %collective-permute-start.2 = (bf16[2,64,1280]{2,1,0:T(8,128)(2,1)S(1)}, bf16[2,64,1280]{2,1,0:T(8,128)(2,1)S(1)}, u32[]{:S(2)}, u32[]{:S(2)}) collective-permute-start(bf16[2,64,1280]{2,1,0:T(8,128)(2,1)S(1)} %get-tuple-element.47), channel_id=1, source_target_pairs={{0,3},{1,0},{2,1},{3,2},{4,7},{5,4},{6,5},{7,6},{8,11},{9,8},{10,9... | collective-permute-start | bytes 983048 | tf_op jit(solution)/shard_map/ppermute | solution.py:127
  24.7 31.7 %all-to-all-start = ((bf16[32,128,128]{2,1,0:T(8,128)(2,1)}), bf16[32,128,128]{2,1,0:T(8,128)(2,1)S(1)}, u32[]{:S(2)}, u32[]{:S(2)}) async-start(bf16[32,128,128]{2,1,0:T(8,128)(2,1)} %get-tuple-element.58), calls=%async_computation | async-start | bytes 2097152 | tf_op jit(solution)/shard_map/all_to_all | solution.py:263
  34.1 11.5 %collective-permute-start.3 = (bf16[2,64,1280]{2,1,0:T(8,128)(2,1)S(1)}, bf16[2,64,1280]{2,1,0:T(8,128)(2,1)S(1)}, u32[]{:S(2)}, u32[]{:S(2)}) collective-permute-start(bf16[2,64,1280]{2,1,0:T(8,128)(2,1)S(1)} %get-tuple-element.49), channel_id=1, source_target_pairs={{0,1},{1,2},{2,3},{3,0},{4,5},{5,6},{6,7},{7,4},{8,9},{9,10},{10,1... | collective-permute-start | bytes 983048 | tf_op jit(solution)/shard_map/ppermute | solution.py:127
  35.4 17.1 %collective-permute-start.4 = (bf16[2,64,1280]{2,1,0:T(8,128)(2,1)S(1)}, bf16[2,64,1280]{2,1,0:T(8,128)(2,1)S(1)}, u32[]{:S(2)}, u32[]{:S(2)}) collective-permute-start(bf16[2,64,1280]{2,1,0:T(8,128)(2,1)S(1)} %get-tuple-element.50), channel_id=1, source_target_pairs={{0,2},{1,3},{2,0},{3,1},{4,6},{5,7},{6,4},{7,5},{8,10},{9,11},{10,... | collective-permute-start | bytes 983048 | tf_op jit(solution)/shard_map/ppermute | solution.py:127
  37.8 15.0 %collective-permute-start.5 = (bf16[2,64,1280]{2,1,0:T(8,128)(2,1)S(1)}, bf16[2,64,1280]{2,1,0:T(8,128)(2,1)S(1)}, u32[]{:S(2)}, u32[]{:S(2)}) collective-permute-start(bf16[2,64,1280]{2,1,0:T(8,128)(2,1)S(1)} %get-tuple-element.51), channel_id=1, source_target_pairs={{0,3},{1,0},{2,1},{3,2},{4,7},{5,4},{6,5},{7,6},{8,11},{9,8},{10,9... | collective-permute-start | bytes 983048 | tf_op jit(solution)/shard_map/ppermute | solution.py:127
  56.4 46.2 %all-to-all-start.1 = ((bf16[32,128,128]{2,1,0:T(8,128)(2,1)}), bf16[32,128,128]{2,1,0:T(8,128)(2,1)S(1)}, u32[]{:S(2)}, u32[]{:S(2)}) async-start(bf16[32,128,128]{2,1,0:T(8,128)(2,1)} %get-tuple-element.61), calls=%async_computation.1 | async-start | bytes 2097152 | tf_op jit(solution)/shard_map/all_to_all | solution.py:263
  65.4 18.0 %collective-permute-start.6 = (bf16[2,128,1280]{2,1,0:T(8,128)(2,1)S(1)}, bf16[2,128,1280]{2,1,0:T(8,128)(2,1)S(1)}, u32[]{:S(2)}, u32[]{:S(2)}) collective-permute-start(bf16[2,128,1280]{2,1,0:T(8,128)(2,1)S(1)} %get-tuple-element.53), channel_id=1, source_target_pairs={{0,1},{1,2},{2,3},{3,0},{4,5},{5,6},{6,7},{7,4},{8,9},{9,10},{10,1... | collective-permute-start | bytes 1966088 | tf_op jit(solution)/shard_map/ppermute | solution.py:127
  67.2 31.2 %collective-permute-start.7 = (bf16[2,128,1280]{2,1,0:T(8,128)(2,1)S(1)}, bf16[2,128,1280]{2,1,0:T(8,128)(2,1)S(1)}, u32[]{:S(2)}, u32[]{:S(2)}) collective-permute-start(bf16[2,128,1280]{2,1,0:T(8,128)(2,1)S(1)} %get-tuple-element.54), channel_id=1, source_target_pairs={{0,2},{1,3},{2,0},{3,1},{4,6},{5,7},{6,4},{7,5},{8,10},{9,11},{10,... | collective-permute-start | bytes 1966088 | tf_op jit(solution)/shard_map/ppermute | solution.py:127
  69.6 28.8 %collective-permute-start.8 = (bf16[2,128,1280]{2,1,0:T(8,128)(2,1)S(1)}, bf16[2,128,1280]{2,1,0:T(8,128)(2,1)S(1)}, u32[]{:S(2)}, u32[]{:S(2)}) collective-permute-start(bf16[2,128,1280]{2,1,0:T(8,128)(2,1)S(1)} %get-tuple-element.55), channel_id=1, source_target_pairs={{0,3},{1,0},{2,1},{3,2},{4,7},{5,4},{6,5},{7,6},{8,11},{9,8},{10,9... | collective-permute-start | bytes 1966088 | tf_op jit(solution)/shard_map/ppermute | solution.py:127
  103.6 34.1 %all-to-all-start.2 = ((bf16[32,256,128]{2,1,0:T(8,128)(2,1)}), bf16[32,256,128]{2,1,0:T(8,128)(2,1)S(1)}, u32[]{:S(2)}, u32[]{:S(2)}) async-start(bf16[32,256,128]{2,1,0:T(8,128)(2,1)} %get-tuple-element.65), calls=%async_computation.2 | async-start | bytes 4194304 | tf_op jit(solution)/shard_map/all_to_all | solution.py:263
  146.9 39.4 %collective-permute-start.9 = (bf16[128,1280]{1,0:T(8,128)(2,1)}, bf16[128,1280]{1,0:T(8,128)(2,1)S(1)}, u32[]{:S(2)}, u32[]{:S(2)}) collective-permute-start(bf16[128,1280]{1,0:T(8,128)(2,1)} %get-tuple-element.67), channel_id=1, source_target_pairs={{0,1},{1,2},{2,3},{3,0},{4,5},{5,6},{6,7},{7,4},{8,9},{9,10},{10,1... | collective-permute-start | bytes 983048 | tf_op jit(solution)/shard_map/ppermute | solution.py:127
  148.5 39.7 %collective-permute-start.10 = (bf16[128,1280]{1,0:T(8,128)(2,1)}, bf16[128,1280]{1,0:T(8,128)(2,1)S(1)}, u32[]{:S(2)}, u32[]{:S(2)}) collective-permute-start(bf16[128,1280]{1,0:T(8,128)(2,1)} %get-tuple-element.68), channel_id=1, source_target_pairs={{0,2},{1,3},{2,0},{3,1},{4,6},{5,7},{6,4},{7,5},{8,10},{9,11},{10,... | collective-permute-start | bytes 983048 | tf_op jit(solution)/shard_map/ppermute | solution.py:127
  150.8 21.6 %all-to-all-start.3 = ((f32[32,8,256]{2,1,0:T(8,128)}), f32[32,8,256]{2,1,0:T(8,128)S(1)}, u32[]{:S(2)}, u32[]{:S(2)}) async-start(f32[32,8,256]{2,1,0:T(8,128)} %get-tuple-element.75), calls=%async_computation.3 | async-start | bytes 524288 | tf_op jit(solution)/shard_map/all_to_all | solution.py:263
  156.8 31.7 %collective-permute-start.11 = (bf16[128,1280]{1,0:T(8,128)(2,1)}, bf16[128,1280]{1,0:T(8,128)(2,1)S(1)}, u32[]{:S(2)}, u32[]{:S(2)}) collective-permute-start(bf16[128,1280]{1,0:T(8,128)(2,1)} %get-tuple-element.69), channel_id=1, source_target_pairs={{0,3},{1,0},{2,1},{3,2},{4,7},{5,4},{6,5},{7,6},{8,11},{9,8},{10,9... | collective-permute-start | bytes 983048 | tf_op jit(solution)/shard_map/ppermute | solution.py:127
  170.3 20.5 %collective-permute-start.12 = (bf16[128,1280]{1,0:T(8,128)(2,1)}, bf16[128,1280]{1,0:T(8,128)(2,1)S(1)}, u32[]{:S(2)}, u32[]{:S(2)}) collective-permute-start(bf16[128,1280]{1,0:T(8,128)(2,1)} %get-tuple-element.72), channel_id=1, source_target_pairs={{0,1},{1,2},{2,3},{3,0},{4,5},{5,6},{6,7},{7,4},{8,9},{9,10},{10,1... | collective-permute-start | bytes 983048 | tf_op jit(solution)/shard_map/ppermute | solution.py:127
  171.3 21.9 %collective-permute-start.13 = (bf16[128,1280]{1,0:T(8,128)(2,1)}, bf16[128,1280]{1,0:T(8,128)(2,1)S(1)}, u32[]{:S(2)}, u32[]{:S(2)}) collective-permute-start(bf16[128,1280]{1,0:T(8,128)(2,1)} %get-tuple-element.73), channel_id=1, source_target_pairs={{0,2},{1,3},{2,0},{3,1},{4,6},{5,7},{6,4},{7,5},{8,10},{9,11},{10,... | collective-permute-start | bytes 983048 | tf_op jit(solution)/shard_map/ppermute | solution.py:127
  186.3 16.6 %collective-permute-start.14 = (bf16[128,1280]{1,0:T(8,128)(2,1)S(1)}, bf16[128,1280]{1,0:T(8,128)(2,1)S(1)}, u32[]{:S(2)}, u32[]{:S(2)}) collective-permute-start(bf16[128,1280]{1,0:T(8,128)(2,1)S(1)} %copy-done.8), channel_id=1, source_target_pairs={{0,3},{1,0},{2,1},{3,2},{4,7},{5,4},{6,5},{7,6},{8,11},{9,8},{10,9... | collective-permute-start | bytes 983048 | tf_op jit(solution)/shard_map/ppermute | solution.py:127
  188.2 19.0 %collective-permute-start.15 = (bf16[128,1280]{1,0:T(8,128)(2,1)}, bf16[128,1280]{1,0:T(8,128)(2,1)S(1)}, u32[]{:S(2)}, u32[]{:S(2)}) collective-permute-start(bf16[128,1280]{1,0:T(8,128)(2,1)} %get-tuple-element.79), channel_id=1, source_target_pairs={{0,1},{1,2},{2,3},{3,0},{4,5},{5,6},{6,7},{7,4},{8,9},{9,10},{10,1... | collective-permute-start | bytes 983048 | tf_op jit(solution)/shard_map/ppermute | solution.py:127
  188.6 22.4 %collective-permute-start.16 = (bf16[128,1280]{1,0:T(8,128)(2,1)}, bf16[128,1280]{1,0:T(8,128)(2,1)S(1)}, u32[]{:S(2)}, u32[]{:S(2)}) collective-permute-start(bf16[128,1280]{1,0:T(8,128)(2,1)} %get-tuple-element.80), channel_id=1, source_target_pairs={{0,2},{1,3},{2,0},{3,1},{4,6},{5,7},{6,4},{7,5},{8,10},{9,11},{10,... | collective-permute-start | bytes 983048 | tf_op jit(solution)/shard_map/ppermute | solution.py:127
  190.8 26.2 %collective-permute-start.17 = (bf16[128,1280]{1,0:T(8,128)(2,1)}, bf16[128,1280]{1,0:T(8,128)(2,1)S(1)}, u32[]{:S(2)}, u32[]{:S(2)}) collective-permute-start(bf16[128,1280]{1,0:T(8,128)(2,1)} %get-tuple-element.81), channel_id=1, source_target_pairs={{0,3},{1,0},{2,1},{3,2},{4,7},{5,4},{6,5},{7,6},{8,11},{9,8},{10,9... | collective-permute-start | bytes 983048 | tf_op jit(solution)/shard_map/ppermute | solution.py:127
  193.2 25.0 %collective-permute-start.18 = (bf16[128,1280]{1,0:T(8,128)(2,1)}, bf16[128,1280]{1,0:T(8,128)(2,1)S(1)}, u32[]{:S(2)}, u32[]{:S(2)}) collective-permute-start(bf16[128,1280]{1,0:T(8,128)(2,1)} %get-tuple-element.83), channel_id=1, source_target_pairs={{0,1},{1,2},{2,3},{3,0},{4,5},{5,6},{6,7},{7,4},{8,9},{9,10},{10,1... | collective-permute-start | bytes 983048 | tf_op jit(solution)/shard_map/ppermute | solution.py:127
  202.9 15.2 %collective-permute-start.19 = (bf16[128,1280]{1,0:T(8,128)(2,1)}, bf16[128,1280]{1,0:T(8,128)(2,1)S(1)}, u32[]{:S(2)}, u32[]{:S(2)}) collective-permute-start(bf16[128,1280]{1,0:T(8,128)(2,1)} %get-tuple-element.84), channel_id=1, source_target_pairs={{0,2},{1,3},{2,0},{3,1},{4,6},{5,7},{6,4},{7,5},{8,10},{9,11},{10,... | collective-permute-start | bytes 983048 | tf_op jit(solution)/shard_map/ppermute | solution.py:127
  207.2 15.3 %collective-permute-start.20 = (bf16[128,1280]{1,0:T(8,128)(2,1)}, bf16[128,1280]{1,0:T(8,128)(2,1)S(1)}, u32[]{:S(2)}, u32[]{:S(2)}) collective-permute-start(bf16[128,1280]{1,0:T(8,128)(2,1)} %get-tuple-element.85), channel_id=1, source_target_pairs={{0,3},{1,0},{2,1},{3,2},{4,7},{5,4},{6,5},{7,6},{8,11},{9,8},{10,9... | collective-permute-start | bytes 983048 | tf_op jit(solution)/shard_map/ppermute | solution.py:127
  (10 other events, 101.1 us)
